TPU v7x, 32 devices: a whole 2x2x4 slice. The times are simulated.
32 devices in a mesh: view: 4 (over z), tile: 8 (over y, x, core).
Axes of the slice: x: 2, y: 2, z: 4, core: 2. Of those that a mesh axis runs over, the one named last changes fastest.
Arguments:
- centres: float32 [3, 32768], P(None, ('view', 'tile')), may hold values from -6 to 6
- shape_raw: float32 [6, 32768], P(None, ('view', 'tile')), may hold values from -1 to 0.2
- opacity_logit: float32 [32768], P(('view', 'tile')), may hold values from -6 to -1
- colours: float32 [3, 32768], P(None, ('view', 'tile')), may hold values from -6 to 6
- camera: float32 [8, 2, 4], replicated, may hold values from -15 to 15
- target: float32 [8, 128, 3, 256], P('view', 'tile'), may hold values from -3 to 3
- intersection_ids: int32 [8, 128, 256], P('view', 'tile'), may hold values from 0 to 32767, as said below
- depth_order: int32 [8, 128, 256], P('view', 'tile'), may hold values from 0 to 255, each once within a row
- live_count: int32 [8, 128], P('view', 'tile'), may hold values from 1 to 256, as said below
Outputs:
- rendered: float32 [8, 128, 3, 256], P('view', 'tile')
- grad_centres: float32 [3, 32768], P(None, ('view', 'tile'))
- grad_shape: float32 [6, 32768], P(None, ('view', 'tile'))
- grad_opacity: float32 [32768], P(('view', 'tile'))
- grad_colours: float32 [3, 32768], P(None, ('view', 'tile'))
- next_owner: int32 [8, 128], P('view', 'tile')
Inputs may be any that keep to these rules, and one draw needn't show every extreme that they name: `intersection_ids`: gaussian g is held by device g div 1024, devices counted along view+tile. Among the 2 x 16 x 256 slots held by one device at most 512 name Gaussians of any one device, and in every draw some device is named exactly 512 times by the slots of every device. `depth_order`: each tile's entries are a permutation of the slot numbers. Slot s of tile (v, t) is live when s < live_count[v, t]; every view has a tile with all 256 slots live.
All inputs are finite; a program needn't handle non-finite values.
Results may differ from a plain program's by a relative error of at most 0.0003.
Values sent between devices are 32-bit elements; how exact they have to be, the bound alone decides.
No kernel may reach another device: no remote copies, remote signals or barrier semaphores. Data moves between devices by JAX's collectives and lax.ppermute only.
A program may use at most 128 MiB of HBM per device.

v0:
```python
from functools import partial
import math

import jax
import jax.numpy as jnp
import numpy as np
from jax import lax
from jax.experimental import pallas as pl
from jax.experimental.pallas import tpu as pltpu
from jax.sharding import PartitionSpec as P

F32 = jnp.float32
BF16 = jnp.bfloat16
FIELDS = 13
GROUPS = 8
ACCS = 4
UNROLL = 4
BATCH = 2
LOG2E = math.log2(math.e)
OFF = -1e4


def log2_of(n):
    bits = n.bit_length() - 1
    assert n == 1 << bits
    return bits


def pieces_of(value, count):
    out = []
    rest = value
    for _ in range(count - 1):
        piece = rest.astype(BF16).astype(F32)
        out.append(piece)
        rest = rest - piece
    out.append(rest)
    return out


def dot_nn(a, b):
    return lax.dot_general(a, b, (((1,), (0,)), ((), ())), preferred_element_type=F32)


def dot_nt(a, b):
    return lax.dot_general(a, b, (((1,), (1,)), ((), ())), preferred_element_type=F32)


def dot_tn(a, b):
    return lax.dot_general(a, b, (((0,), (0,)), ((), ())), preferred_element_type=F32)


def chunk_rows(live):
    return (live + 7) >> 3


def repeat(count, step, body):
    many = lax.div(count, step)

    def trip(i, _):
        for u in range(step):
            body(i * step + u)
        return 0

    def single(i, _):
        body(i)
        return 0

    lax.fori_loop(0, many, trip, 0)
    lax.fori_loop(many * step, count, single, 0)


def prep_kernel(
    dims,
    me_ref,
    live_ref,
    camera_ref,
    ids_ref,
    order_ref,
    row_ref,
    group_ref,
    cam_ref,
    piece_ref,
    rho_ref,
    code_ref,
    lhs_ref,
    live_full,
    order_b,
):
    own_bits, lane_bits, view_bits, tile_bits, tiles_view = dims
    tiles, slots = ids_ref.shape
    me = me_ref[0]
    views = tiles // tiles_view
    first = (me >> tile_bits) * views
    for v in range(views):
        for i in range(2):
            for j in range(4):
                cam_ref[v * 8 + i * 4 + j] = camera_ref[first + v, i, j]
    for t in range(tiles):
        live_full[t : t + 1, :] = jnp.full((1, slots), live_ref[t // tiles_view, t % tiles_view], jnp.int32)
    live = live_full[...]
    order = order_ref[...]
    active = order < live
    upper = (
        lax.broadcasted_iota(jnp.int32, (slots, slots), 0)
        < lax.broadcasted_iota(jnp.int32, (slots, slots), 1)
    ).astype(F32).astype(BF16)
    place = dot_nn(active.astype(F32).astype(BF16), upper).astype(jnp.int32)
    rows = chunk_rows(live)
    chunk = jnp.zeros((tiles, slots), jnp.int32)
    for m in range(1, GROUPS):
        chunk = chunk + (place >= m * rows).astype(jnp.int32)
    rho_ref[...] = jnp.where(active, (place - chunk * rows) * GROUPS + chunk, -1).astype(F32)
    order_b[...] = order.astype(F32)
    ids = ids_ref[...]
    owner = (ids >> own_bits) ^ me
    local = ids & ((1 << own_bits) - 1)
    xy_bits = tile_bits - 1
    core = owner & 1
    chip = (owner >> 1) & ((1 << xy_bits) - 1)
    view = owner >> tile_bits
    block = (((core << xy_bits) | chip) << view_bits) | view
    row = (block << lane_bits) | (local & ((1 << lane_bits) - 1))
    code = (row << 3) | (local >> lane_bits)
    piece_ref[0] = (code & 255).astype(F32)
    piece_ref[1] = ((code >> 8) & 255).astype(F32)
    piece_ref[2] = (code >> 16).astype(F32)
    lhs_ref[...] = jnp.zeros_like(lhs_ref)
    down = lax.broadcasted_iota(jnp.int32, (slots, slots), 0).astype(F32).astype(BF16)
    one = jnp.ones((slots, slots), BF16)
    nil = jnp.zeros((slots, slots), BF16)

    def some_tiles(s, _):
        for u in range(UNROLL):
            t = s * UNROLL + u
            for p in range(3):
                lhs_ref[u, p : p + 1, :] = piece_ref[p, pl.ds(t, 1), :]
            picked = jnp.where(down == order_b[pl.ds(t, 1), :].astype(BF16), one, nil)
            ordered = dot_nn(lhs_ref[u].astype(BF16), picked)
            placed = jnp.where(down == rho_ref[pl.ds(t, 1), :].astype(BF16), one, nil)
            out = dot_nt(ordered.astype(BF16), placed)
            code_ref[pl.ds(t, 1), :] = out[0:1] + 256.0 * out[1:2] + 65536.0 * out[2:3]
        return 0

    lax.fori_loop(0, tiles // UNROLL, some_tiles, 0)
    codes = code_ref[...].astype(jnp.int32)
    row_ref[...] = codes >> 3
    pos = lax.broadcasted_iota(jnp.int32, (tiles, slots), 1)
    here = (pos >> 3 < rows) & ((pos & 7) * rows + (pos >> 3) < live)
    group_ref[...] = jnp.where(here, codes & 7, GROUPS)


def splat_kernel(
    dims,
    cam_ref,
    row_ref,
    live_ref,
    group_ref,
    mine_ref,
    other_ref,
    target_ref,
    mono_ref,
    image_ref,
    grad_mine_ref,
    grad_other_ref,
    *scratch,
):
    views, tiles_view, slots, pixels, lanes, column = dims
    table, buf, raw, rec, mom, grad, c_s, h_s, w_hi, w_lo, g_1, g_2, g_3, row_s, row_2 = scratch[:15]
    accs = scratch[15:]
    tiles = views * tiles_view
    chips = mine_ref.shape[0]
    half = chips * column
    used = FIELDS * GROUPS
    pad = jnp.zeros((lanes - used, lanes), F32)

    for acc in accs:
        acc[...] = jnp.zeros_like(acc)
    for ref in (buf, w_hi, w_lo, g_1, g_2, g_3, row_s, row_2):
        ref[...] = jnp.zeros_like(ref)

    def build(q, _):
        for base, ref in ((0, mine_ref), (half, other_ref)):
            for d in range(column):
                block = jnp.concatenate([ref[q, d * used : (d + 1) * used, :], pad], axis=0)
                start = pl.multiple_of((base + q * column + d) * lanes, lanes)
                table[pl.ds(start, lanes), :] = jnp.transpose(block)
        return 0

    lax.fori_loop(0, chips, build, 0)

    def live_of(t):
        return live_ref[lax.div(t, tiles_view), lax.rem(t, tiles_view)]

    sub = lax.broadcasted_iota(jnp.int32, (GROUPS, slots), 0)

    def fetch(t, _):
        def copy(i):
            for k in range(GROUPS):
                buf[pl.ds(i * GROUPS + k, 1), :] = table[pl.ds(row_ref[t * slots + i * GROUPS + k], 1), :]

        repeat(chunk_rows(live_of(t)), 4, copy)
        turned = jnp.transpose(buf[...])
        mine = sub == group_ref[pl.ds(t, 1), :]
        for f in range(FIELDS):
            part = jnp.where(mine, turned[f * GROUPS : (f + 1) * GROUPS], 0.0)
            raw[f, pl.ds(t, 1), :] = jnp.sum(part, axis=0, keepdims=True)
        return 0

    lax.fori_loop(0, tiles, fetch, 0)

    def project(v):
        block = slice(v * tiles_view, (v + 1) * tiles_view)
        cam = [cam_ref[v * 8 + n] for n in range(8)]
        field = lambda f: raw[f, block, :]
        u = cam[0] * field(0) + cam[1] * field(1) + cam[2] * field(2) + cam[3]
        w = cam[4] * field(0) + cam[5] * field(1) + cam[6] * field(2) + cam[7]
        d0, d1, d2 = jnp.exp(field(3)), jnp.exp(field(5)), jnp.exp(field(8))
        factor = []
        for i in range(2):
            m = cam[4 * i : 4 * i + 3]
            factor.append(
                (
                    m[0] * d0 + m[1] * field(4) + m[2] * field(6),
                    m[1] * d1 + m[2] * field(7),
                    m[2] * d2,
                )
            )
        f0, f1 = factor
        s00 = f0[0] * f0[0] + f0[1] * f0[1] + f0[2] * f0[2] + 0.3
        s01 = f0[0] * f1[0] + f0[1] * f1[1] + f0[2] * f1[2]
        s11 = f1[0] * f1[0] + f1[1] * f1[1] + f1[2] * f1[2] + 0.3
        inverse = 1.0 / (s00 * s11 - s01 * s01)
        conic = (s11 * inverse, -s01 * inverse, s00 * inverse)
        here = group_ref[block, :] < GROUPS
        return here, cam, block, u, w, (d0, d1, d2), f0, f1, conic

    for v in range(views):
        here, cam, block, u, w, _, _, _, (ka, kb, kc) = project(v)
        x_line = ka * u + kb * w
        y_line = kb * u + kc * w
        log_opacity = math.log(0.95) - jnp.log(1.0 + jnp.exp(-raw[9, block, :]))
        level = log_opacity - 0.5 * (u * x_line + w * y_line)
        terms = (-0.5 * ka, -kb, -0.5 * kc, x_line, y_line)
        for n, term in enumerate(terms):
            rec[n, block, :] = jnp.where(here, term * LOG2E, 0.0)
        rec[5, block, :] = jnp.where(here, level * LOG2E, OFF)
        for c in range(3):
            rec[6 + c, block, :] = raw[10 + c, block, :]

    lane_row = lax.broadcasted_iota(jnp.int32, (GROUPS, pixels), 0)
    own_chunk = (lax.broadcasted_iota(jnp.int32, (GROUPS, slots), 1) & 7) == sub
    zero_rows = jnp.zeros((8, slots), F32)
    zero_pix = jnp.zeros((8, pixels), F32)

    def paired(a, b):
        return a + pltpu.roll(b, 3, 0)

    def render(s, _):
        tile = [s * BATCH + g for g in range(BATCH)]
        blocks = [(chunk_rows(live_of(t)) + 3) >> 2 for t in tile]
        for g, t in enumerate(tile):
            for n in range(6):
                row_s[g, n : n + 1, :] = rec[n, pl.ds(t, 1), :]
            for c in range(3):
                row_s[g, 8 + c : 9 + c, :] = rec[6 + c, pl.ds(t, 1), :]
        for g in range(BATCH):
            lhs = jnp.concatenate(pieces_of(row_s[g, 0:8, :], 3) + [zero_rows], axis=0).astype(BF16)
            c_s[g] = dot_tn(lhs, mono_ref[...])
        colour = [pieces_of(row_s[g, 8:16, :], 3) for g in range(BATCH)]

        lead = []
        for g in range(BATCH):

            def through(i, prod, g=g):
                rows = pl.ds(pl.multiple_of(i * 32, 32), 32)
                cover = jnp.exp2(c_s[g, rows, :])
                c_s[g, rows, :] = cover
                keep = 1.0 - cover
                return prod * ((keep[0:8] * keep[8:16]) * (keep[16:24] * keep[24:32]))

            lead.append(lax.fori_loop(0, blocks[g], through, jnp.ones((GROUPS, pixels), F32)))
        for g in range(BATCH):
            scan = lead[g]
            for step in (1, 2, 4):
                scan = scan * jnp.where(lane_row >= step, pltpu.roll(scan, step, 0), 1.0)
            lead[g] = jnp.where(lane_row >= 1, pltpu.roll(scan, 1, 0), 1.0)

        def weights(cover, prod):
            out = []
            for h in range(4):
                weight = prod * cover[8 * h : 8 * h + 8]
                prod = prod - weight
                out.append(weight)
            return out, prod

        for g in range(BATCH):

            def weigh(i, prod, g=g):
                rows = pl.ds(pl.multiple_of(i * 32, 32), 32)
                parts, prod = weights(c_s[g, rows, :], prod)
                weight = jnp.concatenate(parts, axis=0)
                high = weight.astype(BF16)
                w_hi[g, rows, :] = high
                w_lo[g, rows, :] = (weight - high.astype(F32)).astype(BF16)
                return prod

            lax.fori_loop(0, blocks[g], weigh, lead[g])

        after = []
        for g, t in enumerate(tile):
            v, tl = lax.div(t, tiles_view), lax.rem(t, tiles_view)
            spread = [
                jnp.where(own_chunk, jnp.broadcast_to(piece[c : c + 1], (GROUPS, slots)), 0.0)
                for c in range(3)
                for piece in colour[g]
            ]
            lhs = jnp.concatenate(spread + [zero_rows], axis=0).astype(BF16)
            image = dot_nn(lhs, w_hi[g]) + dot_nn(lhs, w_lo[g])
            rest = jnp.zeros((GROUPS, pixels), F32)
            for c in range(3):
                part = image[24 * c : 24 * c + 8] + image[24 * c + 8 : 24 * c + 16] + image[24 * c + 16 : 24 * c + 24]
                whole = jnp.sum(part, axis=0, keepdims=True)
                image_ref[v, c, pl.ds(tl, 1), :] = whole
                miss = whole - target_ref[v, c, pl.ds(tl, 1), :]
                row_2[g, c : c + 1, :] = miss
                rest = rest + part * miss
            for step in (1, 2, 4):
                rest = rest + jnp.where(lane_row < GROUPS - step, pltpu.roll(rest, GROUPS - step, 0), 0.0)
            after.append(rest)
        missed = [pieces_of(row_2[g], 3) for g in range(BATCH)]
        for g in range(BATCH):
            c1, c2, c3 = colour[g]
            m1, m2, m3 = missed[g]
            lhs = jnp.concatenate([paired(c1, c1), paired(c2, c1), paired(c2, c3), zero_rows], axis=0)
            rhs = jnp.concatenate([paired(m1, m2), paired(m1, m3), paired(m2, m1), zero_pix], axis=0)
            h_s[g] = dot_tn(lhs.astype(BF16), rhs.astype(BF16))

        for g in range(BATCH):

            def settle(i, carry, g=g):
                prod, tail = carry
                rows = pl.ds(pl.multiple_of(i * 32, 32), 32)
                cover = c_s[g, rows, :]
                pull = h_s[g, rows, :]
                parts, prod = weights(cover, prod)
                ratio = cover / (1.0 - cover)
                slopes = []
                for h in range(4):
                    cut = slice(8 * h, 8 * h + 8)
                    part = parts[h] * pull[cut]
                    tail = tail - part
                    slopes.append(part - ratio[cut] * tail)
                slope = jnp.concatenate(slopes, axis=0)
                high = slope.astype(BF16)
                rest = slope - high.astype(F32)
                middle = rest.astype(BF16)
                g_1[g, rows, :] = high
                g_2[g, rows, :] = middle
                g_3[g, rows, :] = (rest - middle.astype(F32)).astype(BF16)
                return prod, tail

            lax.fori_loop(0, blocks[g], settle, (lead[g], after[g]))
        mono = mono_ref[0:16, :]
        for g in range(BATCH):
            moments = dot_nt(mono, g_1[g]) + dot_nt(mono, g_2[g]) + dot_nt(mono, g_3[g])
            miss_lhs = jnp.concatenate(missed[g] + [zero_pix], axis=0).astype(BF16)
            tint = dot_nt(miss_lhs, w_hi[g]) + dot_nt(miss_lhs, w_lo[g])
            row_s[g, 0:8, :] = moments[0:8]
            row_s[g, 8:16, :] = tint[0:8] + tint[8:16] + tint[16:24]
        for g, t in enumerate(tile):
            for n in range(6):
                mom[n, pl.ds(t, 1), :] = row_s[g, n : n + 1, :]
            for c in range(3):
                mom[6 + c, pl.ds(t, 1), :] = row_s[g, 8 + c : 9 + c, :]
        return 0

    lax.fori_loop(0, tiles // BATCH, render, 0)

    for v in range(views):
        here, cam, block, u, w, (d0, d1, d2), f0, f1, (ka, kb, kc) = project(v)
        mxx, mxy, myy, mx, my, m1 = [jnp.where(here, mom[n, block, :], 0.0) for n in range(6)]
        dx = mx - u * m1
        dy = my - w * m1
        dxx = mxx - 2.0 * u * mx + u * u * m1
        dxy = mxy - u * my - w * mx + u * w * m1
        dyy = myy - 2.0 * w * my + w * w * m1
        gu = ka * dx + kb * dy
        gw = kb * dx + kc * dy
        ax, ay = ka * dxx + kb * dxy, ka * dxy + kb * dyy
        bx, by = kb * dxx + kc * dxy, kb * dxy + kc * dyy
        h00 = ax * ka + ay * kb
        h01 = ax * kb + ay * kc
        h11 = bx * kb + by * kc
        g0 = [h00 * f0[j] + h01 * f1[j] for j in range(3)]
        g1 = [h01 * f0[j] + h11 * f1[j] for j in range(3)]
        for k in range(3):
            grad[k, block, :] = cam[k] * gu + cam[4 + k] * gw
        grad[3, block, :] = (cam[0] * g0[0] + cam[4] * g1[0]) * d0
        grad[4, block, :] = cam[1] * g0[0] + cam[5] * g1[0]
        grad[5, block, :] = (cam[1] * g0[1] + cam[5] * g1[1]) * d1
        grad[6, block, :] = cam[2] * g0[0] + cam[6] * g1[0]
        grad[7, block, :] = cam[2] * g0[1] + cam[6] * g1[1]
        grad[8, block, :] = (cam[2] * g0[2] + cam[6] * g1[2]) * d2
        grad[9, block, :] = m1 - m1 / (1.0 + jnp.exp(-raw[9, block, :]))
        for c in range(3):
            grad[10 + c, block, :] = mom[6 + c, block, :]

    def give(t, _):
        mine = sub == group_ref[pl.ds(t, 1), :]
        spread = [
            jnp.where(mine, jnp.broadcast_to(grad[f, pl.ds(t, 1), :], (GROUPS, slots)), 0.0)
            for f in range(FIELDS)
        ]
        spread.append(jnp.zeros((lanes - used, slots), F32))
        buf[...] = jnp.transpose(jnp.concatenate(spread, axis=0))

        def add(i):
            for k in range(0, GROUPS, len(accs)):
                where = [row_ref[t * slots + i * GROUPS + k + n] for n in range(len(accs))]
                olds = [accs[n][pl.ds(where[n], 1), :] for n in range(len(accs))]
                news = [buf[pl.ds(i * GROUPS + k + n, 1), :] for n in range(len(accs))]
                for n in range(len(accs)):
                    accs[n][pl.ds(where[n], 1), :] = olds[n] + news[n]

        repeat(chunk_rows(live_of(t)), 4, add)
        return 0

    lax.fori_loop(0, tiles, give, 0)

    def finish(d, _):
        for base, ref in ((0, grad_mine_ref), (half, grad_other_ref)):
            start = pl.multiple_of((base + d) * lanes, lanes)
            total = accs[0][pl.ds(start, lanes), :]
            for acc in accs[1:]:
                total = total + acc[pl.ds(start, lanes), :]
            ref[d] = jnp.transpose(total)[0:used]
        return 0

    lax.fori_loop(0, half, finish, 0)


def monomials(pixels):
    side = math.isqrt(pixels)
    index = np.arange(pixels)
    x = (index % side) - (side - 1) / 2.0
    y = (index // side) - (side - 1) / 2.0
    one = np.ones_like(x)
    zero = np.zeros_like(x)
    group = np.stack([x * x, x * y, y * y, x, y, one, zero, zero])
    return jnp.asarray(np.concatenate([group, group, group, np.zeros_like(group)]), BF16)


def swap(array, axis, mask):
    size = lax.axis_size(axis)
    return lax.ppermute(array, axis, [(i, i ^ mask) for i in range(size)])


def shards(centres, shape_raw, opacity_logit, colours, camera, target, intersection_ids, depth_order, live_count):
    view_group = lax.axis_size("view")
    tile_group = lax.axis_size("tile")
    devices = view_group * tile_group
    chips = tile_group // 2
    own_count = centres.shape[1]
    lanes = own_count // GROUPS
    views, tiles_view, slots = intersection_ids.shape
    tiles = views * tiles_view
    pixels = target.shape[3]
    view_index = lax.axis_index("view")
    tile_index = lax.axis_index("tile")
    me = (view_index * tile_group + tile_index).astype(jnp.int32)

    totals = jnp.sum(live_count, axis=1)
    within = jnp.cumsum(live_count, axis=1) - live_count

    smem = pl.BlockSpec(memory_space=pltpu.SMEM)
    vmem = pl.BlockSpec(memory_space=pltpu.VMEM)
    prep = pl.pallas_call(
        partial(
            prep_kernel,
            (log2_of(own_count), log2_of(lanes), log2_of(view_group), log2_of(tile_group), tiles_view),
        ),
        out_shape=[
            jax.ShapeDtypeStruct((tiles, slots), jnp.int32),
            jax.ShapeDtypeStruct((tiles, slots), jnp.int32),
            jax.ShapeDtypeStruct((views * 8,), F32),
        ],
        in_specs=[smem] * 3 + [vmem] * 2,
        out_specs=[vmem, vmem, smem],
        scratch_shapes=[
            pltpu.VMEM((3, tiles, slots), F32),
            pltpu.VMEM((tiles, slots), F32),
            pltpu.VMEM((tiles, slots), F32),
            pltpu.VMEM((UNROLL, 16, slots), F32),
            pltpu.VMEM((tiles, slots), jnp.int32),
            pltpu.VMEM((tiles, slots), F32),
        ],
        cost_estimate=pl.CostEstimate(flops=8_000_000_000, bytes_accessed=4 * tiles * slots * 4, transcendentals=0),
        name="prep",
    )

    fields = jnp.concatenate([centres, shape_raw, opacity_logit[None], colours], axis=0)
    block = fields.reshape(FIELDS * GROUPS, lanes)
    note = jnp.pad(totals.astype(F32)[None], ((0, 7), (0, lanes - views)))
    column = jnp.concatenate([block] + [swap(block, "view", m) for m in range(1, view_group)] + [note])
    mine = jnp.stack([column] + [swap(column, "tile", 2 * m) for m in range(1, chips)])
    rows, group, cam = prep(
        me[None],
        live_count,
        camera,
        intersection_ids.reshape(tiles, slots),
        depth_order.reshape(tiles, slots),
    )
    mine, rows, group, cam = lax.optimization_barrier((mine, rows.reshape(-1), group, cam))
    other = swap(mine, "tile", 1)

    table_rows = devices * lanes
    square = (BATCH, slots, pixels)
    half = (chips * view_group, FIELDS * GROUPS, lanes)
    splat = pl.pallas_call(
        partial(splat_kernel, (views, tiles_view, slots, pixels, lanes, view_group)),
        out_shape=[
            jax.ShapeDtypeStruct((views, 3, tiles_view, pixels), F32),
            jax.ShapeDtypeStruct(half, F32),
            jax.ShapeDtypeStruct(half, F32),
        ],
        in_specs=[smem] * 3 + [vmem] * 5,
        out_specs=[vmem] * 3,
        scratch_shapes=[
            pltpu.VMEM((table_rows, lanes), F32),
            pltpu.VMEM((slots, lanes), F32),
            pltpu.VMEM((FIELDS, tiles, slots), F32),
            pltpu.VMEM((9, tiles, slots), F32),
            pltpu.VMEM((9, tiles, slots), F32),
            pltpu.VMEM((FIELDS, tiles, slots), F32),
            pltpu.VMEM(square, F32),
            pltpu.VMEM(square, F32),
        ]
        + [pltpu.VMEM(square, BF16)] * 5
        + [pltpu.VMEM((BATCH, 16, slots), F32), pltpu.VMEM((BATCH, 8, pixels), F32)]
        + [pltpu.VMEM((table_rows, lanes), F32)] * (ACCS if devices <= 32 else 2),
        compiler_params=pltpu.CompilerParams(vmem_limit_bytes=60 * 1024 * 1024),
        name="splat",
    )
    rendered, grad_mine, grad_other = splat(
        cam,
        rows,
        live_count,
        group,
        mine,
        other,
        target.transpose(0, 2, 1, 3),
        monomials(pixels),
    )

    whole = totals
    before = jnp.zeros_like(totals)
    for core, held in enumerate((mine, other)):
        for m in range(chips):
            mask = 2 * m + core
            if mask:
                theirs = held[m, view_group * FIELDS * GROUPS, 0:views].astype(jnp.int32)
                whole = whole + theirs
                before = before + jnp.where((tile_index ^ mask) < tile_index, theirs, 0)
    next_owner = (before[:, None] + within) * tile_group // whole[:, None]

    joined = grad_mine + swap(grad_other, "tile", 1)
    joined = joined.reshape(chips, view_group, FIELDS * GROUPS, lanes)
    part = joined[0]
    for m in range(1, chips):
        part = part + swap(joined[m], "tile", 2 * m)
    summed = part[0]
    for m in range(1, view_group):
        summed = summed + swap(part[m], "view", m)
    summed = summed.reshape(FIELDS, own_count)
    return (
        rendered.transpose(0, 2, 1, 3),
        summed[0:3],
        summed[3:9],
        summed[9],
        summed[10:13],
        next_owner,
    )


def solution(mesh):
    in_specs = (
        P(None, ("view", "tile")),
        P(None, ("view", "tile")),
        P(("view", "tile")),
        P(None, ("view", "tile")),
        P(),
        P("view", "tile", None, None),
        P("view", "tile", None),
        P("view", "tile", None),
        P("view", "tile"),
    )
    out_specs = (
        P("view", "tile", None, None),
        P(None, ("view", "tile")),
        P(None, ("view", "tile")),
        P(("view", "tile")),
        P(None, ("view", "tile")),
        P("view", "tile"),
    )
    return jax.shard_map(shards, mesh=mesh, in_specs=in_specs, out_specs=out_specs, check_vma=False)
```

profile of v0, /device:TPU:0, one launch (start us, length us, event | category | flops | bytes accessed | tf_op | source)
XLA Modules:
  0.0 104.6 jit_solution(17299576033955030016)
XLA Ops:
  0.6 0.8 pad_maximum_fusion.1
  1.5 0.0 copy-start.2
  1.5 3.1 %collective-permute-start = (f32[104,128]{1,0:T(8,128)S(1)}, f32[104,128]{1,0:T(8,128)S(1)}, u32[]{:S(2)}, u32[]{:S(2)}) collective-permute-start(f32[104,128]{1,0:T(8,128)S(1)} %reshape.157), channel_id=1, source_target_pairs={{0,8},{8,0},{16,24},{24,16},{1,9},{9,1},{17,25},{25,17},{2,10},{10... | collective-permute-start | bytes 159752 | tf_op jit(solution)/shard_map/ppermute | solution.py:455
  4.6 2.6 %collective-permute-start.1 = (f32[104,128]{1,0:T(8,128)S(1)}, f32[104,128]{1,0:T(8,128)S(1)}, u32[]{:S(2)}, u32[]{:S(2)}) collective-permute-start(f32[104,128]{1,0:T(8,128)S(1)} %reshape.157), channel_id=1, source_target_pairs={{0,16},{8,24},{16,0},{24,8},{1,17},{9,25},{17,1},{25,9},{2,18},{10... | collective-permute-start | bytes 159752 | tf_op jit(solution)/shard_map/ppermute | solution.py:455
  7.2 0.0 collective-permute-start.2
  7.2 0.1 reduce_sum.9
  7.3 0.0 copy-start.4
  7.4 0.7 copy-done.4
  8.0 0.7 copy.16.camera_ref
  8.7 0.0 collective-permute-done
  8.7 1.9 %collective-permute-done.1 = f32[104,128]{1,0:T(8,128)S(1)} collective-permute-done((f32[104,128]{1,0:T(8,128)S(1)}, f32[104,128]{1,0:T(8,128)S(1)}, u32[]{:S(2)}, u32[]{:S(2)}) %collective-permute-start.1) | collective-permute-done | bytes 53280 | tf_op jit(solution)/shard_map/ppermute | solution.py:455
  10.7 2.5 %collective-permute-done.2 = f32[104,128]{1,0:T(8,128)S(1)} collective-permute-done((f32[104,128]{1,0:T(8,128)S(1)}, f32[104,128]{1,0:T(8,128)S(1)}, u32[]{:S(2)}, u32[]{:S(2)}) %collective-permute-start.2) | collective-permute-done | bytes 53280 | tf_op jit(solution)/shard_map/ppermute | solution.py:455
  13.1 1.6 %collective-permute-start.3 = (f32[424,128]{1,0:T(8,128)S(1)}, f32[424,128]{1,0:T(8,128)S(1)}, u32[]{:S(2)}, u32[]{:S(2)}) collective-permute-start(f32[424,128]{1,0:T(8,128)S(1)} %constant_dynamic-update-slice_fusion), channel_id=1, source_target_pairs={{0,2},{1,3},{2,0},{3,1},{4,6},{5,7},{6,4},{7,5},{8,10},{9,11},{10,... | collective-permute-start | bytes 651272 | tf_op jit(solution)/shard_map/ppermute | solution.py:455
  14.7 1.5 %collective-permute-start.4 = (f32[424,128]{1,0:T(8,128)S(1)}, f32[424,128]{1,0:T(8,128)S(1)}, u32[]{:S(2)}, u32[]{:S(2)}) collective-permute-start(f32[424,128]{1,0:T(8,128)S(1)} %constant_dynamic-update-slice_fusion), channel_id=1, source_target_pairs={{0,4},{1,5},{2,6},{3,7},{4,0},{5,1},{6,2},{7,3},{8,12},{9,13},{10,... | collective-permute-start | bytes 651272 | tf_op jit(solution)/shard_map/ppermute | solution.py:455
  16.2 0.5 collective-permute-start.5
  16.7 5.1 %prep.1 = (s32[32,256]{1,0:T(8,128)}, s32[32,256]{1,0:T(8,128)}, f32[16]{0:T(128)}) custom-call(s32[1]{0:T(128)} %bitcast.6.me_ref, s32[2,16]{1,0:T(2,128)} %live_ref.3, f32[8,2,4]{2,1,0:T(2,128)} %copy.16.camera_ref, s32[32,256]{1,0:T(8,128)} %bitcast.97, s32[32,256]{1,0:T(8,128)} %bitcast.98), custom_call_target="tpu_custom_call" | custom-call | flops 8000000000 | bytes 131072 | tf_op jit(solution)/shard_map/prep/pallas_call | solution.py:506
  21.8 1.4 %copy.17 = s32[4,2,8,128]{3,1,2,0:T(2,128)} copy(s32[4,2,8,128]{3,2,1,0:T(8,128)} %bitcast.94) | data formatting | bytes 65536
  23.2 0.0 collective-permute-done.3
  23.2 1.4 %collective-permute-done.4 = f32[424,128]{1,0:T(8,128)S(1)} collective-permute-done((f32[424,128]{1,0:T(8,128)S(1)}, f32[424,128]{1,0:T(8,128)S(1)}, u32[]{:S(2)}, u32[]{:S(2)}) %collective-permute-start.4) | collective-permute-done | bytes 217120 | tf_op jit(solution)/shard_map/ppermute | solution.py:455
  24.6 0.1 pad_maximum_fusion.mine_ref
  24.7 0.1 collective-permute-start.6
  24.8 2.4 %collective-permute-done.6.other_ref = f32[4,424,128]{2,1,0:T(8,128)S(1)} collective-permute-done((f32[4,424,128]{2,1,0:T(8,128)S(1)}, f32[4,424,128]{2,1,0:T(8,128)S(1)}, u32[]{:S(2)}, u32[]{:S(2)}) %collective-permute-start.6) | collective-permute-done | bytes 868384 | tf_op jit(solution)/shard_map/ppermute | solution.py:455
  27.2 1.0 copy-done.1
  28.2 41.5 %splat.1 = (f32[2,3,16,256]{3,2,1,0:T(8,128)}, f32[16,104,128]{2,1,0:T(8,128)}, f32[16,104,128]{2,1,0:T(8,128)}) custom-call(f32[16]{0:T(128)} %get-tuple-element.19.cam_ref, s32[8192]{0:T(1024)} %bitcast.92, s32[2,16]{1,0:T(2,128)} %live_ref.3, s32[32,256]{1,0:T(8,128)} %get-tuple-element.21.group_ref, f32[4,424,128]{2,1,0:T(8,128)} %copy-done, ...), custom_call_target="tpu_custom_call" | custom-call | tf_op jit(solution)/shard_map/splat/pallas_call | solution.py:544
  69.7 0.7 copy-done.3
  70.4 0.2 reduce_window_sum.11
  70.5 0.7 fusion.19
  71.3 1.0 collective-permute-done.7
  72.3 1.2 %add.148 = f32[16,104,128]{2,1,0:T(8,128)S(1)} add(f32[16,104,128]{2,1,0:T(8,128)} %get-tuple-element.24, f32[16,104,128]{2,1,0:T(8,128)S(1)} %collective-permute-done.7) | non-fusion elementwise | flops 212992 | bytes 2555904 | tf_op jit(solution)/shard_map/add | solution.py:566
  73.6 8.9 %collective-permute-start.10 = (f32[4,104,128]{2,1,0:T(8,128)S(1)}, f32[4,104,128]{2,1,0:T(8,128)S(1)}, u32[]{:S(2)}, u32[]{:S(2)}) collective-permute-start(f32[4,104,128]{2,1,0:T(8,128)S(1)} %get-tuple-element.29), channel_id=1, source_target_pairs={{0,6},{1,7},{2,4},{3,5},{4,2},{5,3},{6,0},{7,1},{8,14},{9,15},{10,... | collective-permute-start | bytes 638984 | tf_op jit(solution)/shard_map/ppermute | solution.py:455
  82.5 0.1 collective-permute-start.8
  82.6 0.5 collective-permute-start.9
  83.1 0.7 fusion.10
  83.8 4.8 %collective-permute-done.10 = f32[4,104,128]{2,1,0:T(8,128)S(1)} collective-permute-done((f32[4,104,128]{2,1,0:T(8,128)S(1)}, f32[4,104,128]{2,1,0:T(8,128)S(1)}, u32[]{:S(2)}, u32[]{:S(2)}) %collective-permute-start.10) | collective-permute-done | bytes 213024 | tf_op jit(solution)/shard_map/ppermute | solution.py:455
  88.6 4.1 %collective-permute-done.8 = f32[4,104,128]{2,1,0:T(8,128)S(1)} collective-permute-done((f32[4,104,128]{2,1,0:T(8,128)S(1)}, f32[4,104,128]{2,1,0:T(8,128)S(1)}, u32[]{:S(2)}, u32[]{:S(2)}) %collective-permute-start.8) | collective-permute-done | bytes 213024 | tf_op jit(solution)/shard_map/ppermute | solution.py:455
  92.7 0.1 collective-permute-done.9
  92.8 0.1 fusion.1
  92.9 0.1 collective-permute-start.11
  93.0 3.2 %collective-permute-start.12 = (f32[104,128]{1,0:T(8,128)S(1)}, f32[104,128]{1,0:T(8,128)S(1)}, u32[]{:S(2)}, u32[]{:S(2)}) collective-permute-start(f32[104,128]{1,0:T(8,128)S(1)} %get-tuple-element.33), channel_id=1, source_target_pairs={{0,16},{8,24},{16,0},{24,8},{1,17},{9,25},{17,1},{25,9},{2,18},{10... | collective-permute-start | bytes 159752 | tf_op jit(solution)/shard_map/ppermute | solution.py:455
  96.1 1.4 %collective-permute-start.13 = (f32[104,128]{1,0:T(8,128)S(1)}, f32[104,128]{1,0:T(8,128)S(1)}, u32[]{:S(2)}, u32[]{:S(2)}) collective-permute-start(f32[104,128]{1,0:T(8,128)S(1)} %get-tuple-element.32), channel_id=1, source_target_pairs={{0,24},{8,16},{16,8},{24,0},{1,25},{9,17},{17,9},{25,1},{2,26},{10... | collective-permute-start | bytes 159752 | tf_op jit(solution)/shard_map/ppermute | solution.py:455
  97.5 0.8 and_select_fusion
  98.3 0.0 collective-permute-done.11
  98.3 0.0 collective-permute-done.12
  98.3 3.8 %collective-permute-done.13 = f32[104,128]{1,0:T(8,128)S(1)} collective-permute-done((f32[104,128]{1,0:T(8,128)S(1)}, f32[104,128]{1,0:T(8,128)S(1)}, u32[]{:S(2)}, u32[]{:S(2)}) %collective-permute-start.13) | collective-permute-done | bytes 53280 | tf_op jit(solution)/shard_map/ppermute | solution.py:455
  102.1 0.6 slice_bitcast_fusion.4
  102.7 0.6 slice.82
  103.3 0.6 slice.80
  104.0 0.6 slice.85
  (19 shorter events, 0.1 us)
Async XLA Ops:
  1.5 5.7 %copy-start.2 = (s32[2,16]{1,0:T(2,128)S(1)}, s32[2,16]{1,0:T(2,128)}, u32[]{:S(2)}) copy-start(s32[2,16]{1,0:T(2,128)} %live_ref.3) | copy-start | bytes 388
  1.5 7.2 %collective-permute-start = (f32[104,128]{1,0:T(8,128)S(1)}, f32[104,128]{1,0:T(8,128)S(1)}, u32[]{:S(2)}, u32[]{:S(2)}) collective-permute-start(f32[104,128]{1,0:T(8,128)S(1)} %reshape.157), channel_id=1, source_target_pairs={{0,8},{8,0},{16,24},{24,16},{1,9},{9,1},{17,25},{25,17},{2,10},{10... | collective-permute-start | bytes 159752 | tf_op jit(solution)/shard_map/ppermute | solution.py:455
  4.6 6.1 %collective-permute-start.1 = (f32[104,128]{1,0:T(8,128)S(1)}, f32[104,128]{1,0:T(8,128)S(1)}, u32[]{:S(2)}, u32[]{:S(2)}) collective-permute-start(f32[104,128]{1,0:T(8,128)S(1)} %reshape.157), channel_id=1, source_target_pairs={{0,16},{8,24},{16,0},{24,8},{1,17},{9,25},{17,1},{25,9},{2,18},{10... | collective-permute-start | bytes 159752 | tf_op jit(solution)/shard_map/ppermute | solution.py:455
  7.2 5.9 %collective-permute-start.2 = (f32[104,128]{1,0:T(8,128)S(1)}, f32[104,128]{1,0:T(8,128)S(1)}, u32[]{:S(2)}, u32[]{:S(2)}) collective-permute-start(f32[104,128]{1,0:T(8,128)S(1)} %reshape.157), channel_id=1, source_target_pairs={{0,24},{8,16},{16,8},{24,0},{1,25},{9,17},{17,9},{25,1},{2,26},{10... | collective-permute-start | bytes 159752 | tf_op jit(solution)/shard_map/ppermute | solution.py:455
  7.3 0.7 copy-start.4
  13.1 10.0 %collective-permute-start.3 = (f32[424,128]{1,0:T(8,128)S(1)}, f32[424,128]{1,0:T(8,128)S(1)}, u32[]{:S(2)}, u32[]{:S(2)}) collective-permute-start(f32[424,128]{1,0:T(8,128)S(1)} %constant_dynamic-update-slice_fusion), channel_id=1, source_target_pairs={{0,2},{1,3},{2,0},{3,1},{4,6},{5,7},{6,4},{7,5},{8,10},{9,11},{10,... | collective-permute-start | bytes 651272 | tf_op jit(solution)/shard_map/ppermute | solution.py:455
  14.7 9.9 %collective-permute-start.4 = (f32[424,128]{1,0:T(8,128)S(1)}, f32[424,128]{1,0:T(8,128)S(1)}, u32[]{:S(2)}, u32[]{:S(2)}) collective-permute-start(f32[424,128]{1,0:T(8,128)S(1)} %constant_dynamic-update-slice_fusion), channel_id=1, source_target_pairs={{0,4},{1,5},{2,6},{3,7},{4,0},{5,1},{6,2},{7,3},{8,12},{9,13},{10,... | collective-permute-start | bytes 651272 | tf_op jit(solution)/shard_map/ppermute | solution.py:455
  16.2 8.4 %collective-permute-start.5 = (f32[424,128]{1,0:T(8,128)S(1)}, f32[424,128]{1,0:T(8,128)S(1)}, u32[]{:S(2)}, u32[]{:S(2)}) collective-permute-start(f32[424,128]{1,0:T(8,128)S(1)} %constant_dynamic-update-slice_fusion), channel_id=1, source_target_pairs={{0,6},{1,7},{2,4},{3,5},{4,2},{5,3},{6,0},{7,1},{8,14},{9,15},{10,... | collective-permute-start | bytes 651272 | tf_op jit(solution)/shard_map/ppermute | solution.py:455
  24.7 2.5 %copy-start = (f32[4,424,128]{2,1,0:T(8,128)}, f32[4,424,128]{2,1,0:T(8,128)S(1)}, u32[]{:S(2)}) copy-start(f32[4,424,128]{2,1,0:T(8,128)S(1)} %pad_maximum_fusion.mine_ref) | copy-start | bytes 2605060
  24.7 2.5 %collective-permute-start.6 = (f32[4,424,128]{2,1,0:T(8,128)S(1)}, f32[4,424,128]{2,1,0:T(8,128)S(1)}, u32[]{:S(2)}, u32[]{:S(2)}) collective-permute-start(f32[4,424,128]{2,1,0:T(8,128)S(1)} %pad_maximum_fusion.mine_ref), channel_id=1, source_target_pairs={{0,1},{1,0},{2,3},{3,2},{4,5},{5,4},{6,7},{7,6},{8,9},{9,8},{10,11... | collective-permute-start | bytes 2605064 | tf_op jit(solution)/shard_map/ppermute | solution.py:455
  27.2 1.0 copy-start.1
  69.7 0.7 copy-start.3
  69.7 2.6 %collective-permute-start.7 = (f32[16,104,128]{2,1,0:T(8,128)}, f32[16,104,128]{2,1,0:T(8,128)S(1)}, u32[]{:S(2)}, u32[]{:S(2)}) collective-permute-start(f32[16,104,128]{2,1,0:T(8,128)} %get-tuple-element.25), channel_id=1, source_target_pairs={{0,1},{1,0},{2,3},{3,2},{4,5},{5,4},{6,7},{7,6},{8,9},{9,8},{10,11... | collective-permute-start | bytes 2555912 | tf_op jit(solution)/shard_map/ppermute | solution.py:455
  73.6 15.0 %collective-permute-start.10 = (f32[4,104,128]{2,1,0:T(8,128)S(1)}, f32[4,104,128]{2,1,0:T(8,128)S(1)}, u32[]{:S(2)}, u32[]{:S(2)}) collective-permute-start(f32[4,104,128]{2,1,0:T(8,128)S(1)} %get-tuple-element.29), channel_id=1, source_target_pairs={{0,6},{1,7},{2,4},{3,5},{4,2},{5,3},{6,0},{7,1},{8,14},{9,15},{10,... | collective-permute-start | bytes 638984 | tf_op jit(solution)/shard_map/ppermute | solution.py:455
  82.5 10.3 %collective-permute-start.8 = (f32[4,104,128]{2,1,0:T(8,128)S(1)}, f32[4,104,128]{2,1,0:T(8,128)S(1)}, u32[]{:S(2)}, u32[]{:S(2)}) collective-permute-start(f32[4,104,128]{2,1,0:T(8,128)S(1)} %get-tuple-element.28), channel_id=1, source_target_pairs={{0,2},{1,3},{2,0},{3,1},{4,6},{5,7},{6,4},{7,5},{8,10},{9,11},{10,... | collective-permute-start | bytes 638984 | tf_op jit(solution)/shard_map/ppermute | solution.py:455
  82.6 10.2 %collective-permute-start.9 = (f32[4,104,128]{2,1,0:T(8,128)S(1)}, f32[4,104,128]{2,1,0:T(8,128)S(1)}, u32[]{:S(2)}, u32[]{:S(2)}) collective-permute-start(f32[4,104,128]{2,1,0:T(8,128)S(1)} %get-tuple-element.30), channel_id=1, source_target_pairs={{0,4},{1,5},{2,6},{3,7},{4,0},{5,1},{6,2},{7,3},{8,12},{9,13},{10,... | collective-permute-start | bytes 638984 | tf_op jit(solution)/shard_map/ppermute | solution.py:455
  92.9 5.4 %collective-permute-start.11 = (f32[104,128]{1,0:T(8,128)S(1)}, f32[104,128]{1,0:T(8,128)S(1)}, u32[]{:S(2)}, u32[]{:S(2)}) collective-permute-start(f32[104,128]{1,0:T(8,128)S(1)} %get-tuple-element.31), channel_id=1, source_target_pairs={{0,8},{8,0},{16,24},{24,16},{1,9},{9,1},{17,25},{25,17},{2,10},{10... | collective-permute-start | bytes 159752 | tf_op jit(solution)/shard_map/ppermute | solution.py:455
  93.0 5.3 %collective-permute-start.12 = (f32[104,128]{1,0:T(8,128)S(1)}, f32[104,128]{1,0:T(8,128)S(1)}, u32[]{:S(2)}, u32[]{:S(2)}) collective-permute-start(f32[104,128]{1,0:T(8,128)S(1)} %get-tuple-element.33), channel_id=1, source_target_pairs={{0,16},{8,24},{16,0},{24,8},{1,17},{9,25},{17,1},{25,9},{2,18},{10... | collective-permute-start | bytes 159752 | tf_op jit(solution)/shard_map/ppermute | solution.py:455
  96.1 5.9 %collective-permute-start.13 = (f32[104,128]{1,0:T(8,128)S(1)}, f32[104,128]{1,0:T(8,128)S(1)}, u32[]{:S(2)}, u32[]{:S(2)}) collective-permute-start(f32[104,128]{1,0:T(8,128)S(1)} %get-tuple-element.32), channel_id=1, source_target_pairs={{0,24},{8,16},{16,8},{24,0},{1,25},{9,17},{17,9},{25,1},{2,26},{10... | collective-permute-start | bytes 159752 | tf_op jit(solution)/shard_map/ppermute | solution.py:455
where the time goes:
time: 106 us; the launch traced here: 105 us
  Pallas kernels  46.6 us (44%)
  starting transfers between devices  23.5 us (22%)
  waiting for transfers between devices  22 us (21%)
  local copies, waits for them, and re-layouts  6.94 us (7%)
  other arithmetic  4.77 us (4%)
    pallas_call x1, Pallas kernels, shards(): splat(cam, rows, live_count, group, mine, other, target.transpose(0, 2, 1...  41.5 us
    ppermute x14, starting transfers between devices, swap(): return lax.ppermute(array, axis, [(i, i ^ mask) for i in range(size)])  23.5 us
    ppermute x14, waiting for transfers between devices, swap(): return lax.ppermute(array, axis, [(i, i ^ mask) for i in range(size)])  22 us
    pallas_call x1, Pallas kernels, shards(): prep(me[None], live_count, camera, intersection_ids.reshape(tiles, slots)...  5.1 us
    unnamed x16, local copies, waits for them, and re-layouts  4.41 us
  transfers between devices with their start and end apart: 14, of which 9 were waited for; matrix products, arithmetic and copies ran while one was open for 4% of the time, Pallas kernels for 5%

commit v1 on v0

--- a/solution.py
+++ b/solution.py
@@ -1,3 +1,4 @@
+import functools
 from functools import partial
 import math
 
@@ -15,7 +16,7 @@
 GROUPS = 8
 ACCS = 4
 UNROLL = 4
-BATCH = 2
+BATCH = 4
 LOG2E = math.log2(math.e)
 OFF = -1e4
 
@@ -143,7 +144,17 @@
 
     lax.fori_loop(0, tiles // UNROLL, some_tiles, 0)
     codes = code_ref[...].astype(jnp.int32)
-    row_ref[...] = codes >> 3
+    row_ref[0:tiles, :] = codes >> 3
+    lane = lax.broadcasted_iota(jnp.int32, (tiles, slots), 1)
+    above = lax.broadcasted_iota(jnp.int32, (tiles, slots), 0)
+    across = jnp.full((tiles, slots), -1, jnp.int32)
+    for t in range(tiles):
+        across = jnp.where(lane == t, live_ref[t // tiles_view, t % tiles_view], across)
+    ahead = (across > live) | ((across == live) & (lane < above))
+    rank = jnp.sum(ahead.astype(jnp.int32), axis=1, keepdims=True)
+    ranked = jnp.sum(jnp.where(rank == lane, above, 0), axis=0, keepdims=True)
+    large = jnp.sum((across > slots // 2).astype(jnp.int32), axis=1, keepdims=True)[0:1]
+    row_ref[tiles : tiles + 1, :] = jnp.where(lane[0:1] == tiles, large, ranked)
     pos = lax.broadcasted_iota(jnp.int32, (tiles, slots), 1)
     here = (pos >> 3 < rows) & ((pos & 7) * rows + (pos >> 3) < live)
     group_ref[...] = jnp.where(here, codes & 7, GROUPS)
@@ -191,22 +202,37 @@
     def live_of(t):
         return live_ref[lax.div(t, tiles_view), lax.rem(t, tiles_view)]
 
+    def in_turn(body):
+        def trip(s, _, positions):
+            body([row_ref[tiles * slots + s * BATCH + g] for g in range(BATCH)], positions)
+            return 0
+
+        large = lax.div(row_ref[tiles * slots + tiles] + (BATCH - 1), BATCH)
+        lax.fori_loop(0, large, partial(trip, positions=slots), 0)
+        lax.fori_loop(large, tiles // BATCH, partial(trip, positions=slots // 2), 0)
+
     sub = lax.broadcasted_iota(jnp.int32, (GROUPS, slots), 0)
 
-    def fetch(t, _):
-        def copy(i):
-            for k in range(GROUPS):
-                buf[pl.ds(i * GROUPS + k, 1), :] = table[pl.ds(row_ref[t * slots + i * GROUPS + k], 1), :]
-
-        repeat(chunk_rows(live_of(t)), 4, copy)
-        turned = jnp.transpose(buf[...])
-        mine = sub == group_ref[pl.ds(t, 1), :]
-        for f in range(FIELDS):
-            part = jnp.where(mine, turned[f * GROUPS : (f + 1) * GROUPS], 0.0)
-            raw[f, pl.ds(t, 1), :] = jnp.sum(part, axis=0, keepdims=True)
-        return 0
-
-    lax.fori_loop(0, tiles, fetch, 0)
+    def widen(row):
+        spare = slots - row.shape[1]
+        return jnp.concatenate([row, jnp.zeros((1, spare), F32)], axis=1) if spare else row
+
+    def fetch(tile, positions):
+        for g, t in enumerate(tile):
+
+            def copy(i, t=t, g=g):
+                for k in range(GROUPS):
+                    buf[g, pl.ds(i * GROUPS + k, 1), :] = table[pl.ds(row_ref[t * slots + i * GROUPS + k], 1), :]
+
+            repeat(chunk_rows(live_of(t)), 4, copy)
+        for g, t in enumerate(tile):
+            turned = jnp.transpose(buf[g, 0:positions, :])
+            mine = sub[:, 0:positions] == group_ref[pl.ds(t, 1), :][:, 0:positions]
+            for f in range(FIELDS):
+                part = jnp.where(mine, turned[f * GROUPS : (f + 1) * GROUPS], 0.0)
+                raw[f, pl.ds(t, 1), :] = widen(jnp.sum(part, axis=0, keepdims=True))
+
+    in_turn(fetch)
 
     def project(v):
         block = slice(v * tiles_view, (v + 1) * tiles_view)
@@ -249,36 +275,37 @@
 
     lane_row = lax.broadcasted_iota(jnp.int32, (GROUPS, pixels), 0)
     own_chunk = (lax.broadcasted_iota(jnp.int32, (GROUPS, slots), 1) & 7) == sub
-    zero_rows = jnp.zeros((8, slots), F32)
     zero_pix = jnp.zeros((8, pixels), F32)
 
     def paired(a, b):
         return a + pltpu.roll(b, 3, 0)
 
-    def render(s, _):
-        tile = [s * BATCH + g for g in range(BATCH)]
-        blocks = [(chunk_rows(live_of(t)) + 3) >> 2 for t in tile]
+    def render(tile, positions):
+        zero_rows = jnp.zeros((8, positions), F32)
+        used = slice(0, positions)
+        blocks = (chunk_rows(functools.reduce(jnp.maximum, [live_of(t) for t in tile])) + 3) >> 2
         for g, t in enumerate(tile):
             for n in range(6):
                 row_s[g, n : n + 1, :] = rec[n, pl.ds(t, 1), :]
             for c in range(3):
                 row_s[g, 8 + c : 9 + c, :] = rec[6 + c, pl.ds(t, 1), :]
         for g in range(BATCH):
-            lhs = jnp.concatenate(pieces_of(row_s[g, 0:8, :], 3) + [zero_rows], axis=0).astype(BF16)
-            c_s[g] = dot_tn(lhs, mono_ref[...])
-        colour = [pieces_of(row_s[g, 8:16, :], 3) for g in range(BATCH)]
-
-        lead = []
-        for g in range(BATCH):
-
-            def through(i, prod, g=g):
-                rows = pl.ds(pl.multiple_of(i * 32, 32), 32)
+            lhs = jnp.concatenate(pieces_of(row_s[g, 0:8, used], 3) + [zero_rows], axis=0).astype(BF16)
+            c_s[g, used, :] = dot_tn(lhs, mono_ref[...])
+        colour = [pieces_of(row_s[g, 8:16, used], 3) for g in range(BATCH)]
+
+        def through(i, prods):
+            rows = pl.ds(pl.multiple_of(i * 32, 32), 32)
+            out = []
+            for g in range(BATCH):
                 cover = jnp.exp2(c_s[g, rows, :])
                 c_s[g, rows, :] = cover
                 keep = 1.0 - cover
-                return prod * ((keep[0:8] * keep[8:16]) * (keep[16:24] * keep[24:32]))
-
-            lead.append(lax.fori_loop(0, blocks[g], through, jnp.ones((GROUPS, pixels), F32)))
+                out.append(prods[g] * ((keep[0:8] * keep[8:16]) * (keep[16:24] * keep[24:32])))
+            return tuple(out)
+
+        ones = jnp.ones((GROUPS, pixels), F32)
+        lead = list(lax.fori_loop(0, blocks, through, (ones,) * BATCH))
         for g in range(BATCH):
             scan = lead[g]
             for step in (1, 2, 4):
@@ -293,29 +320,30 @@
                 out.append(weight)
             return out, prod
 
-        for g in range(BATCH):
-
-            def weigh(i, prod, g=g):
-                rows = pl.ds(pl.multiple_of(i * 32, 32), 32)
-                parts, prod = weights(c_s[g, rows, :], prod)
+        def weigh(i, prods):
+            rows = pl.ds(pl.multiple_of(i * 32, 32), 32)
+            out = []
+            for g in range(BATCH):
+                parts, prod = weights(c_s[g, rows, :], prods[g])
                 weight = jnp.concatenate(parts, axis=0)
                 high = weight.astype(BF16)
                 w_hi[g, rows, :] = high
                 w_lo[g, rows, :] = (weight - high.astype(F32)).astype(BF16)
-                return prod
-
-            lax.fori_loop(0, blocks[g], weigh, lead[g])
+                out.append(prod)
+            return tuple(out)
+
+        lax.fori_loop(0, blocks, weigh, tuple(lead))
 
         after = []
         for g, t in enumerate(tile):
             v, tl = lax.div(t, tiles_view), lax.rem(t, tiles_view)
             spread = [
-                jnp.where(own_chunk, jnp.broadcast_to(piece[c : c + 1], (GROUPS, slots)), 0.0)
+                jnp.where(own_chunk[:, used], jnp.broadcast_to(piece[c : c + 1], (GROUPS, positions)), 0.0)
                 for c in range(3)
                 for piece in colour[g]
             ]
             lhs = jnp.concatenate(spread + [zero_rows], axis=0).astype(BF16)
-            image = dot_nn(lhs, w_hi[g]) + dot_nn(lhs, w_lo[g])
+            image = dot_nn(lhs, w_hi[g, used, :]) + dot_nn(lhs, w_lo[g, used, :])
             rest = jnp.zeros((GROUPS, pixels), F32)
             for c in range(3):
                 part = image[24 * c : 24 * c + 8] + image[24 * c + 8 : 24 * c + 16] + image[24 * c + 16 : 24 * c + 24]
@@ -333,13 +361,13 @@
             m1, m2, m3 = missed[g]
             lhs = jnp.concatenate([paired(c1, c1), paired(c2, c1), paired(c2, c3), zero_rows], axis=0)
             rhs = jnp.concatenate([paired(m1, m2), paired(m1, m3), paired(m2, m1), zero_pix], axis=0)
-            h_s[g] = dot_tn(lhs.astype(BF16), rhs.astype(BF16))
-
-        for g in range(BATCH):
-
-            def settle(i, carry, g=g):
-                prod, tail = carry
-                rows = pl.ds(pl.multiple_of(i * 32, 32), 32)
+            h_s[g, used, :] = dot_tn(lhs.astype(BF16), rhs.astype(BF16))
+
+        def settle(i, carry):
+            rows = pl.ds(pl.multiple_of(i * 32, 32), 32)
+            out = []
+            for g in range(BATCH):
+                prod, tail = carry[g]
                 cover = c_s[g, rows, :]
                 pull = h_s[g, rows, :]
                 parts, prod = weights(cover, prod)
@@ -357,24 +385,24 @@
                 g_1[g, rows, :] = high
                 g_2[g, rows, :] = middle
                 g_3[g, rows, :] = (rest - middle.astype(F32)).astype(BF16)
-                return prod, tail
-
-            lax.fori_loop(0, blocks[g], settle, (lead[g], after[g]))
+                out.append((prod, tail))
+            return tuple(out)
+
+        lax.fori_loop(0, blocks, settle, tuple(zip(lead, after)))
         mono = mono_ref[0:16, :]
         for g in range(BATCH):
-            moments = dot_nt(mono, g_1[g]) + dot_nt(mono, g_2[g]) + dot_nt(mono, g_3[g])
+            moments = dot_nt(mono, g_1[g, used, :]) + dot_nt(mono, g_2[g, used, :]) + dot_nt(mono, g_3[g, used, :])
             miss_lhs = jnp.concatenate(missed[g] + [zero_pix], axis=0).astype(BF16)
-            tint = dot_nt(miss_lhs, w_hi[g]) + dot_nt(miss_lhs, w_lo[g])
-            row_s[g, 0:8, :] = moments[0:8]
-            row_s[g, 8:16, :] = tint[0:8] + tint[8:16] + tint[16:24]
+            tint = dot_nt(miss_lhs, w_hi[g, used, :]) + dot_nt(miss_lhs, w_lo[g, used, :])
+            row_s[g, 0:8, used] = moments[0:8]
+            row_s[g, 8:16, used] = tint[0:8] + tint[8:16] + tint[16:24]
         for g, t in enumerate(tile):
             for n in range(6):
                 mom[n, pl.ds(t, 1), :] = row_s[g, n : n + 1, :]
             for c in range(3):
                 mom[6 + c, pl.ds(t, 1), :] = row_s[g, 8 + c : 9 + c, :]
-        return 0
-
-    lax.fori_loop(0, tiles // BATCH, render, 0)
+
+    in_turn(render)
 
     for v in range(views):
         here, cam, block, u, w, (d0, d1, d2), f0, f1, (ka, kb, kc) = project(v)
@@ -405,27 +433,28 @@
         for c in range(3):
             grad[10 + c, block, :] = mom[6 + c, block, :]
 
-    def give(t, _):
-        mine = sub == group_ref[pl.ds(t, 1), :]
-        spread = [
-            jnp.where(mine, jnp.broadcast_to(grad[f, pl.ds(t, 1), :], (GROUPS, slots)), 0.0)
-            for f in range(FIELDS)
-        ]
-        spread.append(jnp.zeros((lanes - used, slots), F32))
-        buf[...] = jnp.transpose(jnp.concatenate(spread, axis=0))
-
-        def add(i):
-            for k in range(0, GROUPS, len(accs)):
-                where = [row_ref[t * slots + i * GROUPS + k + n] for n in range(len(accs))]
-                olds = [accs[n][pl.ds(where[n], 1), :] for n in range(len(accs))]
-                news = [buf[pl.ds(i * GROUPS + k + n, 1), :] for n in range(len(accs))]
-                for n in range(len(accs)):
-                    accs[n][pl.ds(where[n], 1), :] = olds[n] + news[n]
-
-        repeat(chunk_rows(live_of(t)), 4, add)
-        return 0
-
-    lax.fori_loop(0, tiles, give, 0)
+    def give(tile, positions):
+        for g, t in enumerate(tile):
+            mine = sub[:, 0:positions] == group_ref[pl.ds(t, 1), :][:, 0:positions]
+            spread = [
+                jnp.where(mine, jnp.broadcast_to(grad[f, pl.ds(t, 1), :][:, 0:positions], (GROUPS, positions)), 0.0)
+                for f in range(FIELDS)
+            ]
+            spread.append(jnp.zeros((lanes - used, positions), F32))
+            buf[g, 0:positions, :] = jnp.transpose(jnp.concatenate(spread, axis=0))
+        for g, t in enumerate(tile):
+
+            def add(i, t=t, g=g):
+                for k in range(0, GROUPS, len(accs)):
+                    where = [row_ref[t * slots + i * GROUPS + k + n] for n in range(len(accs))]
+                    olds = [accs[n][pl.ds(where[n], 1), :] for n in range(len(accs))]
+                    news = [buf[g, pl.ds(i * GROUPS + k + n, 1), :] for n in range(len(accs))]
+                    for n in range(len(accs)):
+                        accs[n][pl.ds(where[n], 1), :] = olds[n] + news[n]
+
+            repeat(chunk_rows(live_of(t)), 4, add)
+
+    in_turn(give)
 
     def finish(d, _):
         for base, ref in ((0, grad_mine_ref), (half, grad_other_ref)):
@@ -480,7 +509,7 @@
             (log2_of(own_count), log2_of(lanes), log2_of(view_group), log2_of(tile_group), tiles_view),
         ),
         out_shape=[
-            jax.ShapeDtypeStruct((tiles, slots), jnp.int32),
+            jax.ShapeDtypeStruct((tiles + 8, slots), jnp.int32),
             jax.ShapeDtypeStruct((tiles, slots), jnp.int32),
             jax.ShapeDtypeStruct((views * 8,), F32),
         ],
@@ -516,6 +545,8 @@
     table_rows = devices * lanes
     square = (BATCH, slots, pixels)
     half = (chips * view_group, FIELDS * GROUPS, lanes)
+    accs = ACCS if devices <= 32 else 2
+    room = 4 * table_rows * lanes * (accs + 2) + 16 * 1024 * 1024
     splat = pl.pallas_call(
         partial(splat_kernel, (views, tiles_view, slots, pixels, lanes, view_group)),
         out_shape=[
@@ -527,7 +558,7 @@
         out_specs=[vmem] * 3,
         scratch_shapes=[
             pltpu.VMEM((table_rows, lanes), F32),
-            pltpu.VMEM((slots, lanes), F32),
+            pltpu.VMEM((BATCH, slots, lanes), F32),
             pltpu.VMEM((FIELDS, tiles, slots), F32),
             pltpu.VMEM((9, tiles, slots), F32),
             pltpu.VMEM((9, tiles, slots), F32),
@@ -537,8 +568,8 @@
         ]
         + [pltpu.VMEM(square, BF16)] * 5
         + [pltpu.VMEM((BATCH, 16, slots), F32), pltpu.VMEM((BATCH, 8, pixels), F32)]
-        + [pltpu.VMEM((table_rows, lanes), F32)] * (ACCS if devices <= 32 else 2),
-        compiler_params=pltpu.CompilerParams(vmem_limit_bytes=60 * 1024 * 1024),
+        + [pltpu.VMEM((table_rows, lanes), F32)] * accs,
+        compiler_params=pltpu.CompilerParams(vmem_limit_bytes=room),
         name="splat",
     )
     rendered, grad_mine, grad_other = splat(

time: 106 us -> 90.6 us (0.85); the launches traced: 105 us -> 90.8 us
  Pallas kernels: 46.6 us -> 31.5 us
  starting transfers between devices: 23.5 us -> 27.3 us
  local copies, waits for them, and re-layouts: 6.94 us -> 4.74 us
  other arithmetic: 4.77 us -> 3.33 us
  waiting for transfers between devices: 22 us -> 23.1 us
    pallas_call x1, Pallas kernels: 41.5 us -> 26.3 us  [shards(): splat(cam, rows, live_count, group, mine, other, target.transpose(0, 2, 1...]
    ppermute x14, starting transfers between devices: 23.5 us -> 27.3 us  [swap(): return lax.ppermute(array, axis, [(i, i ^ mask) for i in range(size)])]
    unnamed x16 -> x20, local copies, waits for them, and re-layouts: 4.41 us -> 2.21 us
    ppermute x14, waiting for transfers between devices: 22 us -> 23.1 us  [swap(): return lax.ppermute(array, axis, [(i, i ^ mask) for i in range(size)])]
  transfers between devices with their start and end apart: 14 -> 14, of which waited for: 9 -> 9; matrix products, arithmetic and copies ran while one was open for 4% -> 3% of each run, Pallas kernels for 5% -> 6%
where the time goes in v1:
time: 90.6 us; the launch traced here: 90.8 us
  Pallas kernels  31.5 us (35%)
  starting transfers between devices  27.3 us (30%)
  waiting for transfers between devices  23.1 us (25%)
  local copies, waits for them, and re-layouts  4.74 us (5%)
  other arithmetic  3.33 us (4%)
    ppermute x14, starting transfers between devices, swap(): return lax.ppermute(array, axis, [(i, i ^ mask) for i in range(size)])  27.3 us
    pallas_call x1, Pallas kernels, shards(): splat(cam, rows, live_count, group, mine, other, target.transpose(0, 2, 1...  26.3 us
    ppermute x14, waiting for transfers between devices, swap(): return lax.ppermute(array, axis, [(i, i ^ mask) for i in range(size)])  23.1 us
    pallas_call x1, Pallas kernels, shards(): prep(me[None], live_count, camera, intersection_ids.reshape(tiles, slots)...  5.21 us
    unnamed x20, local copies, waits for them, and re-layouts  2.21 us
  transfers between devices with their start and end apart: 14, of which 9 were waited for; matrix products, arithmetic and copies ran while one was open for 3% of the time, Pallas kernels for 6%

profile of v1, /device:TPU:0, one launch (start us, length us, event | category | flops | bytes accessed | tf_op | source)
XLA Modules:
  0.0 90.8 jit_solution(9755061004250154117)
XLA Ops:
  0.6 0.8 pad_maximum_fusion.1
  1.5 0.0 copy-start.3
  1.5 3.1 %collective-permute-start = (f32[104,128]{1,0:T(8,128)S(1)}, f32[104,128]{1,0:T(8,128)S(1)}, u32[]{:S(2)}, u32[]{:S(2)}) collective-permute-start(f32[104,128]{1,0:T(8,128)S(1)} %reshape.157), channel_id=1, source_target_pairs={{0,8},{8,0},{16,24},{24,16},{1,9},{9,1},{17,25},{25,17},{2,10},{10... | collective-permute-start | bytes 159752 | tf_op jit(solution)/shard_map/ppermute | solution.py:484
  4.6 2.6 %collective-permute-start.1 = (f32[104,128]{1,0:T(8,128)S(1)}, f32[104,128]{1,0:T(8,128)S(1)}, u32[]{:S(2)}, u32[]{:S(2)}) collective-permute-start(f32[104,128]{1,0:T(8,128)S(1)} %reshape.157), channel_id=1, source_target_pairs={{0,16},{8,24},{16,0},{24,8},{1,17},{9,25},{17,1},{25,9},{2,18},{10... | collective-permute-start | bytes 159752 | tf_op jit(solution)/shard_map/ppermute | solution.py:484
  7.2 0.0 collective-permute-start.2
  7.2 0.1 reduce_sum.9
  7.3 0.0 copy-start.6
  7.4 0.7 copy-done.6
  8.0 0.7 copy.16.camera_ref
  8.7 0.0 collective-permute-done
  8.7 1.9 %collective-permute-done.1 = f32[104,128]{1,0:T(8,128)S(1)} collective-permute-done((f32[104,128]{1,0:T(8,128)S(1)}, f32[104,128]{1,0:T(8,128)S(1)}, u32[]{:S(2)}, u32[]{:S(2)}) %collective-permute-start.1) | collective-permute-done | bytes 53280 | tf_op jit(solution)/shard_map/ppermute | solution.py:484
  10.7 2.5 %collective-permute-done.2 = f32[104,128]{1,0:T(8,128)S(1)} collective-permute-done((f32[104,128]{1,0:T(8,128)S(1)}, f32[104,128]{1,0:T(8,128)S(1)}, u32[]{:S(2)}, u32[]{:S(2)}) %collective-permute-start.2) | collective-permute-done | bytes 53280 | tf_op jit(solution)/shard_map/ppermute | solution.py:484
  13.1 1.6 %collective-permute-start.3 = (f32[424,128]{1,0:T(8,128)S(1)}, f32[424,128]{1,0:T(8,128)S(1)}, u32[]{:S(2)}, u32[]{:S(2)}) collective-permute-start(f32[424,128]{1,0:T(8,128)S(1)} %constant_dynamic-update-slice_fusion), channel_id=1, source_target_pairs={{0,2},{1,3},{2,0},{3,1},{4,6},{5,7},{6,4},{7,5},{8,10},{9,11},{10,... | collective-permute-start | bytes 651272 | tf_op jit(solution)/shard_map/ppermute | solution.py:484
  14.7 1.5 %collective-permute-start.4 = (f32[424,128]{1,0:T(8,128)S(1)}, f32[424,128]{1,0:T(8,128)S(1)}, u32[]{:S(2)}, u32[]{:S(2)}) collective-permute-start(f32[424,128]{1,0:T(8,128)S(1)} %constant_dynamic-update-slice_fusion), channel_id=1, source_target_pairs={{0,4},{1,5},{2,6},{3,7},{4,0},{5,1},{6,2},{7,3},{8,12},{9,13},{10,... | collective-permute-start | bytes 651272 | tf_op jit(solution)/shard_map/ppermute | solution.py:484
  16.2 0.5 collective-permute-start.5
  16.7 5.2 %prep.1 = (s32[40,256]{1,0:T(8,128)}, s32[32,256]{1,0:T(8,128)}, f32[16]{0:T(128)}) custom-call(s32[1]{0:T(128)} %bitcast.6.me_ref, s32[2,16]{1,0:T(2,128)} %live_ref.3, f32[8,2,4]{2,1,0:T(2,128)} %copy.16.camera_ref, s32[32,256]{1,0:T(8,128)} %bitcast.97, s32[32,256]{1,0:T(8,128)} %bitcast.98), custom_call_target="tpu_custom_call" | custom-call | flops 8000000000 | bytes 131072 | tf_op jit(solution)/shard_map/prep/pallas_call | solution.py:535
  21.9 0.8 copy.17
  22.7 0.0 collective-permute-done.3
  22.7 1.9 %collective-permute-done.4 = f32[424,128]{1,0:T(8,128)S(1)} collective-permute-done((f32[424,128]{1,0:T(8,128)S(1)}, f32[424,128]{1,0:T(8,128)S(1)}, u32[]{:S(2)}, u32[]{:S(2)}) %collective-permute-start.4) | collective-permute-done | bytes 217120 | tf_op jit(solution)/shard_map/ppermute | solution.py:484
  24.6 0.0 collective-permute-done.5
  24.6 0.1 pad_maximum_fusion.mine_ref
  24.7 0.0 copy-start.5
  24.8 0.1 collective-permute-start.6
  24.8 2.4 %collective-permute-done.6.other_ref = f32[4,424,128]{2,1,0:T(8,128)S(1)} collective-permute-done((f32[4,424,128]{2,1,0:T(8,128)S(1)}, f32[4,424,128]{2,1,0:T(8,128)S(1)}, u32[]{:S(2)}, u32[]{:S(2)}) %collective-permute-start.6) | collective-permute-done | bytes 868384 | tf_op jit(solution)/shard_map/ppermute | solution.py:484
  27.2 0.0 copy-done
  27.3 26.3 %splat.1 = (f32[2,3,16,256]{3,2,1,0:T(8,128)}, f32[16,104,128]{2,1,0:T(8,128)S(1)}, f32[16,104,128]{2,1,0:T(8,128)S(1)}) custom-call(f32[16]{0:T(128)S(1)} %copy-done.5, s32[10240]{0:T(1024)S(1)} %bitcast.88, s32[2,16]{1,0:T(2,128)S(1)} %copy-done.4, s32[32,256]{1,0:T(8,128)S(1)} %copy-done.1, f32[4,424,128]{2,1,0:T(8,128)S(1)} %pad_maximum_fusion.mine_ref, ...), custom_call_target="tpu_custom_call" | custom-call | tf_op jit(solution)/shard_map/splat/pallas_call | solution.py:575
  53.6 0.0 collective-permute-start.7
  53.6 0.2 reduce_window_sum.11
  53.8 2.3 %collective-permute-done.7 = f32[16,104,128]{2,1,0:T(8,128)} collective-permute-done((f32[16,104,128]{2,1,0:T(8,128)S(1)}, f32[16,104,128]{2,1,0:T(8,128)}, u32[]{:S(2)}, u32[]{:S(2)}) %collective-permute-start.7) | collective-permute-done | bytes 852000 | tf_op jit(solution)/shard_map/ppermute | solution.py:484
  56.1 1.2 %add.148 = f32[16,104,128]{2,1,0:T(8,128)S(1)} add(f32[16,104,128]{2,1,0:T(8,128)S(1)} %get-tuple-element.24, f32[16,104,128]{2,1,0:T(8,128)} %collective-permute-done.7) | non-fusion elementwise | flops 212992 | bytes 2555904 | tf_op jit(solution)/shard_map/add | solution.py:597
  57.4 12.9 %collective-permute-start.10 = (f32[4,104,128]{2,1,0:T(8,128)S(1)}, f32[4,104,128]{2,1,0:T(8,128)S(1)}, u32[]{:S(2)}, u32[]{:S(2)}) collective-permute-start(f32[4,104,128]{2,1,0:T(8,128)S(1)} %get-tuple-element.29), channel_id=1, source_target_pairs={{0,6},{1,7},{2,4},{3,5},{4,2},{5,3},{6,0},{7,1},{8,14},{9,15},{10,... | collective-permute-start | bytes 638984 | tf_op jit(solution)/shard_map/ppermute | solution.py:484
  70.3 0.0 collective-permute-start.8
  70.3 0.6 collective-permute-start.9
  70.9 5.5 %collective-permute-done.10 = f32[4,104,128]{2,1,0:T(8,128)S(1)} collective-permute-done((f32[4,104,128]{2,1,0:T(8,128)S(1)}, f32[4,104,128]{2,1,0:T(8,128)S(1)}, u32[]{:S(2)}, u32[]{:S(2)}) %collective-permute-start.10) | collective-permute-done | bytes 213024 | tf_op jit(solution)/shard_map/ppermute | solution.py:484
  76.4 3.5 %collective-permute-done.8 = f32[4,104,128]{2,1,0:T(8,128)S(1)} collective-permute-done((f32[4,104,128]{2,1,0:T(8,128)S(1)}, f32[4,104,128]{2,1,0:T(8,128)S(1)}, u32[]{:S(2)}, u32[]{:S(2)}) %collective-permute-start.8) | collective-permute-done | bytes 213024 | tf_op jit(solution)/shard_map/ppermute | solution.py:484
  79.9 0.7 collective-permute-done.9
  80.6 0.1 fusion.1
  80.7 0.1 collective-permute-start.11
  80.8 0.9 collective-permute-start.12
  81.7 3.5 %collective-permute-start.13 = (f32[104,128]{1,0:T(8,128)S(1)}, f32[104,128]{1,0:T(8,128)S(1)}, u32[]{:S(2)}, u32[]{:S(2)}) collective-permute-start(f32[104,128]{1,0:T(8,128)S(1)} %get-tuple-element.32), channel_id=1, source_target_pairs={{0,24},{8,16},{16,8},{24,0},{1,25},{9,17},{17,9},{25,1},{2,26},{10... | collective-permute-start | bytes 159752 | tf_op jit(solution)/shard_map/ppermute | solution.py:484
  85.1 0.8 and_select_fusion
  85.9 0.0 collective-permute-done.11
  85.9 2.5 %collective-permute-done.12 = f32[104,128]{1,0:T(8,128)S(1)} collective-permute-done((f32[104,128]{1,0:T(8,128)S(1)}, f32[104,128]{1,0:T(8,128)S(1)}, u32[]{:S(2)}, u32[]{:S(2)}) %collective-permute-start.12) | collective-permute-done | bytes 53280 | tf_op jit(solution)/shard_map/ppermute | solution.py:484
  88.4 0.0 collective-permute-done.13
  88.4 0.6 slice_bitcast_fusion.4
  89.0 0.6 slice.82
  89.6 0.6 slice.80
  90.2 0.6 slice.85
  (23 shorter events, 0.2 us)
Async XLA Ops:
  1.5 5.7 %copy-start.3 = (s32[2,16]{1,0:T(2,128)S(1)}, s32[2,16]{1,0:T(2,128)}, u32[]{:S(2)}) copy-start(s32[2,16]{1,0:T(2,128)} %live_ref.3) | copy-start | bytes 388
  1.5 7.2 %collective-permute-start = (f32[104,128]{1,0:T(8,128)S(1)}, f32[104,128]{1,0:T(8,128)S(1)}, u32[]{:S(2)}, u32[]{:S(2)}) collective-permute-start(f32[104,128]{1,0:T(8,128)S(1)} %reshape.157), channel_id=1, source_target_pairs={{0,8},{8,0},{16,24},{24,16},{1,9},{9,1},{17,25},{25,17},{2,10},{10... | collective-permute-start | bytes 159752 | tf_op jit(solution)/shard_map/ppermute | solution.py:484
  4.6 6.1 %collective-permute-start.1 = (f32[104,128]{1,0:T(8,128)S(1)}, f32[104,128]{1,0:T(8,128)S(1)}, u32[]{:S(2)}, u32[]{:S(2)}) collective-permute-start(f32[104,128]{1,0:T(8,128)S(1)} %reshape.157), channel_id=1, source_target_pairs={{0,16},{8,24},{16,0},{24,8},{1,17},{9,25},{17,1},{25,9},{2,18},{10... | collective-permute-start | bytes 159752 | tf_op jit(solution)/shard_map/ppermute | solution.py:484
  7.2 5.9 %collective-permute-start.2 = (f32[104,128]{1,0:T(8,128)S(1)}, f32[104,128]{1,0:T(8,128)S(1)}, u32[]{:S(2)}, u32[]{:S(2)}) collective-permute-start(f32[104,128]{1,0:T(8,128)S(1)} %reshape.157), channel_id=1, source_target_pairs={{0,24},{8,16},{16,8},{24,0},{1,25},{9,17},{17,9},{25,1},{2,26},{10... | collective-permute-start | bytes 159752 | tf_op jit(solution)/shard_map/ppermute | solution.py:484
  7.3 0.7 copy-start.6
  13.1 9.6 %collective-permute-start.3 = (f32[424,128]{1,0:T(8,128)S(1)}, f32[424,128]{1,0:T(8,128)S(1)}, u32[]{:S(2)}, u32[]{:S(2)}) collective-permute-start(f32[424,128]{1,0:T(8,128)S(1)} %constant_dynamic-update-slice_fusion), channel_id=1, source_target_pairs={{0,2},{1,3},{2,0},{3,1},{4,6},{5,7},{6,4},{7,5},{8,10},{9,11},{10,... | collective-permute-start | bytes 651272 | tf_op jit(solution)/shard_map/ppermute | solution.py:484
  14.7 9.9 %collective-permute-start.4 = (f32[424,128]{1,0:T(8,128)S(1)}, f32[424,128]{1,0:T(8,128)S(1)}, u32[]{:S(2)}, u32[]{:S(2)}) collective-permute-start(f32[424,128]{1,0:T(8,128)S(1)} %constant_dynamic-update-slice_fusion), channel_id=1, source_target_pairs={{0,4},{1,5},{2,6},{3,7},{4,0},{5,1},{6,2},{7,3},{8,12},{9,13},{10,... | collective-permute-start | bytes 651272 | tf_op jit(solution)/shard_map/ppermute | solution.py:484
  16.2 8.4 %collective-permute-start.5 = (f32[424,128]{1,0:T(8,128)S(1)}, f32[424,128]{1,0:T(8,128)S(1)}, u32[]{:S(2)}, u32[]{:S(2)}) collective-permute-start(f32[424,128]{1,0:T(8,128)S(1)} %constant_dynamic-update-slice_fusion), channel_id=1, source_target_pairs={{0,6},{1,7},{2,4},{3,5},{4,2},{5,3},{6,0},{7,1},{8,14},{9,15},{10,... | collective-permute-start | bytes 651272 | tf_op jit(solution)/shard_map/ppermute | solution.py:484
  24.6 2.6 %copy-start = (f32[2,16,3,256]{3,1,2,0:T(8,128)S(1)}, f32[2,16,3,256]{3,1,2,0:T(8,128)}, u32[]{:S(2)}) copy-start(f32[2,16,3,256]{3,1,2,0:T(8,128)} %param.15) | copy-start | bytes 294916
  24.6 2.6 %copy-start.1 = (s32[32,256]{1,0:T(8,128)S(1)}, s32[32,256]{1,0:T(8,128)}, u32[]{:S(2)}) copy-start(s32[32,256]{1,0:T(8,128)} %get-tuple-element.21.group_ref) | copy-start | bytes 98308
  24.6 2.6 %copy-start.2 = (bf16[32,256]{1,0:T(8,128)(2,1)S(1)}, bf16[32,256]{1,0:T(8,128)(2,1)}, u32[]{:S(2)}) copy-start(bf16[32,256]{1,0:T(8,128)(2,1)} %constant.40.clone.mono_ref) | copy-start | bytes 49156
  24.7 2.5 %copy-start.4 = (s32[2,16]{1,0:T(2,128)S(1)}, s32[2,16]{1,0:T(2,128)}, u32[]{:S(2)}) copy-start(s32[2,16]{1,0:T(2,128)} %live_ref.3) | copy-start | bytes 388
  24.7 2.5 %copy-start.5 = (f32[16]{0:T(128)S(1)}, f32[16]{0:T(128)}, u32[]{:S(2)}) copy-start(f32[16]{0:T(128)} %get-tuple-element.19.cam_ref) | copy-start | bytes 196
  24.8 2.5 %collective-permute-start.6 = (f32[4,424,128]{2,1,0:T(8,128)S(1)}, f32[4,424,128]{2,1,0:T(8,128)S(1)}, u32[]{:S(2)}, u32[]{:S(2)}) collective-permute-start(f32[4,424,128]{2,1,0:T(8,128)S(1)} %pad_maximum_fusion.mine_ref), channel_id=1, source_target_pairs={{0,1},{1,0},{2,3},{3,2},{4,5},{5,4},{6,7},{7,6},{8,9},{9,8},{10,11... | collective-permute-start | bytes 2605064 | tf_op jit(solution)/shard_map/ppermute | solution.py:484
  53.6 2.5 %collective-permute-start.7 = (f32[16,104,128]{2,1,0:T(8,128)S(1)}, f32[16,104,128]{2,1,0:T(8,128)}, u32[]{:S(2)}, u32[]{:S(2)}) collective-permute-start(f32[16,104,128]{2,1,0:T(8,128)S(1)} %get-tuple-element.25), channel_id=1, source_target_pairs={{0,1},{1,0},{2,3},{3,2},{4,5},{5,4},{6,7},{7,6},{8,9},{9,8},{10,11... | collective-permute-start | bytes 2555912 | tf_op jit(solution)/shard_map/ppermute | solution.py:484
  57.4 19.0 %collective-permute-start.10 = (f32[4,104,128]{2,1,0:T(8,128)S(1)}, f32[4,104,128]{2,1,0:T(8,128)S(1)}, u32[]{:S(2)}, u32[]{:S(2)}) collective-permute-start(f32[4,104,128]{2,1,0:T(8,128)S(1)} %get-tuple-element.29), channel_id=1, source_target_pairs={{0,6},{1,7},{2,4},{3,5},{4,2},{5,3},{6,0},{7,1},{8,14},{9,15},{10,... | collective-permute-start | bytes 638984 | tf_op jit(solution)/shard_map/ppermute | solution.py:484
  70.3 9.7 %collective-permute-start.8 = (f32[4,104,128]{2,1,0:T(8,128)S(1)}, f32[4,104,128]{2,1,0:T(8,128)S(1)}, u32[]{:S(2)}, u32[]{:S(2)}) collective-permute-start(f32[4,104,128]{2,1,0:T(8,128)S(1)} %get-tuple-element.28), channel_id=1, source_target_pairs={{0,2},{1,3},{2,0},{3,1},{4,6},{5,7},{6,4},{7,5},{8,10},{9,11},{10,... | collective-permute-start | bytes 638984 | tf_op jit(solution)/shard_map/ppermute | solution.py:484
  70.3 10.4 %collective-permute-start.9 = (f32[4,104,128]{2,1,0:T(8,128)S(1)}, f32[4,104,128]{2,1,0:T(8,128)S(1)}, u32[]{:S(2)}, u32[]{:S(2)}) collective-permute-start(f32[4,104,128]{2,1,0:T(8,128)S(1)} %get-tuple-element.30), channel_id=1, source_target_pairs={{0,4},{1,5},{2,6},{3,7},{4,0},{5,1},{6,2},{7,3},{8,12},{9,13},{10,... | collective-permute-start | bytes 638984 | tf_op jit(solution)/shard_map/ppermute | solution.py:484
  80.7 5.2 %collective-permute-start.11 = (f32[104,128]{1,0:T(8,128)S(1)}, f32[104,128]{1,0:T(8,128)S(1)}, u32[]{:S(2)}, u32[]{:S(2)}) collective-permute-start(f32[104,128]{1,0:T(8,128)S(1)} %get-tuple-element.31), channel_id=1, source_target_pairs={{0,8},{8,0},{16,24},{24,16},{1,9},{9,1},{17,25},{25,17},{2,10},{10... | collective-permute-start | bytes 159752 | tf_op jit(solution)/shard_map/ppermute | solution.py:484
  80.8 7.6 %collective-permute-start.12 = (f32[104,128]{1,0:T(8,128)S(1)}, f32[104,128]{1,0:T(8,128)S(1)}, u32[]{:S(2)}, u32[]{:S(2)}) collective-permute-start(f32[104,128]{1,0:T(8,128)S(1)} %get-tuple-element.33), channel_id=1, source_target_pairs={{0,16},{8,24},{16,0},{24,8},{1,17},{9,25},{17,1},{25,9},{2,18},{10... | collective-permute-start | bytes 159752 | tf_op jit(solution)/shard_map/ppermute | solution.py:484
  81.7 6.7 %collective-permute-start.13 = (f32[104,128]{1,0:T(8,128)S(1)}, f32[104,128]{1,0:T(8,128)S(1)}, u32[]{:S(2)}, u32[]{:S(2)}) collective-permute-start(f32[104,128]{1,0:T(8,128)S(1)} %get-tuple-element.32), channel_id=1, source_target_pairs={{0,24},{8,16},{16,8},{24,0},{1,25},{9,17},{17,9},{25,1},{2,26},{10... | collective-permute-start | bytes 159752 | tf_op jit(solution)/shard_map/ppermute | solution.py:484

commit v2 on v1

--- a/solution.py
+++ b/solution.py
@@ -77,6 +77,7 @@
     camera_ref,
     ids_ref,
     order_ref,
+    theirs_ref,
     row_ref,
     group_ref,
     cam_ref,
@@ -88,9 +89,10 @@
     order_b,
 ):
     own_bits, lane_bits, view_bits, tile_bits, tiles_view = dims
-    tiles, slots = ids_ref.shape
+    views, _, slots = ids_ref.shape
+    tiles = views * tiles_view
+    kept = tiles_view // 2
     me = me_ref[0]
-    views = tiles // tiles_view
     first = (me >> tile_bits) * views
     for v in range(views):
         for i in range(2):
@@ -99,7 +101,10 @@
     for t in range(tiles):
         live_full[t : t + 1, :] = jnp.full((1, slots), live_ref[t // tiles_view, t % tiles_view], jnp.int32)
     live = live_full[...]
-    order = order_ref[...]
+    parts = []
+    for v in range(views):
+        parts += [order_ref[v, 0:kept, :], theirs_ref[v, kept : 2 * kept, :]]
+    order = jnp.concatenate(parts, axis=0)
     active = order < live
     upper = (
         lax.broadcasted_iota(jnp.int32, (slots, slots), 0)
@@ -112,7 +117,10 @@
         chunk = chunk + (place >= m * rows).astype(jnp.int32)
     rho_ref[...] = jnp.where(active, (place - chunk * rows) * GROUPS + chunk, -1).astype(F32)
     order_b[...] = order.astype(F32)
-    ids = ids_ref[...]
+    parts = []
+    for v in range(views):
+        parts += [ids_ref[v, 0:kept, :], theirs_ref[v, 0:kept, :]]
+    ids = jnp.concatenate(parts, axis=0)
     owner = (ids >> own_bits) ^ me
     local = ids & ((1 << own_bits) - 1)
     xy_bits = tile_bits - 1
@@ -169,15 +177,17 @@
     mine_ref,
     other_ref,
     target_ref,
+    their_target_ref,
     mono_ref,
     image_ref,
+    their_image_ref,
     grad_mine_ref,
     grad_other_ref,
     *scratch,
 ):
     views, tiles_view, slots, pixels, lanes, column = dims
-    table, buf, raw, rec, mom, grad, c_s, h_s, w_hi, w_lo, g_1, g_2, g_3, row_s, row_2 = scratch[:15]
-    accs = scratch[15:]
+    table, buf, raw, rec, mom, grad, c_s, h_s, w_hi, w_lo, g_1, g_2, g_3, row_s, row_2, want, got = scratch[:17]
+    accs = scratch[17:]
     tiles = views * tiles_view
     chips = mine_ref.shape[0]
     half = chips * column
@@ -188,6 +198,10 @@
         acc[...] = jnp.zeros_like(acc)
     for ref in (buf, w_hi, w_lo, g_1, g_2, g_3, row_s, row_2):
         ref[...] = jnp.zeros_like(ref)
+
+    kept = tiles_view // 2
+    want[:, :, 0:kept, :] = target_ref[:, :, 0:kept, :]
+    want[:, :, kept:, :] = their_target_ref[...]
 
     def build(q, _):
         for base, ref in ((0, mine_ref), (half, other_ref)):
@@ -348,8 +362,8 @@
             for c in range(3):
                 part = image[24 * c : 24 * c + 8] + image[24 * c + 8 : 24 * c + 16] + image[24 * c + 16 : 24 * c + 24]
                 whole = jnp.sum(part, axis=0, keepdims=True)
-                image_ref[v, c, pl.ds(tl, 1), :] = whole
-                miss = whole - target_ref[v, c, pl.ds(tl, 1), :]
+                got[v, c, pl.ds(tl, 1), :] = whole
+                miss = whole - want[v, c, pl.ds(tl, 1), :]
                 row_2[g, c : c + 1, :] = miss
                 rest = rest + part * miss
             for step in (1, 2, 4):
@@ -403,6 +417,8 @@
                 mom[6 + c, pl.ds(t, 1), :] = row_s[g, 8 + c : 9 + c, :]
 
     in_turn(render)
+    image_ref[...] = got[:, :, 0:kept, :]
+    their_image_ref[...] = got[:, :, kept:, :]
 
     for v in range(views):
         here, cam, block, u, w, (d0, d1, d2), f0, f1, (ka, kb, kc) = project(v)
@@ -468,6 +484,22 @@
     lax.fori_loop(0, half, finish, 0)
 
 
+def tail_kernel(*refs):
+    parts, (centres_ref, shape_ref, opacity_ref, colours_ref), total = refs[:-5], refs[-5:-1], refs[-1]
+    lanes = total.shape[1]
+    value = parts[0][...]
+    for part in parts[1:]:
+        value = value + part[...]
+    total[...] = value
+    field = 0
+    for ref in (centres_ref, shape_ref, opacity_ref, colours_ref):
+        for row in range(ref.shape[0]):
+            for k in range(GROUPS):
+                at = field * GROUPS + k
+                ref[row : row + 1, k * lanes : (k + 1) * lanes] = total[at : at + 1, :]
+            field += 1
+
+
 def monomials(pixels):
     side = math.isqrt(pixels)
     index = np.arange(pixels)
@@ -513,7 +545,7 @@
             jax.ShapeDtypeStruct((tiles, slots), jnp.int32),
             jax.ShapeDtypeStruct((views * 8,), F32),
         ],
-        in_specs=[smem] * 3 + [vmem] * 2,
+        in_specs=[smem] * 3 + [vmem] * 3,
         out_specs=[vmem, vmem, smem],
         scratch_shapes=[
             pltpu.VMEM((3, tiles, slots), F32),
@@ -527,19 +559,26 @@
         name="prep",
     )
 
+    kept = tiles_view // 2
+    mirror = tile_group - 1
+    live_row = jnp.pad(live_count[:, None, kept:], ((0, 0), (0, 7), (0, slots - kept)))
+    theirs = jnp.concatenate([intersection_ids[:, kept:], depth_order[:, kept:], live_row], axis=1)
+
     fields = jnp.concatenate([centres, shape_raw, opacity_logit[None], colours], axis=0)
     block = fields.reshape(FIELDS * GROUPS, lanes)
     note = jnp.pad(totals.astype(F32)[None], ((0, 7), (0, lanes - views)))
-    column = jnp.concatenate([block] + [swap(block, "view", m) for m in range(1, view_group)] + [note])
-    mine = jnp.stack([column] + [swap(column, "tile", 2 * m) for m in range(1, chips)])
-    rows, group, cam = prep(
-        me[None],
-        live_count,
-        camera,
-        intersection_ids.reshape(tiles, slots),
-        depth_order.reshape(tiles, slots),
-    )
+    beyond = [swap(block, "view", m) for m in range(1, view_group)]
+    level = [swap(block, "tile", 2 * m) for m in range(1, chips)]
+    theirs = swap(theirs, "tile", mirror)
+    beyond = jnp.concatenate(beyond + [note])
+    beyond, theirs, *level = lax.optimization_barrier((beyond, theirs, *level))
+    far = [swap(beyond, "tile", 2 * m) for m in range(1, chips)]
+    mine = jnp.stack([jnp.concatenate([near, rest]) for near, rest in zip([block] + level, [beyond] + far)])
+    live_now = jnp.concatenate([live_count[:, :kept], theirs[:, 2 * kept, :kept]], axis=1)
+    rows, group, cam = prep(me[None], live_now, camera, intersection_ids, depth_order, theirs)
     mine, rows, group, cam = lax.optimization_barrier((mine, rows.reshape(-1), group, cam))
+    target = target.transpose(0, 2, 1, 3)
+    their_target = swap(target[:, :, kept:], "tile", mirror)
     other = swap(mine, "tile", 1)
 
     table_rows = devices * lanes
@@ -550,12 +589,13 @@
     splat = pl.pallas_call(
         partial(splat_kernel, (views, tiles_view, slots, pixels, lanes, view_group)),
         out_shape=[
-            jax.ShapeDtypeStruct((views, 3, tiles_view, pixels), F32),
+            jax.ShapeDtypeStruct((views, 3, kept, pixels), F32),
+            jax.ShapeDtypeStruct((views, 3, tiles_view - kept, pixels), F32),
             jax.ShapeDtypeStruct(half, F32),
             jax.ShapeDtypeStruct(half, F32),
         ],
-        in_specs=[smem] * 3 + [vmem] * 5,
-        out_specs=[vmem] * 3,
+        in_specs=[smem] * 3 + [vmem] * 6,
+        out_specs=[vmem] * 4,
         scratch_shapes=[
             pltpu.VMEM((table_rows, lanes), F32),
             pltpu.VMEM((BATCH, slots, lanes), F32),
@@ -568,18 +608,20 @@
         ]
         + [pltpu.VMEM(square, BF16)] * 5
         + [pltpu.VMEM((BATCH, 16, slots), F32), pltpu.VMEM((BATCH, 8, pixels), F32)]
+        + [pltpu.VMEM((views, 3, tiles_view, pixels), F32)] * 2
         + [pltpu.VMEM((table_rows, lanes), F32)] * accs,
         compiler_params=pltpu.CompilerParams(vmem_limit_bytes=room),
         name="splat",
     )
-    rendered, grad_mine, grad_other = splat(
+    image, their_image, grad_mine, grad_other = splat(
         cam,
         rows,
-        live_count,
+        live_now,
         group,
         mine,
         other,
-        target.transpose(0, 2, 1, 3),
+        target,
+        their_target,
         monomials(pixels),
     )
 
@@ -594,21 +636,34 @@
                 before = before + jnp.where((tile_index ^ mask) < tile_index, theirs, 0)
     next_owner = (before[:, None] + within) * tile_group // whole[:, None]
 
-    joined = grad_mine + swap(grad_other, "tile", 1)
-    joined = joined.reshape(chips, view_group, FIELDS * GROUPS, lanes)
-    part = joined[0]
-    for m in range(1, chips):
-        part = part + swap(joined[m], "tile", 2 * m)
-    summed = part[0]
-    for m in range(1, view_group):
-        summed = summed + swap(part[m], "view", m)
-    summed = summed.reshape(FIELDS, own_count)
+    grad_other = swap(grad_other, "tile", 1)
+    rendered = jnp.concatenate([image, swap(their_image, "tile", mirror)], axis=2)
+    joined = (grad_mine + grad_other).reshape(chips, view_group, FIELDS * GROUPS, lanes)
+    far = [swap(joined[m, 1:], "tile", 2 * m) for m in range(1, chips)]
+    near = joined[:, 0]
+    near, *far = lax.optimization_barrier((near, *far))
+    beyond = joined[0, 1:]
+    for part in far:
+        beyond = beyond + part
+    parts = [near[0]]
+    parts += [swap(beyond[m - 1], "view", m) for m in range(1, view_group)]
+    parts += [swap(near[m], "tile", 2 * m) for m in range(1, chips)]
+    tail = pl.pallas_call(
+        tail_kernel,
+        out_shape=[jax.ShapeDtypeStruct((count, own_count), F32) for count in (3, 6, 1, 3)],
+        in_specs=[vmem] * len(parts),
+        out_specs=[vmem] * 4,
+        scratch_shapes=[pltpu.VMEM((FIELDS * GROUPS, lanes), F32)],
+        compiler_params=pltpu.CompilerParams(vmem_limit_bytes=8 * 1024 * 1024),
+        name="tail",
+    )
+    grad_centres, grad_shape, grad_opacity, grad_colours = tail(*parts)
     return (
         rendered.transpose(0, 2, 1, 3),
-        summed[0:3],
-        summed[3:9],
-        summed[9],
-        summed[10:13],
+        grad_centres,
+        grad_shape,
+        grad_opacity[0],
+        grad_colours,
         next_owner,
     )
 

time: 90.6 us -> 93.5 us (1.032)
  waiting for transfers between devices: 23.1 us -> 18 us
  Pallas kernels: 31.5 us -> 35.6 us
  starting transfers between devices: 27.3 us -> 30.1 us
  other arithmetic: 3.33 us -> 4.67 us
  local copies, waits for them, and re-layouts: 4.74 us -> 3.76 us
    ppermute x14 -> x23, waiting for transfers between devices: 23.1 us -> 18 us  [swap(): return lax.ppermute(array, axis, [(i, i ^ mask) for i in range(size)])]
    pallas_call x2 -> x3, Pallas kernels: 31.5 us -> 35.6 us  [the longest x1 29.6 us: shards(): splat(cam, rows, live_now, group, mine, other, target, their_target, mono...]
    ppermute x14 -> x23, starting transfers between devices: 27.3 us -> 30.1 us  [swap(): return lax.ppermute(array, axis, [(i, i ^ mask) for i in range(size)])]
    slice x6 -> x7, local copies, waits for them, and re-layouts: 1.9 us -> 0.8 us  [the longest x2 0.7 us: shards(): intersection_ids[:, kept:]]
  transfers between devices with their start and end apart: 14 -> 23, of which waited for: 9 -> 8; matrix products, arithmetic and copies ran while one was open for 3% -> 5% of each run, Pallas kernels for 6% -> 6%
where the time goes in v2:
time: 93.5 us; the launch traced here: 93.1 us
  Pallas kernels  35.6 us (38%)
  starting transfers between devices  30.1 us (32%)
  waiting for transfers between devices  18 us (19%)
  other arithmetic  4.67 us (5%)
  local copies, waits for them, and re-layouts  3.76 us (4%)
    ppermute x23, starting transfers between devices, swap(): return lax.ppermute(array, axis, [(i, i ^ mask) for i in range(size)])  30.1 us
    pallas_call x1, Pallas kernels, shards(): splat(cam, rows, live_now, group, mine, other, target, their_target, mono...  29.6 us
    ppermute x23, waiting for transfers between devices, swap(): return lax.ppermute(array, axis, [(i, i ^ mask) for i in range(size)])  18 us
    pallas_call x1, Pallas kernels, shards(): prep(me[None], live_now, camera, intersection_ids, depth_order, theirs)  5.34 us
    unnamed x20, local copies, waits for them, and re-layouts  2.87 us
  transfers between devices with their start and end apart: 23, of which 8 were waited for; matrix products, arithmetic and copies ran while one was open for 5% of the time, Pallas kernels for 6%

profile of v2, /device:TPU:0, one launch (start us, length us, event | category | flops | bytes accessed | tf_op | source)
XLA Modules:
  0.0 93.1 jit_solution(11280493775144565760)
XLA Ops:
  0.6 0.8 pad_maximum_fusion.1
  1.5 3.1 %collective-permute-start = (f32[104,128]{1,0:T(8,128)S(1)}, f32[104,128]{1,0:T(8,128)S(1)}, u32[]{:S(2)}, u32[]{:S(2)}) collective-permute-start(f32[104,128]{1,0:T(8,128)S(1)} %reshape.139), channel_id=1, source_target_pairs={{0,8},{8,0},{16,24},{24,16},{1,9},{9,1},{17,25},{25,17},{2,10},{10... | collective-permute-start | bytes 159752 | tf_op jit(solution)/shard_map/ppermute | solution.py:516
  4.6 2.6 %collective-permute-start.1 = (f32[104,128]{1,0:T(8,128)S(1)}, f32[104,128]{1,0:T(8,128)S(1)}, u32[]{:S(2)}, u32[]{:S(2)}) collective-permute-start(f32[104,128]{1,0:T(8,128)S(1)} %reshape.139), channel_id=1, source_target_pairs={{0,16},{8,24},{16,0},{24,8},{1,17},{9,25},{17,1},{25,9},{2,18},{10... | collective-permute-start | bytes 159752 | tf_op jit(solution)/shard_map/ppermute | solution.py:516
  7.2 1.7 %collective-permute-start.4 = (f32[104,128]{1,0:T(8,128)S(1)}, f32[104,128]{1,0:T(8,128)S(1)}, u32[]{:S(2)}, u32[]{:S(2)}) collective-permute-start(f32[104,128]{1,0:T(8,128)S(1)} %reshape.139), channel_id=1, source_target_pairs={{0,2},{1,3},{2,0},{3,1},{4,6},{5,7},{6,4},{7,5},{8,10},{9,11},{10,... | collective-permute-start | bytes 159752 | tf_op jit(solution)/shard_map/ppermute | solution.py:516
  8.9 1.5 %collective-permute-start.5 = (f32[104,128]{1,0:T(8,128)S(1)}, f32[104,128]{1,0:T(8,128)S(1)}, u32[]{:S(2)}, u32[]{:S(2)}) collective-permute-start(f32[104,128]{1,0:T(8,128)S(1)} %reshape.139), channel_id=1, source_target_pairs={{0,4},{1,5},{2,6},{3,7},{4,0},{5,1},{6,2},{7,3},{8,12},{9,13},{10,... | collective-permute-start | bytes 159752 | tf_op jit(solution)/shard_map/ppermute | solution.py:516
  10.4 0.1 fusion.19
  10.5 0.1 reduce_sum.9
  10.6 0.7 slice-done
  11.3 0.0 slice-done.1
  11.4 0.7 copy-done.7
  12.1 0.7 copy.22.camera_ref
  12.7 0.3 collective-permute-start.6
  13.0 0.5 collective-permute-start.3
  13.5 4.1 %collective-permute-done.3.theirs_ref = s32[2,24,256]{2,1,0:T(8,128)S(1)} collective-permute-done((s32[2,24,256]{2,1,0:T(8,128)S(1)}, s32[2,24,256]{2,1,0:T(8,128)S(1)}, u32[]{:S(2)}, u32[]{:S(2)}) %collective-permute-start.3) | collective-permute-done | bytes 49184 | tf_op jit(solution)/shard_map/ppermute | solution.py:516
  17.6 0.3 collective-permute-done.6
  18.0 1.5 %collective-permute-start.7 = (f32[320,128]{1,0:T(8,128)S(1)}, f32[320,128]{1,0:T(8,128)S(1)}, u32[]{:S(2)}, u32[]{:S(2)}) collective-permute-start(f32[320,128]{1,0:T(8,128)S(1)} %select_maximum_fusion), channel_id=1, source_target_pairs={{0,2},{1,3},{2,0},{3,1},{4,6},{5,7},{6,4},{7,5},{8,10},{9,11},{10,... | collective-permute-start | bytes 491528 | tf_op jit(solution)/shard_map/ppermute | solution.py:516
  19.5 1.3 %collective-permute-start.8 = (f32[320,128]{1,0:T(8,128)S(1)}, f32[320,128]{1,0:T(8,128)S(1)}, u32[]{:S(2)}, u32[]{:S(2)}) collective-permute-start(f32[320,128]{1,0:T(8,128)S(1)} %select_maximum_fusion), channel_id=1, source_target_pairs={{0,4},{1,5},{2,6},{3,7},{4,0},{5,1},{6,2},{7,3},{8,12},{9,13},{10,... | collective-permute-start | bytes 491528 | tf_op jit(solution)/shard_map/ppermute | solution.py:516
  20.7 0.7 collective-permute-start.9
  21.5 0.6 pad_add_fusion.1.live_ref
  22.1 5.3 %prep.1 = (s32[40,256]{1,0:T(8,128)}, s32[32,256]{1,0:T(8,128)}, f32[16]{0:T(128)}) custom-call(s32[1]{0:T(128)} %bitcast.8.me_ref, s32[2,16]{1,0:T(2,128)} %pad_add_fusion.1.live_ref, f32[8,2,4]{2,1,0:T(2,128)} %copy.22.camera_ref, s32[2,16,256]{2,1,0:T(8,128)} %ids_ref.1, s32[2,16,256]{2,1,0:T(8,128)} %order_ref.1, s32[2,24,256]{2,1,0:T(8,128)} %copy-done.8), custom_call_target="tpu_custom_call" | custom-call | flops 8000000000 | bytes 131072 | tf_op jit(solution)/shard_map/prep/pallas_call | solution.py:578
  27.5 0.7 copy-done.5
  28.3 0.3 collective-permute-done.8
  28.7 0.1 pad_maximum_fusion.mine_ref
  28.8 0.1 collective-permute-start.10
  28.8 0.7 copy-done
  29.6 1.4 %collective-permute-start.11 = (f32[2,3,8,256]{3,2,1,0:T(8,128)S(1)}, f32[2,3,8,256]{3,2,1,0:T(8,128)S(1)}, u32[]{:S(2)}, u32[]{:S(2)}) collective-permute-start(f32[2,3,8,256]{3,2,1,0:T(8,128)S(1)} %slice.100), channel_id=1, source_target_pairs={{0,7},{1,6},{2,5},{3,4},{4,3},{5,2},{6,1},{7,0},{8,15},{9,14},{10,... | collective-permute-start | bytes 147464 | tf_op jit(solution)/shard_map/ppermute | solution.py:516
  31.0 3.6 %collective-permute-done.11.their_target_ref = f32[2,3,8,256]{3,2,1,0:T(8,128)S(1)} collective-permute-done((f32[2,3,8,256]{3,2,1,0:T(8,128)S(1)}, f32[2,3,8,256]{3,2,1,0:T(8,128)S(1)}, u32[]{:S(2)}, u32[]{:S(2)}) %collective-permute-start.11) | collective-permute-done | bytes 49184 | tf_op jit(solution)/shard_map/ppermute | solution.py:516
  34.6 29.6 %splat.1 = (f32[2,3,8,256]{3,2,1,0:T(8,128)S(1)}, f32[2,3,8,256]{3,2,1,0:T(8,128)S(1)}, f32[16,104,128]{2,1,0:T(8,128)S(1)}, f32[16,104,128]{2,1,0:T(8,128)S(1)}) custom-call(f32[16]{0:T(128)S(1)} %copy-done.4, s32[10240]{0:T(1024)S(1)} %bitcast.115, s32[2,16]{1,0:T(2,128)S(1)} %copy-done.3, s32[32,256]{1,0:T(8,128)S(1)} %copy-done.1, ...), custom_call_target="tpu_custom_call" | custom-call | tf_op jit(solution)/shard_map/splat/pallas_call | solution.py:616
  64.2 0.1 collective-permute-start.13
  64.3 0.2 reduce_window_sum.11
  64.5 3.9 %collective-permute-start.12 = (f32[2,3,8,256]{3,2,1,0:T(8,128)S(1)}, f32[2,3,8,256]{3,2,1,0:T(8,128)S(1)}, u32[]{:S(2)}, u32[]{:S(2)}) collective-permute-start(f32[2,3,8,256]{3,2,1,0:T(8,128)S(1)} %get-tuple-element.43), channel_id=1, source_target_pairs={{0,7},{1,6},{2,5},{3,4},{4,3},{5,2},{6,1},{7,0},{8,15},{9,14},{10,... | collective-permute-start | bytes 147464 | tf_op jit(solution)/shard_map/ppermute | solution.py:516
  68.4 0.8 and_select_fusion
  69.1 1.2 %add.141 = f32[16,104,128]{2,1,0:T(8,128)S(1)} add(f32[16,104,128]{2,1,0:T(8,128)S(1)} %get-tuple-element.44, f32[16,104,128]{2,1,0:T(8,128)} %collective-permute-done.13) | non-fusion elementwise | flops 212992 | bytes 2555904 | tf_op jit(solution)/shard_map/add | solution.py:641
  70.4 1.0 %collective-permute-start.14 = (f32[3,104,128]{2,1,0:T(8,128)S(1)}, f32[3,104,128]{2,1,0:T(8,128)S(1)}, u32[]{:S(2)}, u32[]{:S(2)}) collective-permute-start(f32[3,104,128]{2,1,0:T(8,128)S(1)} %get-tuple-element.58), channel_id=1, source_target_pairs={{0,2},{1,3},{2,0},{3,1},{4,6},{5,7},{6,4},{7,5},{8,10},{9,11},{10,... | collective-permute-start | bytes 479240 | tf_op jit(solution)/shard_map/ppermute | solution.py:516
  71.5 1.1 %collective-permute-start.15 = (f32[3,104,128]{2,1,0:T(8,128)S(1)}, f32[3,104,128]{2,1,0:T(8,128)S(1)}, u32[]{:S(2)}, u32[]{:S(2)}) collective-permute-start(f32[3,104,128]{2,1,0:T(8,128)S(1)} %get-tuple-element.57), channel_id=1, source_target_pairs={{0,4},{1,5},{2,6},{3,7},{4,0},{5,1},{6,2},{7,3},{8,12},{9,13},{10,... | collective-permute-start | bytes 479240 | tf_op jit(solution)/shard_map/ppermute | solution.py:516
  72.6 1.4 %collective-permute-start.16 = (f32[3,104,128]{2,1,0:T(8,128)S(1)}, f32[3,104,128]{2,1,0:T(8,128)S(1)}, u32[]{:S(2)}, u32[]{:S(2)}) collective-permute-start(f32[3,104,128]{2,1,0:T(8,128)S(1)} %get-tuple-element.56), channel_id=1, source_target_pairs={{0,6},{1,7},{2,4},{3,5},{4,2},{5,3},{6,0},{7,1},{8,14},{9,15},{10,... | collective-permute-start | bytes 479240 | tf_op jit(solution)/shard_map/ppermute | solution.py:516
  74.0 3.5 %collective-permute-done.14 = f32[3,104,128]{2,1,0:T(8,128)S(1)} collective-permute-done((f32[3,104,128]{2,1,0:T(8,128)S(1)}, f32[3,104,128]{2,1,0:T(8,128)S(1)}, u32[]{:S(2)}, u32[]{:S(2)}) %collective-permute-start.14) | collective-permute-done | bytes 159776 | tf_op jit(solution)/shard_map/ppermute | solution.py:516
  77.5 3.2 %collective-permute-done.15 = f32[3,104,128]{2,1,0:T(8,128)S(1)} collective-permute-done((f32[3,104,128]{2,1,0:T(8,128)S(1)}, f32[3,104,128]{2,1,0:T(8,128)S(1)}, u32[]{:S(2)}, u32[]{:S(2)}) %collective-permute-start.15) | collective-permute-done | bytes 159776 | tf_op jit(solution)/shard_map/ppermute | solution.py:516
  80.7 0.6 collective-permute-start.17
  81.3 3.8 %collective-permute-start.18 = (f32[104,128]{1,0:T(8,128)S(1)}, f32[104,128]{1,0:T(8,128)S(1)}, u32[]{:S(2)}, u32[]{:S(2)}) collective-permute-start(f32[104,128]{1,0:T(8,128)S(1)} %get-tuple-element.64), channel_id=1, source_target_pairs={{0,16},{8,24},{16,0},{24,8},{1,17},{9,25},{17,1},{25,9},{2,18},{10... | collective-permute-start | bytes 159752 | tf_op jit(solution)/shard_map/ppermute | solution.py:516
  85.1 0.0 collective-permute-start.19
  85.2 1.6 %collective-permute-start.20 = (f32[104,128]{1,0:T(8,128)S(1)}, f32[104,128]{1,0:T(8,128)S(1)}, u32[]{:S(2)}, u32[]{:S(2)}) collective-permute-start(f32[104,128]{1,0:T(8,128)S(1)} %get-tuple-element.61), channel_id=1, source_target_pairs={{0,2},{1,3},{2,0},{3,1},{4,6},{5,7},{6,4},{7,5},{8,10},{9,11},{10,... | collective-permute-start | bytes 159752 | tf_op jit(solution)/shard_map/ppermute | solution.py:516
  86.8 0.6 collective-permute-start.21
  87.4 1.4 %collective-permute-start.22 = (f32[104,128]{1,0:T(8,128)S(1)}, f32[104,128]{1,0:T(8,128)S(1)}, u32[]{:S(2)}, u32[]{:S(2)}) collective-permute-start(f32[104,128]{1,0:T(8,128)S(1)} %get-tuple-element.59), channel_id=1, source_target_pairs={{0,6},{1,7},{2,4},{3,5},{4,2},{5,3},{6,0},{7,1},{8,14},{9,15},{10,... | collective-permute-start | bytes 159752 | tf_op jit(solution)/shard_map/ppermute | solution.py:516
  88.7 0.6 maximum_bitcast_fusion.4
  89.4 1.7 %collective-permute-done.19.refs_3_ = f32[104,128]{1,0:T(8,128)S(1)} collective-permute-done((f32[104,128]{1,0:T(8,128)S(1)}, f32[104,128]{1,0:T(8,128)S(1)}, u32[]{:S(2)}, u32[]{:S(2)}) %collective-permute-start.19) | collective-permute-done | bytes 53280 | tf_op jit(solution)/shard_map/ppermute | solution.py:516
  91.1 1.3 %collective-permute-done.22.refs_6_ = f32[104,128]{1,0:T(8,128)S(1)} collective-permute-done((f32[104,128]{1,0:T(8,128)S(1)}, f32[104,128]{1,0:T(8,128)S(1)}, u32[]{:S(2)}, u32[]{:S(2)}) %collective-permute-start.22) | collective-permute-done | bytes 53280 | tf_op jit(solution)/shard_map/ppermute | solution.py:516
  92.4 0.7 tail.1
  (51 shorter events, 0.4 us)
Async XLA Ops:
  1.5 9.0 %copy-start.6 = (s32[2,16]{1,0:T(2,128)S(1)}, s32[2,16]{1,0:T(2,128)}, u32[]{:S(2)}) copy-start(s32[2,16]{1,0:T(2,128)} %param.18) | copy-start | bytes 388
  1.5 11.3 %collective-permute-start = (f32[104,128]{1,0:T(8,128)S(1)}, f32[104,128]{1,0:T(8,128)S(1)}, u32[]{:S(2)}, u32[]{:S(2)}) collective-permute-start(f32[104,128]{1,0:T(8,128)S(1)} %reshape.139), channel_id=1, source_target_pairs={{0,8},{8,0},{16,24},{24,16},{1,9},{9,1},{17,25},{25,17},{2,10},{10... | collective-permute-start | bytes 159752 | tf_op jit(solution)/shard_map/ppermute | solution.py:516
  4.6 8.4 %collective-permute-start.1 = (f32[104,128]{1,0:T(8,128)S(1)}, f32[104,128]{1,0:T(8,128)S(1)}, u32[]{:S(2)}, u32[]{:S(2)}) collective-permute-start(f32[104,128]{1,0:T(8,128)S(1)} %reshape.139), channel_id=1, source_target_pairs={{0,16},{8,24},{16,0},{24,8},{1,17},{9,25},{17,1},{25,9},{2,18},{10... | collective-permute-start | bytes 159752 | tf_op jit(solution)/shard_map/ppermute | solution.py:516
  7.2 6.3 %collective-permute-start.2 = (f32[104,128]{1,0:T(8,128)S(1)}, f32[104,128]{1,0:T(8,128)S(1)}, u32[]{:S(2)}, u32[]{:S(2)}) collective-permute-start(f32[104,128]{1,0:T(8,128)S(1)} %reshape.139), channel_id=1, source_target_pairs={{0,24},{8,16},{16,8},{24,0},{1,25},{9,17},{17,9},{25,1},{2,26},{10... | collective-permute-start | bytes 159752 | tf_op jit(solution)/shard_map/ppermute | solution.py:516
  7.2 10.4 %collective-permute-start.4 = (f32[104,128]{1,0:T(8,128)S(1)}, f32[104,128]{1,0:T(8,128)S(1)}, u32[]{:S(2)}, u32[]{:S(2)}) collective-permute-start(f32[104,128]{1,0:T(8,128)S(1)} %reshape.139), channel_id=1, source_target_pairs={{0,2},{1,3},{2,0},{3,1},{4,6},{5,7},{6,4},{7,5},{8,10},{9,11},{10,... | collective-permute-start | bytes 159752 | tf_op jit(solution)/shard_map/ppermute | solution.py:516
  8.9 8.7 %collective-permute-start.5 = (f32[104,128]{1,0:T(8,128)S(1)}, f32[104,128]{1,0:T(8,128)S(1)}, u32[]{:S(2)}, u32[]{:S(2)}) collective-permute-start(f32[104,128]{1,0:T(8,128)S(1)} %reshape.139), channel_id=1, source_target_pairs={{0,4},{1,5},{2,6},{3,7},{4,0},{5,1},{6,2},{7,3},{8,12},{9,13},{10,... | collective-permute-start | bytes 159752 | tf_op jit(solution)/shard_map/ppermute | solution.py:516
  10.6 0.7 slice-start
  10.6 0.7 slice-start.1
  11.4 0.7 copy-start.7
  12.7 5.2 %collective-permute-start.6 = (f32[104,128]{1,0:T(8,128)S(1)}, f32[104,128]{1,0:T(8,128)S(1)}, u32[]{:S(2)}, u32[]{:S(2)}) collective-permute-start(f32[104,128]{1,0:T(8,128)S(1)} %reshape.139), channel_id=1, source_target_pairs={{0,6},{1,7},{2,4},{3,5},{4,2},{5,3},{6,0},{7,1},{8,14},{9,15},{10,... | collective-permute-start | bytes 159752 | tf_op jit(solution)/shard_map/ppermute | solution.py:516
  13.0 4.6 %collective-permute-start.3 = (s32[2,24,256]{2,1,0:T(8,128)S(1)}, s32[2,24,256]{2,1,0:T(8,128)S(1)}, u32[]{:S(2)}, u32[]{:S(2)}) collective-permute-start(s32[2,24,256]{2,1,0:T(8,128)S(1)} %pad_add_fusion), channel_id=1, source_target_pairs={{0,7},{1,6},{2,5},{3,4},{4,3},{5,2},{6,1},{7,0},{8,15},{9,14},{10,... | collective-permute-start | bytes 147464 | tf_op jit(solution)/shard_map/ppermute | solution.py:516
  17.6 4.5 %copy-start.8 = (s32[2,24,256]{2,1,0:T(8,128)}, s32[2,24,256]{2,1,0:T(8,128)S(1)}, u32[]{:S(2)}) copy-start(s32[2,24,256]{2,1,0:T(8,128)S(1)} %collective-permute-done.3.theirs_ref) | copy-start | bytes 147460
  18.0 10.3 %collective-permute-start.7 = (f32[320,128]{1,0:T(8,128)S(1)}, f32[320,128]{1,0:T(8,128)S(1)}, u32[]{:S(2)}, u32[]{:S(2)}) collective-permute-start(f32[320,128]{1,0:T(8,128)S(1)} %select_maximum_fusion), channel_id=1, source_target_pairs={{0,2},{1,3},{2,0},{3,1},{4,6},{5,7},{6,4},{7,5},{8,10},{9,11},{10,... | collective-permute-start | bytes 491528 | tf_op jit(solution)/shard_map/ppermute | solution.py:516
  19.5 9.2 %collective-permute-start.8 = (f32[320,128]{1,0:T(8,128)S(1)}, f32[320,128]{1,0:T(8,128)S(1)}, u32[]{:S(2)}, u32[]{:S(2)}) collective-permute-start(f32[320,128]{1,0:T(8,128)S(1)} %select_maximum_fusion), channel_id=1, source_target_pairs={{0,4},{1,5},{2,6},{3,7},{4,0},{5,1},{6,2},{7,3},{8,12},{9,13},{10,... | collective-permute-start | bytes 491528 | tf_op jit(solution)/shard_map/ppermute | solution.py:516
  20.7 7.9 %collective-permute-start.9 = (f32[320,128]{1,0:T(8,128)S(1)}, f32[320,128]{1,0:T(8,128)S(1)}, u32[]{:S(2)}, u32[]{:S(2)}) collective-permute-start(f32[320,128]{1,0:T(8,128)S(1)} %select_maximum_fusion), channel_id=1, source_target_pairs={{0,6},{1,7},{2,4},{3,5},{4,2},{5,3},{6,0},{7,1},{8,14},{9,15},{10,... | collective-permute-start | bytes 491528 | tf_op jit(solution)/shard_map/ppermute | solution.py:516
  27.5 0.8 copy-start.5
  28.7 0.9 copy-start
  28.8 5.8 %collective-permute-start.10 = (f32[4,424,128]{2,1,0:T(8,128)S(1)}, f32[4,424,128]{2,1,0:T(8,128)S(1)}, u32[]{:S(2)}, u32[]{:S(2)}) collective-permute-start(f32[4,424,128]{2,1,0:T(8,128)S(1)} %pad_maximum_fusion.mine_ref), channel_id=1, source_target_pairs={{0,1},{1,0},{2,3},{3,2},{4,5},{5,4},{6,7},{7,6},{8,9},{9,8},{10,11... | collective-permute-start | bytes 2605064 | tf_op jit(solution)/shard_map/ppermute | solution.py:516
  29.6 5.0 %copy-start.1 = (s32[32,256]{1,0:T(8,128)S(1)}, s32[32,256]{1,0:T(8,128)}, u32[]{:S(2)}) copy-start(s32[32,256]{1,0:T(8,128)} %get-tuple-element.40.group_ref) | copy-start | bytes 98308
  29.6 5.0 %copy-start.2 = (bf16[32,256]{1,0:T(8,128)(2,1)S(1)}, bf16[32,256]{1,0:T(8,128)(2,1)}, u32[]{:S(2)}) copy-start(bf16[32,256]{1,0:T(8,128)(2,1)} %constant.40.clone.mono_ref) | copy-start | bytes 49156
  29.6 5.0 %copy-start.3 = (s32[2,16]{1,0:T(2,128)S(1)}, s32[2,16]{1,0:T(2,128)}, u32[]{:S(2)}) copy-start(s32[2,16]{1,0:T(2,128)} %pad_add_fusion.1.live_ref) | copy-start | bytes 388
  29.6 5.0 %copy-start.4 = (f32[16]{0:T(128)S(1)}, f32[16]{0:T(128)}, u32[]{:S(2)}) copy-start(f32[16]{0:T(128)} %get-tuple-element.38.cam_ref) | copy-start | bytes 196
  29.6 5.0 %collective-permute-start.11 = (f32[2,3,8,256]{3,2,1,0:T(8,128)S(1)}, f32[2,3,8,256]{3,2,1,0:T(8,128)S(1)}, u32[]{:S(2)}, u32[]{:S(2)}) collective-permute-start(f32[2,3,8,256]{3,2,1,0:T(8,128)S(1)} %slice.100), channel_id=1, source_target_pairs={{0,7},{1,6},{2,5},{3,4},{4,3},{5,2},{6,1},{7,0},{8,15},{9,14},{10,... | collective-permute-start | bytes 147464 | tf_op jit(solution)/shard_map/ppermute | solution.py:516
  64.2 4.9 %collective-permute-start.13 = (f32[16,104,128]{2,1,0:T(8,128)S(1)}, f32[16,104,128]{2,1,0:T(8,128)}, u32[]{:S(2)}, u32[]{:S(2)}) collective-permute-start(f32[16,104,128]{2,1,0:T(8,128)S(1)} %get-tuple-element.45), channel_id=1, source_target_pairs={{0,1},{1,0},{2,3},{3,2},{4,5},{5,4},{6,7},{7,6},{8,9},{9,8},{10,11... | collective-permute-start | bytes 2555912 | tf_op jit(solution)/shard_map/ppermute | solution.py:516
  64.5 22.3 %collective-permute-start.12 = (f32[2,3,8,256]{3,2,1,0:T(8,128)S(1)}, f32[2,3,8,256]{3,2,1,0:T(8,128)S(1)}, u32[]{:S(2)}, u32[]{:S(2)}) collective-permute-start(f32[2,3,8,256]{3,2,1,0:T(8,128)S(1)} %get-tuple-element.43), channel_id=1, source_target_pairs={{0,7},{1,6},{2,5},{3,4},{4,3},{5,2},{6,1},{7,0},{8,15},{9,14},{10,... | collective-permute-start | bytes 147464 | tf_op jit(solution)/shard_map/ppermute | solution.py:516
  70.4 7.0 %collective-permute-start.14 = (f32[3,104,128]{2,1,0:T(8,128)S(1)}, f32[3,104,128]{2,1,0:T(8,128)S(1)}, u32[]{:S(2)}, u32[]{:S(2)}) collective-permute-start(f32[3,104,128]{2,1,0:T(8,128)S(1)} %get-tuple-element.58), channel_id=1, source_target_pairs={{0,2},{1,3},{2,0},{3,1},{4,6},{5,7},{6,4},{7,5},{8,10},{9,11},{10,... | collective-permute-start | bytes 479240 | tf_op jit(solution)/shard_map/ppermute | solution.py:516
  71.5 9.2 %collective-permute-start.15 = (f32[3,104,128]{2,1,0:T(8,128)S(1)}, f32[3,104,128]{2,1,0:T(8,128)S(1)}, u32[]{:S(2)}, u32[]{:S(2)}) collective-permute-start(f32[3,104,128]{2,1,0:T(8,128)S(1)} %get-tuple-element.57), channel_id=1, source_target_pairs={{0,4},{1,5},{2,6},{3,7},{4,0},{5,1},{6,2},{7,3},{8,12},{9,13},{10,... | collective-permute-start | bytes 479240 | tf_op jit(solution)/shard_map/ppermute | solution.py:516
  72.6 8.1 %collective-permute-start.16 = (f32[3,104,128]{2,1,0:T(8,128)S(1)}, f32[3,104,128]{2,1,0:T(8,128)S(1)}, u32[]{:S(2)}, u32[]{:S(2)}) collective-permute-start(f32[3,104,128]{2,1,0:T(8,128)S(1)} %get-tuple-element.56), channel_id=1, source_target_pairs={{0,6},{1,7},{2,4},{3,5},{4,2},{5,3},{6,0},{7,1},{8,14},{9,15},{10,... | collective-permute-start | bytes 479240 | tf_op jit(solution)/shard_map/ppermute | solution.py:516
  80.7 6.6 %collective-permute-start.17 = (f32[104,128]{1,0:T(8,128)S(1)}, f32[104,128]{1,0:T(8,128)S(1)}, u32[]{:S(2)}, u32[]{:S(2)}) collective-permute-start(f32[104,128]{1,0:T(8,128)S(1)} %get-tuple-element.65), channel_id=1, source_target_pairs={{0,8},{8,0},{16,24},{24,16},{1,9},{9,1},{17,25},{25,17},{2,10},{10... | collective-permute-start | bytes 159752 | tf_op jit(solution)/shard_map/ppermute | solution.py:516
  81.3 8.1 %collective-permute-start.18 = (f32[104,128]{1,0:T(8,128)S(1)}, f32[104,128]{1,0:T(8,128)S(1)}, u32[]{:S(2)}, u32[]{:S(2)}) collective-permute-start(f32[104,128]{1,0:T(8,128)S(1)} %get-tuple-element.64), channel_id=1, source_target_pairs={{0,16},{8,24},{16,0},{24,8},{1,17},{9,25},{17,1},{25,9},{2,18},{10... | collective-permute-start | bytes 159752 | tf_op jit(solution)/shard_map/ppermute | solution.py:516
  85.1 5.9 %collective-permute-start.19 = (f32[104,128]{1,0:T(8,128)S(1)}, f32[104,128]{1,0:T(8,128)S(1)}, u32[]{:S(2)}, u32[]{:S(2)}) collective-permute-start(f32[104,128]{1,0:T(8,128)S(1)} %get-tuple-element.63), channel_id=1, source_target_pairs={{0,24},{8,16},{16,8},{24,0},{1,25},{9,17},{17,9},{25,1},{2,26},{10... | collective-permute-start | bytes 159752 | tf_op jit(solution)/shard_map/ppermute | solution.py:516
  85.2 5.9 %collective-permute-start.20 = (f32[104,128]{1,0:T(8,128)S(1)}, f32[104,128]{1,0:T(8,128)S(1)}, u32[]{:S(2)}, u32[]{:S(2)}) collective-permute-start(f32[104,128]{1,0:T(8,128)S(1)} %get-tuple-element.61), channel_id=1, source_target_pairs={{0,2},{1,3},{2,0},{3,1},{4,6},{5,7},{6,4},{7,5},{8,10},{9,11},{10,... | collective-permute-start | bytes 159752 | tf_op jit(solution)/shard_map/ppermute | solution.py:516
  86.8 4.3 %collective-permute-start.21 = (f32[104,128]{1,0:T(8,128)S(1)}, f32[104,128]{1,0:T(8,128)S(1)}, u32[]{:S(2)}, u32[]{:S(2)}) collective-permute-start(f32[104,128]{1,0:T(8,128)S(1)} %get-tuple-element.60), channel_id=1, source_target_pairs={{0,4},{1,5},{2,6},{3,7},{4,0},{5,1},{6,2},{7,3},{8,12},{9,13},{10,... | collective-permute-start | bytes 159752 | tf_op jit(solution)/shard_map/ppermute | solution.py:516
  87.4 5.0 %collective-permute-start.22 = (f32[104,128]{1,0:T(8,128)S(1)}, f32[104,128]{1,0:T(8,128)S(1)}, u32[]{:S(2)}, u32[]{:S(2)}) collective-permute-start(f32[104,128]{1,0:T(8,128)S(1)} %get-tuple-element.59), channel_id=1, source_target_pairs={{0,6},{1,7},{2,4},{3,5},{4,2},{5,3},{6,0},{7,1},{8,14},{9,15},{10,... | collective-permute-start | bytes 159752 | tf_op jit(solution)/shard_map/ppermute | solution.py:516

commit v3 on v2

--- a/solution.py
+++ b/solution.py
@@ -70,41 +70,13 @@
     lax.fori_loop(many * step, count, single, 0)
 
 
-def prep_kernel(
-    dims,
-    me_ref,
-    live_ref,
-    camera_ref,
-    ids_ref,
-    order_ref,
-    theirs_ref,
-    row_ref,
-    group_ref,
-    cam_ref,
-    piece_ref,
-    rho_ref,
-    code_ref,
-    lhs_ref,
-    live_full,
-    order_b,
-):
-    own_bits, lane_bits, view_bits, tile_bits, tiles_view = dims
-    views, _, slots = ids_ref.shape
-    tiles = views * tiles_view
-    kept = tiles_view // 2
-    me = me_ref[0]
-    first = (me >> tile_bits) * views
-    for v in range(views):
-        for i in range(2):
-            for j in range(4):
-                cam_ref[v * 8 + i * 4 + j] = camera_ref[first + v, i, j]
+def place_slots(dims, me, live_at, ids, order, scratch):
+    own_bits, lane_bits, view_bits, tile_bits = dims
+    piece_ref, rho_ref, code_ref, lhs_ref, live_full, order_b = scratch
+    tiles, slots = ids.shape
     for t in range(tiles):
-        live_full[t : t + 1, :] = jnp.full((1, slots), live_ref[t // tiles_view, t % tiles_view], jnp.int32)
+        live_full[t : t + 1, :] = jnp.full((1, slots), live_at(t), jnp.int32)
     live = live_full[...]
-    parts = []
-    for v in range(views):
-        parts += [order_ref[v, 0:kept, :], theirs_ref[v, kept : 2 * kept, :]]
-    order = jnp.concatenate(parts, axis=0)
     active = order < live
     upper = (
         lax.broadcasted_iota(jnp.int32, (slots, slots), 0)
@@ -117,10 +89,6 @@
         chunk = chunk + (place >= m * rows).astype(jnp.int32)
     rho_ref[...] = jnp.where(active, (place - chunk * rows) * GROUPS + chunk, -1).astype(F32)
     order_b[...] = order.astype(F32)
-    parts = []
-    for v in range(views):
-        parts += [ids_ref[v, 0:kept, :], theirs_ref[v, 0:kept, :]]
-    ids = jnp.concatenate(parts, axis=0)
     owner = (ids >> own_bits) ^ me
     local = ids & ((1 << own_bits) - 1)
     xy_bits = tile_bits - 1
@@ -152,20 +120,45 @@
 
     lax.fori_loop(0, tiles // UNROLL, some_tiles, 0)
     codes = code_ref[...].astype(jnp.int32)
-    row_ref[0:tiles, :] = codes >> 3
-    lane = lax.broadcasted_iota(jnp.int32, (tiles, slots), 1)
-    above = lax.broadcasted_iota(jnp.int32, (tiles, slots), 0)
-    across = jnp.full((tiles, slots), -1, jnp.int32)
-    for t in range(tiles):
-        across = jnp.where(lane == t, live_ref[t // tiles_view, t % tiles_view], across)
-    ahead = (across > live) | ((across == live) & (lane < above))
+    pos = lax.broadcasted_iota(jnp.int32, (tiles, slots), 1)
+    here = (pos >> 3 < rows) & ((pos & 7) * rows + (pos >> 3) < live)
+    return codes >> 3, jnp.where(here, codes & 7, GROUPS)
+
+
+def prep_own_kernel(dims, me_ref, live_ref, camera_ref, ids_ref, order_ref, row_ref, group_ref, cam_ref, *scratch):
+    views, tiles_view, _ = ids_ref.shape
+    kept = tiles_view // 2
+    me = me_ref[0]
+    first = (me >> dims[3]) * views
+    for v in range(views):
+        for i in range(2):
+            for j in range(4):
+                cam_ref[v * 8 + i * 4 + j] = camera_ref[first + v, i, j]
+    ids = jnp.concatenate([ids_ref[v, 0:kept, :] for v in range(views)], axis=0)
+    order = jnp.concatenate([order_ref[v, 0:kept, :] for v in range(views)], axis=0)
+    live_at = lambda t: live_ref[t // kept, t % kept]
+    row_ref[...], group_ref[...] = place_slots(dims, me, live_at, ids, order, scratch)
+
+
+def prep_their_kernel(dims, me_ref, live_ref, message_ref, row_ref, group_ref, *scratch):
+    tiles, slots = group_ref.shape
+    total = live_ref.shape[0]
+    ids = message_ref[0:tiles, :].astype(jnp.int32)
+    order = message_ref[tiles : 2 * tiles, :].astype(jnp.int32)
+    live_at = lambda t: live_ref[total - tiles + t]
+    row_ref[0:tiles, :], group_ref[...] = place_slots(dims, me_ref[0], live_at, ids, order, scratch)
+    lane = lax.broadcasted_iota(jnp.int32, (total, slots), 1)
+    above = lax.broadcasted_iota(jnp.int32, (total, slots), 0)
+    across = jnp.full((total, slots), -1, jnp.int32)
+    down = jnp.zeros((total, slots), jnp.int32)
+    for t in range(total):
+        across = jnp.where(lane == t, live_ref[t], across)
+        down = jnp.where(above == t, live_ref[t], down)
+    ahead = (across > down) | ((across == down) & (lane < above))
     rank = jnp.sum(ahead.astype(jnp.int32), axis=1, keepdims=True)
     ranked = jnp.sum(jnp.where(rank == lane, above, 0), axis=0, keepdims=True)
     large = jnp.sum((across > slots // 2).astype(jnp.int32), axis=1, keepdims=True)[0:1]
-    row_ref[tiles : tiles + 1, :] = jnp.where(lane[0:1] == tiles, large, ranked)
-    pos = lax.broadcasted_iota(jnp.int32, (tiles, slots), 1)
-    here = (pos >> 3 < rows) & ((pos & 7) * rows + (pos >> 3) < live)
-    group_ref[...] = jnp.where(here, codes & 7, GROUPS)
+    row_ref[tiles : tiles + 1, :] = jnp.where(lane[0:1] == total, large, ranked)
 
 
 def splat_kernel(
@@ -173,11 +166,12 @@
     cam_ref,
     row_ref,
     live_ref,
-    group_ref,
+    own_group_ref,
+    their_group_ref,
     mine_ref,
     other_ref,
     target_ref,
-    their_target_ref,
+    message_ref,
     mono_ref,
     image_ref,
     their_image_ref,
@@ -186,8 +180,8 @@
     *scratch,
 ):
     views, tiles_view, slots, pixels, lanes, column = dims
-    table, buf, raw, rec, mom, grad, c_s, h_s, w_hi, w_lo, g_1, g_2, g_3, row_s, row_2, want, got = scratch[:17]
-    accs = scratch[17:]
+    table, buf, raw, rec, mom, grad, c_s, h_s, w_hi, w_lo, g_1, g_2, g_3, row_s, row_2, want, got, group_ref = scratch[:18]
+    accs = scratch[18:]
     tiles = views * tiles_view
     chips = mine_ref.shape[0]
     half = chips * column
@@ -200,8 +194,14 @@
         ref[...] = jnp.zeros_like(ref)
 
     kept = tiles_view // 2
-    want[:, :, 0:kept, :] = target_ref[:, :, 0:kept, :]
-    want[:, :, kept:, :] = their_target_ref[...]
+    part_tiles = views * kept
+    for v in range(views):
+        for c in range(3):
+            want[v, c, :, :] = target_ref[v, c, 0:kept, :]
+            start = 2 * part_tiles + (v * 3 + c) * kept
+            want[views + v, c, :, :] = message_ref[start : start + kept, :]
+    group_ref[0:part_tiles, :] = own_group_ref[...]
+    group_ref[part_tiles:, :] = their_group_ref[...]
 
     def build(q, _):
         for base, ref in ((0, mine_ref), (half, other_ref)):
@@ -214,7 +214,7 @@
     lax.fori_loop(0, chips, build, 0)
 
     def live_of(t):
-        return live_ref[lax.div(t, tiles_view), lax.rem(t, tiles_view)]
+        return live_ref[t]
 
     def in_turn(body):
         def trip(s, _, positions):
@@ -249,8 +249,8 @@
     in_turn(fetch)
 
     def project(v):
-        block = slice(v * tiles_view, (v + 1) * tiles_view)
-        cam = [cam_ref[v * 8 + n] for n in range(8)]
+        block = slice(v * kept, (v + 1) * kept)
+        cam = [cam_ref[v % views * 8 + n] for n in range(8)]
         field = lambda f: raw[f, block, :]
         u = cam[0] * field(0) + cam[1] * field(1) + cam[2] * field(2) + cam[3]
         w = cam[4] * field(0) + cam[5] * field(1) + cam[6] * field(2) + cam[7]
@@ -274,7 +274,7 @@
         here = group_ref[block, :] < GROUPS
         return here, cam, block, u, w, (d0, d1, d2), f0, f1, conic
 
-    for v in range(views):
+    for v in range(2 * views):
         here, cam, block, u, w, _, _, _, (ka, kb, kc) = project(v)
         x_line = ka * u + kb * w
         y_line = kb * u + kc * w
@@ -350,7 +350,7 @@
 
         after = []
         for g, t in enumerate(tile):
-            v, tl = lax.div(t, tiles_view), lax.rem(t, tiles_view)
+            v, tl = lax.div(t, kept), lax.rem(t, kept)
             spread = [
                 jnp.where(own_chunk[:, used], jnp.broadcast_to(piece[c : c + 1], (GROUPS, positions)), 0.0)
                 for c in range(3)
@@ -417,10 +417,10 @@
                 mom[6 + c, pl.ds(t, 1), :] = row_s[g, 8 + c : 9 + c, :]
 
     in_turn(render)
-    image_ref[...] = got[:, :, 0:kept, :]
-    their_image_ref[...] = got[:, :, kept:, :]
-
-    for v in range(views):
+    image_ref[...] = got[0:views]
+    their_image_ref[...] = got[views:]
+
+    for v in range(2 * views):
         here, cam, block, u, w, (d0, d1, d2), f0, f1, (ka, kb, kc) = project(v)
         mxx, mxy, myy, mx, my, m1 = [jnp.where(here, mom[n, block, :], 0.0) for n in range(6)]
         dx = mx - u * m1
@@ -535,50 +535,68 @@
 
     smem = pl.BlockSpec(memory_space=pltpu.SMEM)
     vmem = pl.BlockSpec(memory_space=pltpu.VMEM)
-    prep = pl.pallas_call(
-        partial(
-            prep_kernel,
-            (log2_of(own_count), log2_of(lanes), log2_of(view_group), log2_of(tile_group), tiles_view),
-        ),
+    kept = tiles_view // 2
+    part_tiles = views * kept
+    dims = (log2_of(own_count), log2_of(lanes), log2_of(view_group), log2_of(tile_group))
+    prep_options = dict(
+        scratch_shapes=[
+            pltpu.VMEM((3, part_tiles, slots), F32),
+            pltpu.VMEM((part_tiles, slots), F32),
+            pltpu.VMEM((part_tiles, slots), F32),
+            pltpu.VMEM((UNROLL, 16, slots), F32),
+            pltpu.VMEM((part_tiles, slots), jnp.int32),
+            pltpu.VMEM((part_tiles, slots), F32),
+        ],
+        compiler_params=pltpu.CompilerParams(vmem_limit_bytes=8 * 1024 * 1024),
+        cost_estimate=pl.CostEstimate(flops=4_000_000_000, bytes_accessed=8 * tiles * slots, transcendentals=0),
+    )
+    prep_own = pl.pallas_call(
+        partial(prep_own_kernel, dims),
         out_shape=[
-            jax.ShapeDtypeStruct((tiles + 8, slots), jnp.int32),
-            jax.ShapeDtypeStruct((tiles, slots), jnp.int32),
+            jax.ShapeDtypeStruct((part_tiles, slots), jnp.int32),
+            jax.ShapeDtypeStruct((part_tiles, slots), jnp.int32),
             jax.ShapeDtypeStruct((views * 8,), F32),
         ],
-        in_specs=[smem] * 3 + [vmem] * 3,
+        in_specs=[smem] * 3 + [vmem] * 2,
         out_specs=[vmem, vmem, smem],
-        scratch_shapes=[
-            pltpu.VMEM((3, tiles, slots), F32),
-            pltpu.VMEM((tiles, slots), F32),
-            pltpu.VMEM((tiles, slots), F32),
-            pltpu.VMEM((UNROLL, 16, slots), F32),
-            pltpu.VMEM((tiles, slots), jnp.int32),
-            pltpu.VMEM((tiles, slots), F32),
+        name="prep_own",
+        **prep_options,
+    )
+    prep_their = pl.pallas_call(
+        partial(prep_their_kernel, dims),
+        out_shape=[
+            jax.ShapeDtypeStruct((part_tiles + 8, slots), jnp.int32),
+            jax.ShapeDtypeStruct((part_tiles, slots), jnp.int32),
         ],
-        cost_estimate=pl.CostEstimate(flops=8_000_000_000, bytes_accessed=4 * tiles * slots * 4, transcendentals=0),
-        name="prep",
-    )
-
-    kept = tiles_view // 2
+        in_specs=[smem] * 2 + [vmem],
+        out_specs=[vmem] * 2,
+        name="prep_their",
+        **prep_options,
+    )
+
     mirror = tile_group - 1
-    live_row = jnp.pad(live_count[:, None, kept:], ((0, 0), (0, 7), (0, slots - kept)))
-    theirs = jnp.concatenate([intersection_ids[:, kept:], depth_order[:, kept:], live_row], axis=1)
-
+    target = target.transpose(0, 2, 1, 3)
+    message = jnp.concatenate(
+        [
+            intersection_ids[:, kept:].reshape(part_tiles, slots).astype(F32),
+            depth_order[:, kept:].reshape(part_tiles, slots).astype(F32),
+            target[:, :, kept:].reshape(3 * part_tiles, pixels),
+            jnp.pad(live_count[:, kept:].astype(F32), ((0, 8 - views), (0, slots - kept))),
+        ]
+    )
     fields = jnp.concatenate([centres, shape_raw, opacity_logit[None], colours], axis=0)
     block = fields.reshape(FIELDS * GROUPS, lanes)
     note = jnp.pad(totals.astype(F32)[None], ((0, 7), (0, lanes - views)))
-    beyond = [swap(block, "view", m) for m in range(1, view_group)]
-    level = [swap(block, "tile", 2 * m) for m in range(1, chips)]
-    theirs = swap(theirs, "tile", mirror)
-    beyond = jnp.concatenate(beyond + [note])
-    beyond, theirs, *level = lax.optimization_barrier((beyond, theirs, *level))
-    far = [swap(beyond, "tile", 2 * m) for m in range(1, chips)]
-    mine = jnp.stack([jnp.concatenate([near, rest]) for near, rest in zip([block] + level, [beyond] + far)])
-    live_now = jnp.concatenate([live_count[:, :kept], theirs[:, 2 * kept, :kept]], axis=1)
-    rows, group, cam = prep(me[None], live_now, camera, intersection_ids, depth_order, theirs)
-    mine, rows, group, cam = lax.optimization_barrier((mine, rows.reshape(-1), group, cam))
-    target = target.transpose(0, 2, 1, 3)
-    their_target = swap(target[:, :, kept:], "tile", mirror)
+    column = jnp.concatenate([block] + [swap(block, "view", m) for m in range(1, view_group)] + [note])
+    message = swap(message, "tile", mirror)
+    own_rows, own_group, cam = prep_own(me[None], live_count, camera, intersection_ids, depth_order)
+    column, own_rows, own_group, cam = lax.optimization_barrier((column, own_rows, own_group, cam))
+    mine = jnp.stack([column] + [swap(column, "tile", 2 * m) for m in range(1, chips)])
+    their_live = message[5 * part_tiles : 5 * part_tiles + views, :kept].astype(jnp.int32)
+    live_now = jnp.concatenate([live_count[:, :kept].reshape(-1), their_live.reshape(-1)])
+    their_rows, their_group = prep_their(me[None], live_now, message)
+    rows = jnp.concatenate([own_rows, their_rows]).reshape(-1)
+    mine, rows, their_group = lax.optimization_barrier((mine, rows, their_group))
     other = swap(mine, "tile", 1)
 
     table_rows = devices * lanes
@@ -594,7 +612,7 @@
             jax.ShapeDtypeStruct(half, F32),
             jax.ShapeDtypeStruct(half, F32),
         ],
-        in_specs=[smem] * 3 + [vmem] * 6,
+        in_specs=[smem] * 3 + [vmem] * 7,
         out_specs=[vmem] * 4,
         scratch_shapes=[
             pltpu.VMEM((table_rows, lanes), F32),
@@ -608,7 +626,8 @@
         ]
         + [pltpu.VMEM(square, BF16)] * 5
         + [pltpu.VMEM((BATCH, 16, slots), F32), pltpu.VMEM((BATCH, 8, pixels), F32)]
-        + [pltpu.VMEM((views, 3, tiles_view, pixels), F32)] * 2
+        + [pltpu.VMEM((2 * views, 3, kept, pixels), F32)] * 2
+        + [pltpu.VMEM((tiles, slots), jnp.int32)]
         + [pltpu.VMEM((table_rows, lanes), F32)] * accs,
         compiler_params=pltpu.CompilerParams(vmem_limit_bytes=room),
         name="splat",
@@ -617,11 +636,12 @@
         cam,
         rows,
         live_now,
-        group,
+        own_group,
+        their_group,
         mine,
         other,
         target,
-        their_target,
+        message,
         monomials(pixels),
     )
 
@@ -639,15 +659,10 @@
     grad_other = swap(grad_other, "tile", 1)
     rendered = jnp.concatenate([image, swap(their_image, "tile", mirror)], axis=2)
     joined = (grad_mine + grad_other).reshape(chips, view_group, FIELDS * GROUPS, lanes)
-    far = [swap(joined[m, 1:], "tile", 2 * m) for m in range(1, chips)]
-    near = joined[:, 0]
-    near, *far = lax.optimization_barrier((near, *far))
-    beyond = joined[0, 1:]
-    for part in far:
-        beyond = beyond + part
-    parts = [near[0]]
-    parts += [swap(beyond[m - 1], "view", m) for m in range(1, view_group)]
-    parts += [swap(near[m], "tile", 2 * m) for m in range(1, chips)]
+    part = joined[0]
+    for m in range(1, chips):
+        part = part + swap(joined[m], "tile", 2 * m)
+    parts = [part[0]] + [swap(part[m], "view", m) for m in range(1, view_group)]
     tail = pl.pallas_call(
         tail_kernel,
         out_shape=[jax.ShapeDtypeStruct((count, own_count), F32) for count in (3, 6, 1, 3)],

time: 93.5 us -> 89.3 us (0.955)
  starting transfers between devices: 30.1 us -> 18.7 us
  waiting for transfers between devices: 18 us -> 24 us
  Pallas kernels: 35.6 us -> 38.9 us
  local copies, waits for them, and re-layouts: 3.76 us -> 1.77 us
    ppermute x23 -> x16, starting transfers between devices: 30.1 us -> 18.7 us  [swap(): return lax.ppermute(array, axis, [(i, i ^ mask) for i in range(size)])]
    ppermute x23 -> x16, waiting for transfers between devices: 18 us -> 24 us  [swap(): return lax.ppermute(array, axis, [(i, i ^ mask) for i in range(size)])]
    pallas_call x2 -> x3, Pallas kernels: 34.9 us -> 38.2 us  [the longest x1 32.9 us: shards(): splat(cam, rows, live_now, own_group, their_group, mine, other, target, m...]
    unnamed x20 -> x18, local copies, waits for them, and re-layouts: 2.87 us -> 1.52 us
  transfers between devices with their start and end apart: 23 -> 16, of which waited for: 8 -> 8; matrix products, arithmetic and copies ran while one was open for 5% -> 4% of each run, Pallas kernels for 6% -> 6%
where the time goes in v3:
time: 89.3 us; the launch traced here: 88.4 us
  Pallas kernels  38.9 us (44%)
  waiting for transfers between devices  24 us (27%)
  starting transfers between devices  18.7 us (21%)
  other arithmetic  4.17 us (5%)
  local copies, waits for them, and re-layouts  1.77 us (2%)
    pallas_call x1, Pallas kernels, shards(): splat(cam, rows, live_now, own_group, their_group, mine, other, target, m...  32.9 us
    ppermute x16, waiting for transfers between devices, swap(): return lax.ppermute(array, axis, [(i, i ^ mask) for i in range(size)])  24 us
    ppermute x16, starting transfers between devices, swap(): return lax.ppermute(array, axis, [(i, i ^ mask) for i in range(size)])  18.7 us
    pallas_call x1, Pallas kernels, shards(): prep_own(me[None], live_count, camera, intersection_ids, depth_order)  2.76 us
    pallas_call x1, Pallas kernels, shards(): their_rows, their_group = prep_their(me[None], live_now, message)  2.55 us
  transfers between devices with their start and end apart: 16, of which 8 were waited for; matrix products, arithmetic and copies ran while one was open for 4% of the time, Pallas kernels for 6%

profile of v3, /device:TPU:0, one launch (start us, length us, event | category | flops | bytes accessed | tf_op | source)
XLA Modules:
  0.0 88.4 jit_solution(7502147142097700196)
XLA Ops:
  0.6 0.8 pad_maximum_fusion.1
  1.5 3.1 %collective-permute-start = (f32[104,128]{1,0:T(8,128)S(1)}, f32[104,128]{1,0:T(8,128)S(1)}, u32[]{:S(2)}, u32[]{:S(2)}) collective-permute-start(f32[104,128]{1,0:T(8,128)S(1)} %reshape.158), channel_id=1, source_target_pairs={{0,8},{8,0},{16,24},{24,16},{1,9},{9,1},{17,25},{25,17},{2,10},{10... | collective-permute-start | bytes 159752 | tf_op jit(solution)/shard_map/ppermute | solution.py:516
  4.6 2.6 %collective-permute-start.1 = (f32[104,128]{1,0:T(8,128)S(1)}, f32[104,128]{1,0:T(8,128)S(1)}, u32[]{:S(2)}, u32[]{:S(2)}) collective-permute-start(f32[104,128]{1,0:T(8,128)S(1)} %reshape.158), channel_id=1, source_target_pairs={{0,16},{8,24},{16,0},{24,8},{1,17},{9,25},{17,1},{25,9},{2,18},{10... | collective-permute-start | bytes 159752 | tf_op jit(solution)/shard_map/ppermute | solution.py:516
  7.2 0.0 collective-permute-start.2
  7.2 0.0 copy-start.4
  7.3 0.6 copy-done.1
  7.9 0.1 fusion.19
  8.0 0.0 copy-done.3
  8.0 0.0 copy-done.4
  8.0 1.4 %collective-permute-start.6 = (f32[88,256]{1,0:T(8,128)S(1)}, f32[88,256]{1,0:T(8,128)S(1)}, u32[]{:S(2)}, u32[]{:S(2)}) collective-permute-start(f32[88,256]{1,0:T(8,128)S(1)} %select_maximum_fusion), channel_id=1, source_target_pairs={{0,7},{1,6},{2,5},{3,4},{4,3},{5,2},{6,1},{7,0},{8,15},{9,14},{10,... | collective-permute-start | bytes 270344 | tf_op jit(solution)/shard_map/ppermute | solution.py:516
  9.4 0.7 copy-done.5
  10.1 0.1 copy.16.camera_ref
  10.2 0.1 reduce_sum.9
  10.3 2.8 %prep_own.1 = (s32[16,256]{1,0:T(8,128)S(1)}, s32[16,256]{1,0:T(8,128)S(1)}, f32[16]{0:T(128)S(1)}) custom-call(s32[1]{0:T(128)} %bitcast.2.me_ref, s32[2,16]{1,0:T(2,128)S(1)} %copy-done.1, f32[8,2,4]{2,1,0:T(2,128)S(1)} %copy.16.camera_ref, s32[2,16,256]{2,1,0:T(8,128)S(1)} %copy-done.3, s32[2,16,256]{2,1,0:T(8,128)S(1)} %copy-done.4), custom_call_target="tpu_custom_call" | custom-call | flops 4000000000 | bytes 65536 | tf_op jit(solution)/shard_map/prep_own/pallas_call | solution.py:592
  13.1 0.1 reshape.159
  13.2 0.0 collective-permute-done
  13.2 0.0 collective-permute-done.1
  13.2 0.0 collective-permute-done.2
  13.3 1.5 %collective-permute-start.3 = (f32[424,128]{1,0:T(8,128)S(1)}, f32[424,128]{1,0:T(8,128)S(1)}, u32[]{:S(2)}, u32[]{:S(2)}) collective-permute-start(f32[424,128]{1,0:T(8,128)S(1)} %constant_dynamic-update-slice_fusion), channel_id=1, source_target_pairs={{0,2},{1,3},{2,0},{3,1},{4,6},{5,7},{6,4},{7,5},{8,10},{9,11},{10,... | collective-permute-start | bytes 651272 | tf_op jit(solution)/shard_map/ppermute | solution.py:516
  14.7 1.5 %collective-permute-start.4 = (f32[424,128]{1,0:T(8,128)S(1)}, f32[424,128]{1,0:T(8,128)S(1)}, u32[]{:S(2)}, u32[]{:S(2)}) collective-permute-start(f32[424,128]{1,0:T(8,128)S(1)} %constant_dynamic-update-slice_fusion), channel_id=1, source_target_pairs={{0,4},{1,5},{2,6},{3,7},{4,0},{5,1},{6,2},{7,3},{8,12},{9,13},{10,... | collective-permute-start | bytes 651272 | tf_op jit(solution)/shard_map/ppermute | solution.py:516
  16.2 0.6 collective-permute-start.5
  16.8 0.1 reshape.161
  16.9 0.1 pad_add_fusion.live_ref
  17.0 2.6 %prep_their.1 = (s32[24,256]{1,0:T(8,128)S(1)}, s32[16,256]{1,0:T(8,128)S(1)}) custom-call(s32[1]{0:T(128)} %bitcast.2.me_ref, s32[32]{0:T(128)S(1)} %pad_add_fusion.live_ref, f32[88,256]{1,0:T(8,128)S(1)} %collective-permute-done.6.message_ref), custom_call_target="tpu_custom_call" | custom-call | flops 4000000000 | bytes 65536 | tf_op jit(solution)/shard_map/prep_their/pallas_call | solution.py:597
  19.6 1.5 %collective-permute-done.3 = f32[424,128]{1,0:T(8,128)S(1)} collective-permute-done((f32[424,128]{1,0:T(8,128)S(1)}, f32[424,128]{1,0:T(8,128)S(1)}, u32[]{:S(2)}, u32[]{:S(2)}) %collective-permute-start.3) | collective-permute-done | bytes 217120 | tf_op jit(solution)/shard_map/ppermute | solution.py:516
  21.1 5.9 %collective-permute-done.4 = f32[424,128]{1,0:T(8,128)S(1)} collective-permute-done((f32[424,128]{1,0:T(8,128)S(1)}, f32[424,128]{1,0:T(8,128)S(1)}, u32[]{:S(2)}, u32[]{:S(2)}) %collective-permute-start.4) | collective-permute-done | bytes 217120 | tf_op jit(solution)/shard_map/ppermute | solution.py:516
  26.9 0.1 pad_maximum_fusion.mine_ref
  27.0 0.1 collective-permute-start.7
  27.1 2.4 %collective-permute-done.7.other_ref = f32[4,424,128]{2,1,0:T(8,128)S(1)} collective-permute-done((f32[4,424,128]{2,1,0:T(8,128)S(1)}, f32[4,424,128]{2,1,0:T(8,128)S(1)}, u32[]{:S(2)}, u32[]{:S(2)}) %collective-permute-start.7) | collective-permute-done | bytes 868384 | tf_op jit(solution)/shard_map/ppermute | solution.py:516
  29.5 32.9 %splat.1 = (f32[2,3,8,256]{3,2,1,0:T(8,128)S(1)}, f32[2,3,8,256]{3,2,1,0:T(8,128)S(1)}, f32[16,104,128]{2,1,0:T(8,128)S(1)}, f32[16,104,128]{2,1,0:T(8,128)}) custom-call(f32[16]{0:T(128)S(1)} %get-tuple-element.29.cam_ref, s32[10240]{0:T(1024)S(1)} %bitcast.88, s32[32]{0:T(128)S(1)} %pad_add_fusion.live_ref, s32[16,256]{1,0:T(8,128)S(1)} %get-tuple-element.35.own_group_ref, ...), custom_call_target="tpu_custom_call" | custom-call | tf_op jit(solution)/shard_map/splat/pallas_call | solution.py:635
  62.4 0.2 reduce_window_sum.11
  62.6 0.0 collective-permute-start.8
  62.7 2.5 %collective-permute-done.9 = f32[16,104,128]{2,1,0:T(8,128)} collective-permute-done((f32[16,104,128]{2,1,0:T(8,128)}, f32[16,104,128]{2,1,0:T(8,128)}, u32[]{:S(2)}, u32[]{:S(2)}) %collective-permute-start.9) | collective-permute-done | bytes 852000 | tf_op jit(solution)/shard_map/ppermute | solution.py:516
  65.2 1.2 %add.141 = f32[16,104,128]{2,1,0:T(8,128)S(1)} add(f32[16,104,128]{2,1,0:T(8,128)S(1)} %get-tuple-element.40, f32[16,104,128]{2,1,0:T(8,128)} %collective-permute-done.9) | non-fusion elementwise | flops 212992 | bytes 2555904 | tf_op jit(solution)/shard_map/add | solution.py:661
  66.5 0.1 collective-permute-start.10
  66.5 1.1 %collective-permute-start.11 = (f32[4,104,128]{2,1,0:T(8,128)S(1)}, f32[4,104,128]{2,1,0:T(8,128)S(1)}, u32[]{:S(2)}, u32[]{:S(2)}) collective-permute-start(f32[4,104,128]{2,1,0:T(8,128)S(1)} %get-tuple-element.50), channel_id=1, source_target_pairs={{0,4},{1,5},{2,6},{3,7},{4,0},{5,1},{6,2},{7,3},{8,12},{9,13},{10,... | collective-permute-start | bytes 638984 | tf_op jit(solution)/shard_map/ppermute | solution.py:516
  67.6 2.4 %collective-permute-start.12 = (f32[4,104,128]{2,1,0:T(8,128)S(1)}, f32[4,104,128]{2,1,0:T(8,128)S(1)}, u32[]{:S(2)}, u32[]{:S(2)}) collective-permute-start(f32[4,104,128]{2,1,0:T(8,128)S(1)} %get-tuple-element.49), channel_id=1, source_target_pairs={{0,6},{1,7},{2,4},{3,5},{4,2},{5,3},{6,0},{7,1},{8,14},{9,15},{10,... | collective-permute-start | bytes 638984 | tf_op jit(solution)/shard_map/ppermute | solution.py:516
  70.0 0.8 and_select_fusion
  70.8 3.9 %collective-permute-done.10 = f32[4,104,128]{2,1,0:T(8,128)S(1)} collective-permute-done((f32[4,104,128]{2,1,0:T(8,128)S(1)}, f32[4,104,128]{2,1,0:T(8,128)S(1)}, u32[]{:S(2)}, u32[]{:S(2)}) %collective-permute-start.10) | collective-permute-done | bytes 213024 | tf_op jit(solution)/shard_map/ppermute | solution.py:516
  74.6 3.8 %collective-permute-done.11 = f32[4,104,128]{2,1,0:T(8,128)S(1)} collective-permute-done((f32[4,104,128]{2,1,0:T(8,128)S(1)}, f32[4,104,128]{2,1,0:T(8,128)S(1)}, u32[]{:S(2)}, u32[]{:S(2)}) %collective-permute-start.11) | collective-permute-done | bytes 213024 | tf_op jit(solution)/shard_map/ppermute | solution.py:516
  78.5 0.1 fusion.1
  78.5 1.9 %collective-permute-start.13 = (f32[104,128]{1,0:T(8,128)S(1)}, f32[104,128]{1,0:T(8,128)S(1)}, u32[]{:S(2)}, u32[]{:S(2)}) collective-permute-start(f32[104,128]{1,0:T(8,128)S(1)} %get-tuple-element.53), channel_id=1, source_target_pairs={{0,8},{8,0},{16,24},{24,16},{1,9},{9,1},{17,25},{25,17},{2,10},{10... | collective-permute-start | bytes 159752 | tf_op jit(solution)/shard_map/ppermute | solution.py:516
  80.5 1.4 %collective-permute-start.14 = (f32[104,128]{1,0:T(8,128)S(1)}, f32[104,128]{1,0:T(8,128)S(1)}, u32[]{:S(2)}, u32[]{:S(2)}) collective-permute-start(f32[104,128]{1,0:T(8,128)S(1)} %get-tuple-element.52), channel_id=1, source_target_pairs={{0,16},{8,24},{16,0},{24,8},{1,17},{9,25},{17,1},{25,9},{2,18},{10... | collective-permute-start | bytes 159752 | tf_op jit(solution)/shard_map/ppermute | solution.py:516
  81.8 1.2 %collective-permute-start.15 = (f32[104,128]{1,0:T(8,128)S(1)}, f32[104,128]{1,0:T(8,128)S(1)}, u32[]{:S(2)}, u32[]{:S(2)}) collective-permute-start(f32[104,128]{1,0:T(8,128)S(1)} %get-tuple-element.51), channel_id=1, source_target_pairs={{0,24},{8,16},{16,8},{24,0},{1,25},{9,17},{17,9},{25,1},{2,26},{10... | collective-permute-start | bytes 159752 | tf_op jit(solution)/shard_map/ppermute | solution.py:516
  83.0 0.7 maximum_bitcast_fusion
  83.7 2.6 %collective-permute-done.14.refs_2_ = f32[104,128]{1,0:T(8,128)S(1)} collective-permute-done((f32[104,128]{1,0:T(8,128)S(1)}, f32[104,128]{1,0:T(8,128)S(1)}, u32[]{:S(2)}, u32[]{:S(2)}) %collective-permute-start.14) | collective-permute-done | bytes 53280 | tf_op jit(solution)/shard_map/ppermute | solution.py:516
  86.3 1.5 %collective-permute-done.15.refs_3_ = f32[104,128]{1,0:T(8,128)S(1)} collective-permute-done((f32[104,128]{1,0:T(8,128)S(1)}, f32[104,128]{1,0:T(8,128)S(1)}, u32[]{:S(2)}, u32[]{:S(2)}) %collective-permute-start.15) | collective-permute-done | bytes 53280 | tf_op jit(solution)/shard_map/ppermute | solution.py:516
  87.8 0.7 tail.1
  (30 shorter events, 0.2 us)
Async XLA Ops:
  0.6 6.6 %copy-start = (f32[2,16,3,256]{3,1,2,0:T(8,128)S(1)}, f32[2,16,3,256]{3,1,2,0:T(8,128)}, u32[]{:S(2)}) copy-start(f32[2,16,3,256]{3,1,2,0:T(8,128)} %param.15) | copy-start | bytes 294916
  1.5 11.7 %collective-permute-start = (f32[104,128]{1,0:T(8,128)S(1)}, f32[104,128]{1,0:T(8,128)S(1)}, u32[]{:S(2)}, u32[]{:S(2)}) collective-permute-start(f32[104,128]{1,0:T(8,128)S(1)} %reshape.158), channel_id=1, source_target_pairs={{0,8},{8,0},{16,24},{24,16},{1,9},{9,1},{17,25},{25,17},{2,10},{10... | collective-permute-start | bytes 159752 | tf_op jit(solution)/shard_map/ppermute | solution.py:516
  4.6 8.6 %collective-permute-start.1 = (f32[104,128]{1,0:T(8,128)S(1)}, f32[104,128]{1,0:T(8,128)S(1)}, u32[]{:S(2)}, u32[]{:S(2)}) collective-permute-start(f32[104,128]{1,0:T(8,128)S(1)} %reshape.158), channel_id=1, source_target_pairs={{0,16},{8,24},{16,0},{24,8},{1,17},{9,25},{17,1},{25,9},{2,18},{10... | collective-permute-start | bytes 159752 | tf_op jit(solution)/shard_map/ppermute | solution.py:516
  7.2 6.0 %collective-permute-start.2 = (f32[104,128]{1,0:T(8,128)S(1)}, f32[104,128]{1,0:T(8,128)S(1)}, u32[]{:S(2)}, u32[]{:S(2)}) collective-permute-start(f32[104,128]{1,0:T(8,128)S(1)} %reshape.158), channel_id=1, source_target_pairs={{0,24},{8,16},{16,8},{24,0},{1,25},{9,17},{17,9},{25,1},{2,26},{10... | collective-permute-start | bytes 159752 | tf_op jit(solution)/shard_map/ppermute | solution.py:516
  7.2 0.7 copy-start.1
  7.2 0.8 copy-start.3
  7.2 0.8 copy-start.4
  8.0 8.8 %collective-permute-start.6 = (f32[88,256]{1,0:T(8,128)S(1)}, f32[88,256]{1,0:T(8,128)S(1)}, u32[]{:S(2)}, u32[]{:S(2)}) collective-permute-start(f32[88,256]{1,0:T(8,128)S(1)} %select_maximum_fusion), channel_id=1, source_target_pairs={{0,7},{1,6},{2,5},{3,4},{4,3},{5,2},{6,1},{7,0},{8,15},{9,14},{10,... | collective-permute-start | bytes 270344 | tf_op jit(solution)/shard_map/ppermute | solution.py:516
  9.4 0.7 copy-start.5
  13.3 7.8 %collective-permute-start.3 = (f32[424,128]{1,0:T(8,128)S(1)}, f32[424,128]{1,0:T(8,128)S(1)}, u32[]{:S(2)}, u32[]{:S(2)}) collective-permute-start(f32[424,128]{1,0:T(8,128)S(1)} %constant_dynamic-update-slice_fusion), channel_id=1, source_target_pairs={{0,2},{1,3},{2,0},{3,1},{4,6},{5,7},{6,4},{7,5},{8,10},{9,11},{10,... | collective-permute-start | bytes 651272 | tf_op jit(solution)/shard_map/ppermute | solution.py:516
  14.7 12.2 %collective-permute-start.4 = (f32[424,128]{1,0:T(8,128)S(1)}, f32[424,128]{1,0:T(8,128)S(1)}, u32[]{:S(2)}, u32[]{:S(2)}) collective-permute-start(f32[424,128]{1,0:T(8,128)S(1)} %constant_dynamic-update-slice_fusion), channel_id=1, source_target_pairs={{0,4},{1,5},{2,6},{3,7},{4,0},{5,1},{6,2},{7,3},{8,12},{9,13},{10,... | collective-permute-start | bytes 651272 | tf_op jit(solution)/shard_map/ppermute | solution.py:516
  16.2 10.7 %collective-permute-start.5 = (f32[424,128]{1,0:T(8,128)S(1)}, f32[424,128]{1,0:T(8,128)S(1)}, u32[]{:S(2)}, u32[]{:S(2)}) collective-permute-start(f32[424,128]{1,0:T(8,128)S(1)} %constant_dynamic-update-slice_fusion), channel_id=1, source_target_pairs={{0,6},{1,7},{2,4},{3,5},{4,2},{5,3},{6,0},{7,1},{8,14},{9,15},{10,... | collective-permute-start | bytes 651272 | tf_op jit(solution)/shard_map/ppermute | solution.py:516
  26.9 2.6 %copy-start.2 = (bf16[32,256]{1,0:T(8,128)(2,1)S(1)}, bf16[32,256]{1,0:T(8,128)(2,1)}, u32[]{:S(2)}) copy-start(bf16[32,256]{1,0:T(8,128)(2,1)} %constant.40.clone.mono_ref) | copy-start | bytes 49156
  27.0 2.5 %collective-permute-start.7 = (f32[4,424,128]{2,1,0:T(8,128)S(1)}, f32[4,424,128]{2,1,0:T(8,128)S(1)}, u32[]{:S(2)}, u32[]{:S(2)}) collective-permute-start(f32[4,424,128]{2,1,0:T(8,128)S(1)} %pad_maximum_fusion.mine_ref), channel_id=1, source_target_pairs={{0,1},{1,0},{2,3},{3,2},{4,5},{5,4},{6,7},{7,6},{8,9},{9,8},{10,11... | collective-permute-start | bytes 2605064 | tf_op jit(solution)/shard_map/ppermute | solution.py:516
  62.4 2.7 %collective-permute-start.9 = (f32[16,104,128]{2,1,0:T(8,128)}, f32[16,104,128]{2,1,0:T(8,128)}, u32[]{:S(2)}, u32[]{:S(2)}) collective-permute-start(f32[16,104,128]{2,1,0:T(8,128)} %get-tuple-element.41), channel_id=1, source_target_pairs={{0,1},{1,0},{2,3},{3,2},{4,5},{5,4},{6,7},{7,6},{8,9},{9,8},{10,11... | collective-permute-start | bytes 2555912 | tf_op jit(solution)/shard_map/ppermute | solution.py:516
  62.6 20.4 %collective-permute-start.8 = (f32[2,3,8,256]{3,2,1,0:T(8,128)S(1)}, f32[2,3,8,256]{3,2,1,0:T(8,128)S(1)}, u32[]{:S(2)}, u32[]{:S(2)}) collective-permute-start(f32[2,3,8,256]{3,2,1,0:T(8,128)S(1)} %get-tuple-element.39), channel_id=1, source_target_pairs={{0,7},{1,6},{2,5},{3,4},{4,3},{5,2},{6,1},{7,0},{8,15},{9,14},{10,... | collective-permute-start | bytes 147464 | tf_op jit(solution)/shard_map/ppermute | solution.py:516
  66.5 8.2 %collective-permute-start.10 = (f32[4,104,128]{2,1,0:T(8,128)S(1)}, f32[4,104,128]{2,1,0:T(8,128)S(1)}, u32[]{:S(2)}, u32[]{:S(2)}) collective-permute-start(f32[4,104,128]{2,1,0:T(8,128)S(1)} %get-tuple-element.48), channel_id=1, source_target_pairs={{0,2},{1,3},{2,0},{3,1},{4,6},{5,7},{6,4},{7,5},{8,10},{9,11},{10,... | collective-permute-start | bytes 638984 | tf_op jit(solution)/shard_map/ppermute | solution.py:516
  66.5 11.9 %collective-permute-start.11 = (f32[4,104,128]{2,1,0:T(8,128)S(1)}, f32[4,104,128]{2,1,0:T(8,128)S(1)}, u32[]{:S(2)}, u32[]{:S(2)}) collective-permute-start(f32[4,104,128]{2,1,0:T(8,128)S(1)} %get-tuple-element.50), channel_id=1, source_target_pairs={{0,4},{1,5},{2,6},{3,7},{4,0},{5,1},{6,2},{7,3},{8,12},{9,13},{10,... | collective-permute-start | bytes 638984 | tf_op jit(solution)/shard_map/ppermute | solution.py:516
  67.6 10.8 %collective-permute-start.12 = (f32[4,104,128]{2,1,0:T(8,128)S(1)}, f32[4,104,128]{2,1,0:T(8,128)S(1)}, u32[]{:S(2)}, u32[]{:S(2)}) collective-permute-start(f32[4,104,128]{2,1,0:T(8,128)S(1)} %get-tuple-element.49), channel_id=1, source_target_pairs={{0,6},{1,7},{2,4},{3,5},{4,2},{5,3},{6,0},{7,1},{8,14},{9,15},{10,... | collective-permute-start | bytes 638984 | tf_op jit(solution)/shard_map/ppermute | solution.py:516
  78.5 5.1 %collective-permute-start.13 = (f32[104,128]{1,0:T(8,128)S(1)}, f32[104,128]{1,0:T(8,128)S(1)}, u32[]{:S(2)}, u32[]{:S(2)}) collective-permute-start(f32[104,128]{1,0:T(8,128)S(1)} %get-tuple-element.53), channel_id=1, source_target_pairs={{0,8},{8,0},{16,24},{24,16},{1,9},{9,1},{17,25},{25,17},{2,10},{10... | collective-permute-start | bytes 159752 | tf_op jit(solution)/shard_map/ppermute | solution.py:516
  80.5 5.8 %collective-permute-start.14 = (f32[104,128]{1,0:T(8,128)S(1)}, f32[104,128]{1,0:T(8,128)S(1)}, u32[]{:S(2)}, u32[]{:S(2)}) collective-permute-start(f32[104,128]{1,0:T(8,128)S(1)} %get-tuple-element.52), channel_id=1, source_target_pairs={{0,16},{8,24},{16,0},{24,8},{1,17},{9,25},{17,1},{25,9},{2,18},{10... | collective-permute-start | bytes 159752 | tf_op jit(solution)/shard_map/ppermute | solution.py:516
  81.8 5.9 %collective-permute-start.15 = (f32[104,128]{1,0:T(8,128)S(1)}, f32[104,128]{1,0:T(8,128)S(1)}, u32[]{:S(2)}, u32[]{:S(2)}) collective-permute-start(f32[104,128]{1,0:T(8,128)S(1)} %get-tuple-element.51), channel_id=1, source_target_pairs={{0,24},{8,16},{16,8},{24,0},{1,25},{9,17},{17,9},{25,1},{2,26},{10... | collective-permute-start | bytes 159752 | tf_op jit(solution)/shard_map/ppermute | solution.py:516

commit v4 on v3

--- a/solution.py
+++ b/solution.py
@@ -15,8 +15,9 @@
 FIELDS = 13
 GROUPS = 8
 ACCS = 4
-UNROLL = 4
-BATCH = 4
+UNROLL = 8
+SIZES = 3
+BATCH = 8
 LOG2E = math.log2(math.e)
 OFF = -1e4
 
@@ -157,8 +158,10 @@
     ahead = (across > down) | ((across == down) & (lane < above))
     rank = jnp.sum(ahead.astype(jnp.int32), axis=1, keepdims=True)
     ranked = jnp.sum(jnp.where(rank == lane, above, 0), axis=0, keepdims=True)
-    large = jnp.sum((across > slots // 2).astype(jnp.int32), axis=1, keepdims=True)[0:1]
-    row_ref[tiles : tiles + 1, :] = jnp.where(lane[0:1] == total, large, ranked)
+    for n in range(1, SIZES):
+        over = jnp.sum((across > slots >> n).astype(jnp.int32), axis=1, keepdims=True)[0:1]
+        ranked = jnp.where(lane[0:1] == total + n - 1, over, ranked)
+    row_ref[tiles : tiles + 1, :] = ranked
 
 
 def splat_kernel(
@@ -216,14 +219,19 @@
     def live_of(t):
         return live_ref[t]
 
+    sizes = [slots >> n for n in range(SIZES)]
+
     def in_turn(body):
         def trip(s, _, positions):
             body([row_ref[tiles * slots + s * BATCH + g] for g in range(BATCH)], positions)
             return 0
 
-        large = lax.div(row_ref[tiles * slots + tiles] + (BATCH - 1), BATCH)
-        lax.fori_loop(0, large, partial(trip, positions=slots), 0)
-        lax.fori_loop(large, tiles // BATCH, partial(trip, positions=slots // 2), 0)
+        start = 0
+        for n, positions in enumerate(sizes):
+            over = row_ref[tiles * slots + tiles + n] if n + 1 < len(sizes) else tiles
+            end = lax.div(over + (BATCH - 1), BATCH)
+            lax.fori_loop(start, end, partial(trip, positions=positions), 0)
+            start = end
 
     sub = lax.broadcasted_iota(jnp.int32, (GROUPS, slots), 0)
 
@@ -511,6 +519,11 @@
     return jnp.asarray(np.concatenate([group, group, group, np.zeros_like(group)]), BF16)
 
 
+def gather(array, axis, masks):
+    got = {mask: swap(array, axis, mask) for mask in sorted(masks, reverse=True)}
+    return [got[mask] for mask in masks]
+
+
 def swap(array, axis, mask):
     size = lax.axis_size(axis)
     return lax.ppermute(array, axis, [(i, i ^ mask) for i in range(size)])
@@ -587,16 +600,16 @@
     fields = jnp.concatenate([centres, shape_raw, opacity_logit[None], colours], axis=0)
     block = fields.reshape(FIELDS * GROUPS, lanes)
     note = jnp.pad(totals.astype(F32)[None], ((0, 7), (0, lanes - views)))
-    column = jnp.concatenate([block] + [swap(block, "view", m) for m in range(1, view_group)] + [note])
+    column = jnp.concatenate([block] + gather(block, "view", range(1, view_group)) + [note])
     message = swap(message, "tile", mirror)
+    column, me = lax.optimization_barrier((column, me))
+    mine = jnp.stack([column] + gather(column, "tile", range(2, tile_group, 2)))
     own_rows, own_group, cam = prep_own(me[None], live_count, camera, intersection_ids, depth_order)
-    column, own_rows, own_group, cam = lax.optimization_barrier((column, own_rows, own_group, cam))
-    mine = jnp.stack([column] + [swap(column, "tile", 2 * m) for m in range(1, chips)])
     their_live = message[5 * part_tiles : 5 * part_tiles + views, :kept].astype(jnp.int32)
     live_now = jnp.concatenate([live_count[:, :kept].reshape(-1), their_live.reshape(-1)])
     their_rows, their_group = prep_their(me[None], live_now, message)
     rows = jnp.concatenate([own_rows, their_rows]).reshape(-1)
-    mine, rows, their_group = lax.optimization_barrier((mine, rows, their_group))
+    mine, rows, own_group, their_group, cam = lax.optimization_barrier((mine, rows, own_group, their_group, cam))
     other = swap(mine, "tile", 1)
 
     table_rows = devices * lanes
@@ -660,9 +673,9 @@
     rendered = jnp.concatenate([image, swap(their_image, "tile", mirror)], axis=2)
     joined = (grad_mine + grad_other).reshape(chips, view_group, FIELDS * GROUPS, lanes)
     part = joined[0]
-    for m in range(1, chips):
+    for m in reversed(range(1, chips)):
         part = part + swap(joined[m], "tile", 2 * m)
-    parts = [part[0]] + [swap(part[m], "view", m) for m in range(1, view_group)]
+    parts = [part[0]] + [swap(part[m], "view", m) for m in reversed(range(1, view_group))]
     tail = pl.pallas_call(
         tail_kernel,
         out_shape=[jax.ShapeDtypeStruct((count, own_count), F32) for count in (3, 6, 1, 3)],

time: 89.3 us -> 82.9 us (0.928)
  Pallas kernels: 38.9 us -> 35.2 us
  waiting for transfers between devices: 24 us -> 20.5 us
  starting transfers between devices: 18.7 us -> 20.6 us
    ppermute x16, waiting for transfers between devices: 24 us -> 20.5 us  [swap(): return lax.ppermute(array, axis, [(i, i ^ mask) for i in range(size)])]
    pallas_call x1, Pallas kernels: 32.9 us -> 29.8 us  [shards(): splat(cam, rows, live_now, own_group, their_group, mine, other, target, m...]
    ppermute x16, starting transfers between devices: 18.7 us -> 20.6 us  [swap(): return lax.ppermute(array, axis, [(i, i ^ mask) for i in range(size)])]
  transfers between devices with their start and end apart: 16 -> 16, of which waited for: 8 -> 10; matrix products, arithmetic and copies ran while one was open for 4% -> 4% of each run, Pallas kernels for 6% -> 6%
where the time goes in v4:
time: 82.9 us
  Pallas kernels  35.2 us (42%)
  starting transfers between devices  20.6 us (25%)
  waiting for transfers between devices  20.5 us (25%)
  other arithmetic  4.17 us (5%)
  local copies, waits for them, and re-layouts  1.68 us (2%)
    pallas_call x1, Pallas kernels, shards(): splat(cam, rows, live_now, own_group, their_group, mine, other, target, m...  29.8 us
    ppermute x16, starting transfers between devices, swap(): return lax.ppermute(array, axis, [(i, i ^ mask) for i in range(size)])  20.6 us
    ppermute x16, waiting for transfers between devices, swap(): return lax.ppermute(array, axis, [(i, i ^ mask) for i in range(size)])  20.5 us
    pallas_call x1, Pallas kernels, shards(): prep_own(me[None], live_count, camera, intersection_ids, depth_order)  2.5 us
    pallas_call x1, Pallas kernels, shards(): their_rows, their_group = prep_their(me[None], live_now, message)  2.29 us
  transfers between devices with their start and end apart: 16, of which 10 were waited for; matrix products, arithmetic and copies ran while one was open for 4% of the time, Pallas kernels for 6%

profile of v4, /device:TPU:0, one launch (start us, length us, event | category | flops | bytes accessed | tf_op | source)
XLA Modules:
  0.0 82.9 jit_solution(9190906683154718721)
XLA Ops:
  0.6 0.8 %pad_maximum_fusion.1 = f32[13,1024]{1,0:T(8,128)S(1)} fusion(f32[3,1024]{1,0:T(4,128)} %param.13, f32[1,1024]{1,0:T(1,128)} %bitcast.94, f32[6,1024]{1,0:T(8,128)} %param.11, f32[3,1024]{1,0:T(4,128)} %param.10), kind=kLoop, calls=%fused_computation.7 | loop fusion | flops 39936 | bytes 106496 | tf_op jit(solution)/shard_map/concatenate | solution.py:600
  1.5 3.1 %collective-permute-start = (f32[104,128]{1,0:T(8,128)S(1)}, f32[104,128]{1,0:T(8,128)S(1)}, u32[]{:S(2)}, u32[]{:S(2)}) collective-permute-start(f32[104,128]{1,0:T(8,128)S(1)} %reshape.158), channel_id=1, source_target_pairs={{0,8},{8,0},{16,24},{24,16},{1,9},{9,1},{17,25},{25,17},{2,10},{10... | collective-permute-start | bytes 159752 | tf_op jit(solution)/shard_map/ppermute | solution.py:529
  4.6 2.6 %collective-permute-start.1 = (f32[104,128]{1,0:T(8,128)S(1)}, f32[104,128]{1,0:T(8,128)S(1)}, u32[]{:S(2)}, u32[]{:S(2)}) collective-permute-start(f32[104,128]{1,0:T(8,128)S(1)} %reshape.158), channel_id=1, source_target_pairs={{0,16},{8,24},{16,0},{24,8},{1,17},{9,25},{17,1},{25,9},{2,18},{10... | collective-permute-start | bytes 159752 | tf_op jit(solution)/shard_map/ppermute | solution.py:529
  7.2 0.0 collective-permute-start.2
  7.2 0.0 copy-start.4
  7.3 0.6 copy-done.1
  7.9 0.1 fusion.19
  8.0 0.0 copy-done.3
  8.0 0.0 copy-done.4
  8.0 1.4 %collective-permute-start.6 = (f32[88,256]{1,0:T(8,128)S(1)}, f32[88,256]{1,0:T(8,128)S(1)}, u32[]{:S(2)}, u32[]{:S(2)}) collective-permute-start(f32[88,256]{1,0:T(8,128)S(1)} %select_maximum_fusion), channel_id=1, source_target_pairs={{0,7},{1,6},{2,5},{3,4},{4,3},{5,2},{6,1},{7,0},{8,15},{9,14},{10,... | collective-permute-start | bytes 270344 | tf_op jit(solution)/shard_map/ppermute | solution.py:529
  9.4 0.1 reduce_sum.9
  9.6 0.0 copy-start.5
  9.6 0.1 reshape.159
  9.7 0.6 copy-done.5
  10.3 0.1 copy.16.camera_ref
  10.3 0.0 collective-permute-done
  10.4 0.3 collective-permute-done.1
  10.7 2.5 %collective-permute-done.2 = f32[104,128]{1,0:T(8,128)S(1)} collective-permute-done((f32[104,128]{1,0:T(8,128)S(1)}, f32[104,128]{1,0:T(8,128)S(1)}, u32[]{:S(2)}, u32[]{:S(2)}) %collective-permute-start.2) | collective-permute-done | bytes 53280 | tf_op jit(solution)/shard_map/ppermute | solution.py:529
  13.2 1.6 %collective-permute-start.3 = (f32[424,128]{1,0:T(8,128)S(1)}, f32[424,128]{1,0:T(8,128)S(1)}, u32[]{:S(2)}, u32[]{:S(2)}) collective-permute-start(f32[424,128]{1,0:T(8,128)S(1)} %constant_dynamic-update-slice_fusion), channel_id=1, source_target_pairs={{0,2},{1,3},{2,0},{3,1},{4,6},{5,7},{6,4},{7,5},{8,10},{9,11},{10,... | collective-permute-start | bytes 651272 | tf_op jit(solution)/shard_map/ppermute | solution.py:529
  14.7 1.5 %collective-permute-start.4 = (f32[424,128]{1,0:T(8,128)S(1)}, f32[424,128]{1,0:T(8,128)S(1)}, u32[]{:S(2)}, u32[]{:S(2)}) collective-permute-start(f32[424,128]{1,0:T(8,128)S(1)} %constant_dynamic-update-slice_fusion), channel_id=1, source_target_pairs={{0,4},{1,5},{2,6},{3,7},{4,0},{5,1},{6,2},{7,3},{8,12},{9,13},{10,... | collective-permute-start | bytes 651272 | tf_op jit(solution)/shard_map/ppermute | solution.py:529
  16.2 0.5 collective-permute-start.5
  16.7 2.5 %prep_own.1 = (s32[16,256]{1,0:T(8,128)S(1)}, s32[16,256]{1,0:T(8,128)S(1)}, f32[16]{0:T(128)S(1)}) custom-call(s32[1]{0:T(128)} %bitcast.6.me_ref, s32[2,16]{1,0:T(2,128)S(1)} %copy-done.1, f32[8,2,4]{2,1,0:T(2,128)S(1)} %copy.16.camera_ref, s32[2,16,256]{2,1,0:T(8,128)S(1)} %copy-done.3, s32[2,16,256]{2,1,0:T(8,128)S(1)} %copy-done.4), custom_call_target="tpu_custom_call" | custom-call | flops 4000000000 | bytes 65536 | tf_op jit(solution)/shard_map/prep_own/pallas_call | solution.py:607
  19.3 0.1 reshape.161
  19.3 0.1 pad_add_fusion.live_ref
  19.4 2.3 %prep_their.1 = (s32[24,256]{1,0:T(8,128)S(1)}, s32[16,256]{1,0:T(8,128)S(1)}) custom-call(s32[1]{0:T(128)} %bitcast.6.me_ref, s32[32]{0:T(128)S(1)} %pad_add_fusion.live_ref, f32[88,256]{1,0:T(8,128)S(1)} %collective-permute-done.6.message_ref), custom_call_target="tpu_custom_call" | custom-call | flops 4000000000 | bytes 65536 | tf_op jit(solution)/shard_map/prep_their/pallas_call | solution.py:610
  21.8 0.0 collective-permute-done.3
  21.8 2.9 %collective-permute-done.4 = f32[424,128]{1,0:T(8,128)S(1)} collective-permute-done((f32[424,128]{1,0:T(8,128)S(1)}, f32[424,128]{1,0:T(8,128)S(1)}, u32[]{:S(2)}, u32[]{:S(2)}) %collective-permute-start.4) | collective-permute-done | bytes 217120 | tf_op jit(solution)/shard_map/ppermute | solution.py:529
  24.7 0.1 pad_maximum_fusion.mine_ref
  24.8 0.1 collective-permute-start.7
  24.8 2.4 %collective-permute-done.7.other_ref = f32[4,424,128]{2,1,0:T(8,128)S(1)} collective-permute-done((f32[4,424,128]{2,1,0:T(8,128)S(1)}, f32[4,424,128]{2,1,0:T(8,128)S(1)}, u32[]{:S(2)}, u32[]{:S(2)}) %collective-permute-start.7) | collective-permute-done | bytes 868384 | tf_op jit(solution)/shard_map/ppermute | solution.py:529
  27.2 29.8 %splat.1 = (f32[2,3,8,256]{3,2,1,0:T(8,128)S(1)}, f32[2,3,8,256]{3,2,1,0:T(8,128)S(1)}, f32[16,104,128]{2,1,0:T(8,128)S(1)}, f32[16,104,128]{2,1,0:T(8,128)}) custom-call(f32[16]{0:T(128)S(1)} %get-tuple-element.33.cam_ref, s32[10240]{0:T(1024)S(1)} %bitcast.88, s32[32]{0:T(128)S(1)} %pad_add_fusion.live_ref, s32[16,256]{1,0:T(8,128)S(1)} %get-tuple-element.35.own_group_ref, ...), custom_call_target="tpu_custom_call" | custom-call | tf_op jit(solution)/shard_map/splat/pallas_call | solution.py:648
  57.0 0.2 reduce_window_sum.11
  57.2 1.8 %collective-permute-start.8 = (f32[2,3,8,256]{3,2,1,0:T(8,128)S(1)}, f32[2,3,8,256]{3,2,1,0:T(8,128)S(1)}, u32[]{:S(2)}, u32[]{:S(2)}) collective-permute-start(f32[2,3,8,256]{3,2,1,0:T(8,128)S(1)} %get-tuple-element.39), channel_id=1, source_target_pairs={{0,7},{1,6},{2,5},{3,4},{4,3},{5,2},{6,1},{7,0},{8,15},{9,14},{10,... | collective-permute-start | bytes 147464 | tf_op jit(solution)/shard_map/ppermute | solution.py:529
  59.0 0.7 collective-permute-done.9
  59.7 1.2 %add.141 = f32[16,104,128]{2,1,0:T(8,128)S(1)} add(f32[16,104,128]{2,1,0:T(8,128)S(1)} %get-tuple-element.40, f32[16,104,128]{2,1,0:T(8,128)} %collective-permute-done.9) | non-fusion elementwise | flops 212992 | bytes 2555904 | tf_op jit(solution)/shard_map/add | solution.py:674
  61.0 1.8 %collective-permute-start.10 = (f32[4,104,128]{2,1,0:T(8,128)S(1)}, f32[4,104,128]{2,1,0:T(8,128)S(1)}, u32[]{:S(2)}, u32[]{:S(2)}) collective-permute-start(f32[4,104,128]{2,1,0:T(8,128)S(1)} %get-tuple-element.48), channel_id=1, source_target_pairs={{0,6},{1,7},{2,4},{3,5},{4,2},{5,3},{6,0},{7,1},{8,14},{9,15},{10,... | collective-permute-start | bytes 638984 | tf_op jit(solution)/shard_map/ppermute | solution.py:529
  62.8 1.8 %collective-permute-start.12 = (f32[4,104,128]{2,1,0:T(8,128)S(1)}, f32[4,104,128]{2,1,0:T(8,128)S(1)}, u32[]{:S(2)}, u32[]{:S(2)}) collective-permute-start(f32[4,104,128]{2,1,0:T(8,128)S(1)} %get-tuple-element.49), channel_id=1, source_target_pairs={{0,2},{1,3},{2,0},{3,1},{4,6},{5,7},{6,4},{7,5},{8,10},{9,11},{10,... | collective-permute-start | bytes 638984 | tf_op jit(solution)/shard_map/ppermute | solution.py:529
  64.6 0.8 and_select_fusion
  65.3 4.8 %collective-permute-done.10 = f32[4,104,128]{2,1,0:T(8,128)S(1)} collective-permute-done((f32[4,104,128]{2,1,0:T(8,128)S(1)}, f32[4,104,128]{2,1,0:T(8,128)S(1)}, u32[]{:S(2)}, u32[]{:S(2)}) %collective-permute-start.10) | collective-permute-done | bytes 213024 | tf_op jit(solution)/shard_map/ppermute | solution.py:529
  70.1 3.7 %collective-permute-done.11 = f32[4,104,128]{2,1,0:T(8,128)S(1)} collective-permute-done((f32[4,104,128]{2,1,0:T(8,128)S(1)}, f32[4,104,128]{2,1,0:T(8,128)S(1)}, u32[]{:S(2)}, u32[]{:S(2)}) %collective-permute-start.11) | collective-permute-done | bytes 213024 | tf_op jit(solution)/shard_map/ppermute | solution.py:529
  73.8 0.1 fusion.1
  73.9 3.1 %collective-permute-start.13 = (f32[104,128]{1,0:T(8,128)S(1)}, f32[104,128]{1,0:T(8,128)S(1)}, u32[]{:S(2)}, u32[]{:S(2)}) collective-permute-start(f32[104,128]{1,0:T(8,128)S(1)} %get-tuple-element.53), channel_id=1, source_target_pairs={{0,24},{8,16},{16,8},{24,0},{1,25},{9,17},{17,9},{25,1},{2,26},{10... | collective-permute-start | bytes 159752 | tf_op jit(solution)/shard_map/ppermute | solution.py:529
  77.0 1.3 %collective-permute-start.15 = (f32[104,128]{1,0:T(8,128)S(1)}, f32[104,128]{1,0:T(8,128)S(1)}, u32[]{:S(2)}, u32[]{:S(2)}) collective-permute-start(f32[104,128]{1,0:T(8,128)S(1)} %get-tuple-element.51), channel_id=1, source_target_pairs={{0,8},{8,0},{16,24},{24,16},{1,9},{9,1},{17,25},{25,17},{2,10},{10... | collective-permute-start | bytes 159752 | tf_op jit(solution)/shard_map/ppermute | solution.py:529
  78.4 0.7 maximum_bitcast_fusion
  79.0 1.1 %collective-permute-done.13.refs_1_ = f32[104,128]{1,0:T(8,128)S(1)} collective-permute-done((f32[104,128]{1,0:T(8,128)S(1)}, f32[104,128]{1,0:T(8,128)S(1)}, u32[]{:S(2)}, u32[]{:S(2)}) %collective-permute-start.13) | collective-permute-done | bytes 53280 | tf_op jit(solution)/shard_map/ppermute | solution.py:529
  80.2 1.9 %collective-permute-done.14.refs_2_ = f32[104,128]{1,0:T(8,128)S(1)} collective-permute-done((f32[104,128]{1,0:T(8,128)S(1)}, f32[104,128]{1,0:T(8,128)S(1)}, u32[]{:S(2)}, u32[]{:S(2)}) %collective-permute-start.14) | collective-permute-done | bytes 53280 | tf_op jit(solution)/shard_map/ppermute | solution.py:529
  82.1 0.1 collective-permute-done.15.refs_3_
  82.2 0.7 tail.1
  (30 shorter events, 0.2 us)
Async XLA Ops:
  0.6 6.6 %copy-start = (f32[2,16,3,256]{3,1,2,0:T(8,128)S(1)}, f32[2,16,3,256]{3,1,2,0:T(8,128)}, u32[]{:S(2)}) copy-start(f32[2,16,3,256]{3,1,2,0:T(8,128)} %param.15) | copy-start | bytes 294916
  1.5 8.8 %collective-permute-start = (f32[104,128]{1,0:T(8,128)S(1)}, f32[104,128]{1,0:T(8,128)S(1)}, u32[]{:S(2)}, u32[]{:S(2)}) collective-permute-start(f32[104,128]{1,0:T(8,128)S(1)} %reshape.158), channel_id=1, source_target_pairs={{0,8},{8,0},{16,24},{24,16},{1,9},{9,1},{17,25},{25,17},{2,10},{10... | collective-permute-start | bytes 159752 | tf_op jit(solution)/shard_map/ppermute | solution.py:529
  4.6 6.1 %collective-permute-start.1 = (f32[104,128]{1,0:T(8,128)S(1)}, f32[104,128]{1,0:T(8,128)S(1)}, u32[]{:S(2)}, u32[]{:S(2)}) collective-permute-start(f32[104,128]{1,0:T(8,128)S(1)} %reshape.158), channel_id=1, source_target_pairs={{0,16},{8,24},{16,0},{24,8},{1,17},{9,25},{17,1},{25,9},{2,18},{10... | collective-permute-start | bytes 159752 | tf_op jit(solution)/shard_map/ppermute | solution.py:529
  7.2 5.9 %collective-permute-start.2 = (f32[104,128]{1,0:T(8,128)S(1)}, f32[104,128]{1,0:T(8,128)S(1)}, u32[]{:S(2)}, u32[]{:S(2)}) collective-permute-start(f32[104,128]{1,0:T(8,128)S(1)} %reshape.158), channel_id=1, source_target_pairs={{0,24},{8,16},{16,8},{24,0},{1,25},{9,17},{17,9},{25,1},{2,26},{10... | collective-permute-start | bytes 159752 | tf_op jit(solution)/shard_map/ppermute | solution.py:529
  7.2 0.7 copy-start.1
  7.2 0.8 copy-start.3
  7.2 0.8 copy-start.4
  8.0 11.2 %collective-permute-start.6 = (f32[88,256]{1,0:T(8,128)S(1)}, f32[88,256]{1,0:T(8,128)S(1)}, u32[]{:S(2)}, u32[]{:S(2)}) collective-permute-start(f32[88,256]{1,0:T(8,128)S(1)} %select_maximum_fusion), channel_id=1, source_target_pairs={{0,7},{1,6},{2,5},{3,4},{4,3},{5,2},{6,1},{7,0},{8,15},{9,14},{10,... | collective-permute-start | bytes 270344 | tf_op jit(solution)/shard_map/ppermute | solution.py:529
  9.6 0.7 copy-start.5
  13.2 8.6 %collective-permute-start.3 = (f32[424,128]{1,0:T(8,128)S(1)}, f32[424,128]{1,0:T(8,128)S(1)}, u32[]{:S(2)}, u32[]{:S(2)}) collective-permute-start(f32[424,128]{1,0:T(8,128)S(1)} %constant_dynamic-update-slice_fusion), channel_id=1, source_target_pairs={{0,2},{1,3},{2,0},{3,1},{4,6},{5,7},{6,4},{7,5},{8,10},{9,11},{10,... | collective-permute-start | bytes 651272 | tf_op jit(solution)/shard_map/ppermute | solution.py:529
  14.7 9.9 %collective-permute-start.4 = (f32[424,128]{1,0:T(8,128)S(1)}, f32[424,128]{1,0:T(8,128)S(1)}, u32[]{:S(2)}, u32[]{:S(2)}) collective-permute-start(f32[424,128]{1,0:T(8,128)S(1)} %constant_dynamic-update-slice_fusion), channel_id=1, source_target_pairs={{0,4},{1,5},{2,6},{3,7},{4,0},{5,1},{6,2},{7,3},{8,12},{9,13},{10,... | collective-permute-start | bytes 651272 | tf_op jit(solution)/shard_map/ppermute | solution.py:529
  16.2 8.4 %collective-permute-start.5 = (f32[424,128]{1,0:T(8,128)S(1)}, f32[424,128]{1,0:T(8,128)S(1)}, u32[]{:S(2)}, u32[]{:S(2)}) collective-permute-start(f32[424,128]{1,0:T(8,128)S(1)} %constant_dynamic-update-slice_fusion), channel_id=1, source_target_pairs={{0,6},{1,7},{2,4},{3,5},{4,2},{5,3},{6,0},{7,1},{8,14},{9,15},{10,... | collective-permute-start | bytes 651272 | tf_op jit(solution)/shard_map/ppermute | solution.py:529
  24.7 2.6 %copy-start.2 = (bf16[32,256]{1,0:T(8,128)(2,1)S(1)}, bf16[32,256]{1,0:T(8,128)(2,1)}, u32[]{:S(2)}) copy-start(bf16[32,256]{1,0:T(8,128)(2,1)} %constant.40.clone.mono_ref) | copy-start | bytes 49156
  24.8 2.5 %collective-permute-start.7 = (f32[4,424,128]{2,1,0:T(8,128)S(1)}, f32[4,424,128]{2,1,0:T(8,128)S(1)}, u32[]{:S(2)}, u32[]{:S(2)}) collective-permute-start(f32[4,424,128]{2,1,0:T(8,128)S(1)} %pad_maximum_fusion.mine_ref), channel_id=1, source_target_pairs={{0,1},{1,0},{2,3},{3,2},{4,5},{5,4},{6,7},{7,6},{8,9},{9,8},{10,11... | collective-permute-start | bytes 2605064 | tf_op jit(solution)/shard_map/ppermute | solution.py:529
  57.0 2.7 %collective-permute-start.9 = (f32[16,104,128]{2,1,0:T(8,128)}, f32[16,104,128]{2,1,0:T(8,128)}, u32[]{:S(2)}, u32[]{:S(2)}) collective-permute-start(f32[16,104,128]{2,1,0:T(8,128)} %get-tuple-element.41), channel_id=1, source_target_pairs={{0,1},{1,0},{2,3},{3,2},{4,5},{5,4},{6,7},{7,6},{8,9},{9,8},{10,11... | collective-permute-start | bytes 2555912 | tf_op jit(solution)/shard_map/ppermute | solution.py:529
  57.2 21.2 %collective-permute-start.8 = (f32[2,3,8,256]{3,2,1,0:T(8,128)S(1)}, f32[2,3,8,256]{3,2,1,0:T(8,128)S(1)}, u32[]{:S(2)}, u32[]{:S(2)}) collective-permute-start(f32[2,3,8,256]{3,2,1,0:T(8,128)S(1)} %get-tuple-element.39), channel_id=1, source_target_pairs={{0,7},{1,6},{2,5},{3,4},{4,3},{5,2},{6,1},{7,0},{8,15},{9,14},{10,... | collective-permute-start | bytes 147464 | tf_op jit(solution)/shard_map/ppermute | solution.py:529
  61.0 9.1 %collective-permute-start.10 = (f32[4,104,128]{2,1,0:T(8,128)S(1)}, f32[4,104,128]{2,1,0:T(8,128)S(1)}, u32[]{:S(2)}, u32[]{:S(2)}) collective-permute-start(f32[4,104,128]{2,1,0:T(8,128)S(1)} %get-tuple-element.48), channel_id=1, source_target_pairs={{0,6},{1,7},{2,4},{3,5},{4,2},{5,3},{6,0},{7,1},{8,14},{9,15},{10,... | collective-permute-start | bytes 638984 | tf_op jit(solution)/shard_map/ppermute | solution.py:529
  62.8 11.0 %collective-permute-start.11 = (f32[4,104,128]{2,1,0:T(8,128)S(1)}, f32[4,104,128]{2,1,0:T(8,128)S(1)}, u32[]{:S(2)}, u32[]{:S(2)}) collective-permute-start(f32[4,104,128]{2,1,0:T(8,128)S(1)} %get-tuple-element.50), channel_id=1, source_target_pairs={{0,4},{1,5},{2,6},{3,7},{4,0},{5,1},{6,2},{7,3},{8,12},{9,13},{10,... | collective-permute-start | bytes 638984 | tf_op jit(solution)/shard_map/ppermute | solution.py:529
  62.8 11.0 %collective-permute-start.12 = (f32[4,104,128]{2,1,0:T(8,128)S(1)}, f32[4,104,128]{2,1,0:T(8,128)S(1)}, u32[]{:S(2)}, u32[]{:S(2)}) collective-permute-start(f32[4,104,128]{2,1,0:T(8,128)S(1)} %get-tuple-element.49), channel_id=1, source_target_pairs={{0,2},{1,3},{2,0},{3,1},{4,6},{5,7},{6,4},{7,5},{8,10},{9,11},{10,... | collective-permute-start | bytes 638984 | tf_op jit(solution)/shard_map/ppermute | solution.py:529
  73.9 6.2 %collective-permute-start.13 = (f32[104,128]{1,0:T(8,128)S(1)}, f32[104,128]{1,0:T(8,128)S(1)}, u32[]{:S(2)}, u32[]{:S(2)}) collective-permute-start(f32[104,128]{1,0:T(8,128)S(1)} %get-tuple-element.53), channel_id=1, source_target_pairs={{0,24},{8,16},{16,8},{24,0},{1,25},{9,17},{17,9},{25,1},{2,26},{10... | collective-permute-start | bytes 159752 | tf_op jit(solution)/shard_map/ppermute | solution.py:529
  77.0 5.0 %collective-permute-start.14 = (f32[104,128]{1,0:T(8,128)S(1)}, f32[104,128]{1,0:T(8,128)S(1)}, u32[]{:S(2)}, u32[]{:S(2)}) collective-permute-start(f32[104,128]{1,0:T(8,128)S(1)} %get-tuple-element.52), channel_id=1, source_target_pairs={{0,16},{8,24},{16,0},{24,8},{1,17},{9,25},{17,1},{25,9},{2,18},{10... | collective-permute-start | bytes 159752 | tf_op jit(solution)/shard_map/ppermute | solution.py:529
  77.0 5.2 %collective-permute-start.15 = (f32[104,128]{1,0:T(8,128)S(1)}, f32[104,128]{1,0:T(8,128)S(1)}, u32[]{:S(2)}, u32[]{:S(2)}) collective-permute-start(f32[104,128]{1,0:T(8,128)S(1)} %get-tuple-element.51), channel_id=1, source_target_pairs={{0,8},{8,0},{16,24},{24,16},{1,9},{9,1},{17,25},{25,17},{2,10},{10... | collective-permute-start | bytes 159752 | tf_op jit(solution)/shard_map/ppermute | solution.py:529

commit v5 on v4

--- a/solution.py
+++ b/solution.py
@@ -56,19 +56,12 @@
 
 
 def repeat(count, step, body):
-    many = lax.div(count, step)
-
     def trip(i, _):
         for u in range(step):
             body(i * step + u)
         return 0
 
-    def single(i, _):
-        body(i)
-        return 0
-
-    lax.fori_loop(0, many, trip, 0)
-    lax.fori_loop(many * step, count, single, 0)
+    lax.fori_loop(0, lax.div(count + (step - 1), step), trip, 0)
 
 
 def place_slots(dims, me, live_at, ids, order, scratch):
@@ -480,16 +473,17 @@
 
     in_turn(give)
 
-    def finish(d, _):
+    def finish(q, _):
         for base, ref in ((0, grad_mine_ref), (half, grad_other_ref)):
-            start = pl.multiple_of((base + d) * lanes, lanes)
-            total = accs[0][pl.ds(start, lanes), :]
-            for acc in accs[1:]:
-                total = total + acc[pl.ds(start, lanes), :]
-            ref[d] = jnp.transpose(total)[0:used]
+            for d in range(column):
+                start = pl.multiple_of((base + q * column + d) * lanes, lanes)
+                total = accs[0][pl.ds(start, lanes), :]
+                for acc in accs[1:]:
+                    total = total + acc[pl.ds(start, lanes), :]
+                ref[q * column + d] = jnp.transpose(total)[0:used]
         return 0
 
-    lax.fori_loop(0, half, finish, 0)
+    lax.fori_loop(0, chips, finish, 0)
 
 
 def tail_kernel(*refs):
@@ -670,11 +664,13 @@
     next_owner = (before[:, None] + within) * tile_group // whole[:, None]
 
     grad_other = swap(grad_other, "tile", 1)
-    rendered = jnp.concatenate([image, swap(their_image, "tile", mirror)], axis=2)
-    joined = (grad_mine + grad_other).reshape(chips, view_group, FIELDS * GROUPS, lanes)
+    joined = grad_mine + grad_other
+    joined, their_image = lax.optimization_barrier((joined, their_image))
+    joined = joined.reshape(chips, view_group, FIELDS * GROUPS, lanes)
     part = joined[0]
     for m in reversed(range(1, chips)):
         part = part + swap(joined[m], "tile", 2 * m)
+    rendered = jnp.concatenate([image, swap(their_image, "tile", mirror)], axis=2)
     parts = [part[0]] + [swap(part[m], "view", m) for m in reversed(range(1, view_group))]
     tail = pl.pallas_call(
         tail_kernel,

time: 82.9 us -> 82.5 us (level)
  waiting for transfers between devices: 20.5 us -> 22.6 us
  Pallas kernels: 35.2 us -> 33.2 us
    ppermute x16, waiting for transfers between devices: 20.5 us -> 22.6 us  [swap(): return lax.ppermute(array, axis, [(i, i ^ mask) for i in range(size)])]
    pallas_call x1, Pallas kernels: 29.8 us -> 27.8 us  [shards(): splat(cam, rows, live_now, own_group, their_group, mine, other, target, m...]
  transfers between devices with their start and end apart: 16 -> 16, of which waited for: 10 -> 11; matrix products, arithmetic and copies ran while one was open for 4% -> 3% of each run, Pallas kernels for 6% -> 6%
where the time goes in v5:
time: 82.5 us; the launch traced here: 82.8 us
  Pallas kernels  33.2 us (40%)
  waiting for transfers between devices  22.6 us (27%)
  starting transfers between devices  20.4 us (25%)
  other arithmetic  4.16 us (5%)
  local copies, waits for them, and re-layouts  1.68 us (2%)
    pallas_call x1, Pallas kernels, shards(): splat(cam, rows, live_now, own_group, their_group, mine, other, target, m...  27.8 us
    ppermute x16, waiting for transfers between devices, swap(): return lax.ppermute(array, axis, [(i, i ^ mask) for i in range(size)])  22.6 us
    ppermute x16, starting transfers between devices, swap(): return lax.ppermute(array, axis, [(i, i ^ mask) for i in range(size)])  20.4 us
    pallas_call x1, Pallas kernels, shards(): prep_own(me[None], live_count, camera, intersection_ids, depth_order)  2.5 us
    pallas_call x1, Pallas kernels, shards(): their_rows, their_group = prep_their(me[None], live_now, message)  2.29 us
  transfers between devices with their start and end apart: 16, of which 11 were waited for; matrix products, arithmetic and copies ran while one was open for 3% of the time, Pallas kernels for 6%

profile of v5, /device:TPU:0, one launch (start us, length us, event | category | flops | bytes accessed | tf_op | source)
XLA Modules:
  0.0 82.8 jit_solution(13820931205601660881)
XLA Ops:
  0.6 0.8 %pad_maximum_fusion.1 = f32[13,1024]{1,0:T(8,128)S(1)} fusion(f32[3,1024]{1,0:T(4,128)} %param.13, f32[1,1024]{1,0:T(1,128)} %bitcast.94, f32[6,1024]{1,0:T(8,128)} %param.11, f32[3,1024]{1,0:T(4,128)} %param.10), kind=kLoop, calls=%fused_computation.5 | loop fusion | flops 39936 | bytes 106496 | tf_op jit(solution)/shard_map/concatenate | solution.py:594
  1.5 3.1 %collective-permute-start = (f32[104,128]{1,0:T(8,128)S(1)}, f32[104,128]{1,0:T(8,128)S(1)}, u32[]{:S(2)}, u32[]{:S(2)}) collective-permute-start(f32[104,128]{1,0:T(8,128)S(1)} %reshape.158), channel_id=1, source_target_pairs={{0,8},{8,0},{16,24},{24,16},{1,9},{9,1},{17,25},{25,17},{2,10},{10... | collective-permute-start | bytes 159752 | tf_op jit(solution)/shard_map/ppermute | solution.py:523
  4.6 2.6 %collective-permute-start.1 = (f32[104,128]{1,0:T(8,128)S(1)}, f32[104,128]{1,0:T(8,128)S(1)}, u32[]{:S(2)}, u32[]{:S(2)}) collective-permute-start(f32[104,128]{1,0:T(8,128)S(1)} %reshape.158), channel_id=1, source_target_pairs={{0,16},{8,24},{16,0},{24,8},{1,17},{9,25},{17,1},{25,9},{2,18},{10... | collective-permute-start | bytes 159752 | tf_op jit(solution)/shard_map/ppermute | solution.py:523
  7.2 0.0 copy-start.4
  7.3 0.6 copy-done.1
  7.9 0.1 fusion.17
  8.0 0.0 copy-done.3
  8.0 0.0 copy-done.4
  8.0 1.4 %collective-permute-start.6 = (f32[88,256]{1,0:T(8,128)S(1)}, f32[88,256]{1,0:T(8,128)S(1)}, u32[]{:S(2)}, u32[]{:S(2)}) collective-permute-start(f32[88,256]{1,0:T(8,128)S(1)} %select_maximum_fusion), channel_id=1, source_target_pairs={{0,7},{1,6},{2,5},{3,4},{4,3},{5,2},{6,1},{7,0},{8,15},{9,14},{10,... | collective-permute-start | bytes 270344 | tf_op jit(solution)/shard_map/ppermute | solution.py:523
  9.4 0.1 reduce_sum.9
  9.6 0.0 copy-start.5
  9.6 0.1 reshape.159
  9.7 0.6 copy-done.5
  10.3 0.1 copy.16.camera_ref
  10.3 0.0 collective-permute-done
  10.4 0.3 collective-permute-done.1
  10.7 2.5 %collective-permute-done.2 = f32[104,128]{1,0:T(8,128)S(1)} collective-permute-done((f32[104,128]{1,0:T(8,128)S(1)}, f32[104,128]{1,0:T(8,128)S(1)}, u32[]{:S(2)}, u32[]{:S(2)}) %collective-permute-start.2) | collective-permute-done | bytes 53280 | tf_op jit(solution)/shard_map/ppermute | solution.py:523
  13.2 1.6 %collective-permute-start.3 = (f32[424,128]{1,0:T(8,128)S(1)}, f32[424,128]{1,0:T(8,128)S(1)}, u32[]{:S(2)}, u32[]{:S(2)}) collective-permute-start(f32[424,128]{1,0:T(8,128)S(1)} %constant_dynamic-update-slice_fusion), channel_id=1, source_target_pairs={{0,2},{1,3},{2,0},{3,1},{4,6},{5,7},{6,4},{7,5},{8,10},{9,11},{10,... | collective-permute-start | bytes 651272 | tf_op jit(solution)/shard_map/ppermute | solution.py:523
  14.7 1.5 %collective-permute-start.4 = (f32[424,128]{1,0:T(8,128)S(1)}, f32[424,128]{1,0:T(8,128)S(1)}, u32[]{:S(2)}, u32[]{:S(2)}) collective-permute-start(f32[424,128]{1,0:T(8,128)S(1)} %constant_dynamic-update-slice_fusion), channel_id=1, source_target_pairs={{0,4},{1,5},{2,6},{3,7},{4,0},{5,1},{6,2},{7,3},{8,12},{9,13},{10,... | collective-permute-start | bytes 651272 | tf_op jit(solution)/shard_map/ppermute | solution.py:523
  16.2 0.5 collective-permute-start.5
  16.7 2.5 %prep_own.1 = (s32[16,256]{1,0:T(8,128)S(1)}, s32[16,256]{1,0:T(8,128)S(1)}, f32[16]{0:T(128)S(1)}) custom-call(s32[1]{0:T(128)} %bitcast.6.me_ref, s32[2,16]{1,0:T(2,128)S(1)} %copy-done.1, f32[8,2,4]{2,1,0:T(2,128)S(1)} %copy.16.camera_ref, s32[2,16,256]{2,1,0:T(8,128)S(1)} %copy-done.3, s32[2,16,256]{2,1,0:T(8,128)S(1)} %copy-done.4), custom_call_target="tpu_custom_call" | custom-call | flops 4000000000 | bytes 65536 | tf_op jit(solution)/shard_map/prep_own/pallas_call | solution.py:601
  19.3 0.1 reshape.161
  19.3 0.1 pad_add_fusion.live_ref
  19.4 2.3 %prep_their.1 = (s32[24,256]{1,0:T(8,128)S(1)}, s32[16,256]{1,0:T(8,128)S(1)}) custom-call(s32[1]{0:T(128)} %bitcast.6.me_ref, s32[32]{0:T(128)S(1)} %pad_add_fusion.live_ref, f32[88,256]{1,0:T(8,128)S(1)} %collective-permute-done.6.message_ref), custom_call_target="tpu_custom_call" | custom-call | flops 4000000000 | bytes 65536 | tf_op jit(solution)/shard_map/prep_their/pallas_call | solution.py:604
  21.8 2.9 %collective-permute-done.4 = f32[424,128]{1,0:T(8,128)S(1)} collective-permute-done((f32[424,128]{1,0:T(8,128)S(1)}, f32[424,128]{1,0:T(8,128)S(1)}, u32[]{:S(2)}, u32[]{:S(2)}) %collective-permute-start.4) | collective-permute-done | bytes 217120 | tf_op jit(solution)/shard_map/ppermute | solution.py:523
  24.7 0.1 pad_maximum_fusion.mine_ref
  24.8 0.1 collective-permute-start.7
  24.8 2.4 %collective-permute-done.7.other_ref = f32[4,424,128]{2,1,0:T(8,128)S(1)} collective-permute-done((f32[4,424,128]{2,1,0:T(8,128)S(1)}, f32[4,424,128]{2,1,0:T(8,128)S(1)}, u32[]{:S(2)}, u32[]{:S(2)}) %collective-permute-start.7) | collective-permute-done | bytes 868384 | tf_op jit(solution)/shard_map/ppermute | solution.py:523
  27.2 27.8 %splat.1 = (f32[2,3,8,256]{3,2,1,0:T(8,128)S(1)}, f32[2,3,8,256]{3,2,1,0:T(8,128)S(1)}, f32[16,104,128]{2,1,0:T(8,128)S(1)}, f32[16,104,128]{2,1,0:T(8,128)}) custom-call(f32[16]{0:T(128)S(1)} %get-tuple-element.35.cam_ref, s32[10240]{0:T(1024)S(1)} %bitcast.88, s32[32]{0:T(128)S(1)} %pad_add_fusion.live_ref, s32[16,256]{1,0:T(8,128)S(1)} %get-tuple-element.37.own_group_ref, ...), custom_call_target="tpu_custom_call" | custom-call | tf_op jit(solution)/shard_map/splat/pallas_call | solution.py:642
  55.0 0.2 reduce_window_sum.11
  55.2 2.5 %collective-permute-done.8 = f32[16,104,128]{2,1,0:T(8,128)} collective-permute-done((f32[16,104,128]{2,1,0:T(8,128)}, f32[16,104,128]{2,1,0:T(8,128)}, u32[]{:S(2)}, u32[]{:S(2)}) %collective-permute-start.8) | collective-permute-done | bytes 852000 | tf_op jit(solution)/shard_map/ppermute | solution.py:523
  57.7 1.2 %add.141 = f32[16,104,128]{2,1,0:T(8,128)S(1)} add(f32[16,104,128]{2,1,0:T(8,128)S(1)} %get-tuple-element.41, f32[16,104,128]{2,1,0:T(8,128)} %collective-permute-done.8) | non-fusion elementwise | flops 212992 | bytes 2555904 | tf_op jit(solution)/shard_map/add | solution.py:667
  59.0 0.8 %collective-permute-start.10 = (f32[4,104,128]{2,1,0:T(8,128)S(1)}, f32[4,104,128]{2,1,0:T(8,128)S(1)}, u32[]{:S(2)}, u32[]{:S(2)}) collective-permute-start(f32[4,104,128]{2,1,0:T(8,128)S(1)} %get-tuple-element.52), channel_id=1, source_target_pairs={{0,6},{1,7},{2,4},{3,5},{4,2},{5,3},{6,0},{7,1},{8,14},{9,15},{10,... | collective-permute-start | bytes 638984 | tf_op jit(solution)/shard_map/ppermute | solution.py:523
  59.8 2.6 %collective-permute-start.11 = (f32[4,104,128]{2,1,0:T(8,128)S(1)}, f32[4,104,128]{2,1,0:T(8,128)S(1)}, u32[]{:S(2)}, u32[]{:S(2)}) collective-permute-start(f32[4,104,128]{2,1,0:T(8,128)S(1)} %get-tuple-element.54), channel_id=1, source_target_pairs={{0,4},{1,5},{2,6},{3,7},{4,0},{5,1},{6,2},{7,3},{8,12},{9,13},{10,... | collective-permute-start | bytes 638984 | tf_op jit(solution)/shard_map/ppermute | solution.py:523
  62.4 0.9 %collective-permute-start.12 = (f32[4,104,128]{2,1,0:T(8,128)S(1)}, f32[4,104,128]{2,1,0:T(8,128)S(1)}, u32[]{:S(2)}, u32[]{:S(2)}) collective-permute-start(f32[4,104,128]{2,1,0:T(8,128)S(1)} %get-tuple-element.53), channel_id=1, source_target_pairs={{0,2},{1,3},{2,0},{3,1},{4,6},{5,7},{6,4},{7,5},{8,10},{9,11},{10,... | collective-permute-start | bytes 638984 | tf_op jit(solution)/shard_map/ppermute | solution.py:523
  63.3 0.8 and_select_fusion
  64.1 0.9 %collective-permute-start.9 = (f32[2,3,8,256]{3,2,1,0:T(8,128)S(1)}, f32[2,3,8,256]{3,2,1,0:T(8,128)S(1)}, u32[]{:S(2)}, u32[]{:S(2)}) collective-permute-start(f32[2,3,8,256]{3,2,1,0:T(8,128)S(1)} %get-tuple-element.44), channel_id=1, source_target_pairs={{0,7},{1,6},{2,5},{3,4},{4,3},{5,2},{6,1},{7,0},{8,15},{9,14},{10,... | collective-permute-start | bytes 147464 | tf_op jit(solution)/shard_map/ppermute | solution.py:523
  65.0 3.2 %collective-permute-done.10 = f32[4,104,128]{2,1,0:T(8,128)S(1)} collective-permute-done((f32[4,104,128]{2,1,0:T(8,128)S(1)}, f32[4,104,128]{2,1,0:T(8,128)S(1)}, u32[]{:S(2)}, u32[]{:S(2)}) %collective-permute-start.10) | collective-permute-done | bytes 213024 | tf_op jit(solution)/shard_map/ppermute | solution.py:523
  68.1 4.2 %collective-permute-done.11 = f32[4,104,128]{2,1,0:T(8,128)S(1)} collective-permute-done((f32[4,104,128]{2,1,0:T(8,128)S(1)}, f32[4,104,128]{2,1,0:T(8,128)S(1)}, u32[]{:S(2)}, u32[]{:S(2)}) %collective-permute-start.11) | collective-permute-done | bytes 213024 | tf_op jit(solution)/shard_map/ppermute | solution.py:523
  72.4 1.6 %collective-permute-done.12 = f32[4,104,128]{2,1,0:T(8,128)S(1)} collective-permute-done((f32[4,104,128]{2,1,0:T(8,128)S(1)}, f32[4,104,128]{2,1,0:T(8,128)S(1)}, u32[]{:S(2)}, u32[]{:S(2)}) %collective-permute-start.12) | collective-permute-done | bytes 213024 | tf_op jit(solution)/shard_map/ppermute | solution.py:523
  74.0 0.1 add_add_fusion
  74.0 2.9 %collective-permute-start.13 = (f32[104,128]{1,0:T(8,128)S(1)}, f32[104,128]{1,0:T(8,128)S(1)}, u32[]{:S(2)}, u32[]{:S(2)}) collective-permute-start(f32[104,128]{1,0:T(8,128)S(1)} %get-tuple-element.57), channel_id=1, source_target_pairs={{0,24},{8,16},{16,8},{24,0},{1,25},{9,17},{17,9},{25,1},{2,26},{10... | collective-permute-start | bytes 159752 | tf_op jit(solution)/shard_map/ppermute | solution.py:523
  76.9 1.6 %collective-permute-start.15 = (f32[104,128]{1,0:T(8,128)S(1)}, f32[104,128]{1,0:T(8,128)S(1)}, u32[]{:S(2)}, u32[]{:S(2)}) collective-permute-start(f32[104,128]{1,0:T(8,128)S(1)} %get-tuple-element.55), channel_id=1, source_target_pairs={{0,8},{8,0},{16,24},{24,16},{1,9},{9,1},{17,25},{25,17},{2,10},{10... | collective-permute-start | bytes 159752 | tf_op jit(solution)/shard_map/ppermute | solution.py:523
  78.5 0.6 maximum_bitcast_fusion
  79.2 1.0 %collective-permute-done.13.refs_1_ = f32[104,128]{1,0:T(8,128)S(1)} collective-permute-done((f32[104,128]{1,0:T(8,128)S(1)}, f32[104,128]{1,0:T(8,128)S(1)}, u32[]{:S(2)}, u32[]{:S(2)}) %collective-permute-start.13) | collective-permute-done | bytes 53280 | tf_op jit(solution)/shard_map/ppermute | solution.py:523
  80.1 1.8 %collective-permute-done.14.refs_2_ = f32[104,128]{1,0:T(8,128)S(1)} collective-permute-done((f32[104,128]{1,0:T(8,128)S(1)}, f32[104,128]{1,0:T(8,128)S(1)}, u32[]{:S(2)}, u32[]{:S(2)}) %collective-permute-start.14) | collective-permute-done | bytes 53280 | tf_op jit(solution)/shard_map/ppermute | solution.py:523
  81.9 0.2 collective-permute-done.15.refs_3_
  82.1 0.7 tail.1
  (30 shorter events, 0.2 us)
Async XLA Ops:
  0.6 6.6 %copy-start = (f32[2,16,3,256]{3,1,2,0:T(8,128)S(1)}, f32[2,16,3,256]{3,1,2,0:T(8,128)}, u32[]{:S(2)}) copy-start(f32[2,16,3,256]{3,1,2,0:T(8,128)} %param.15) | copy-start | bytes 294916
  1.5 8.8 %collective-permute-start = (f32[104,128]{1,0:T(8,128)S(1)}, f32[104,128]{1,0:T(8,128)S(1)}, u32[]{:S(2)}, u32[]{:S(2)}) collective-permute-start(f32[104,128]{1,0:T(8,128)S(1)} %reshape.158), channel_id=1, source_target_pairs={{0,8},{8,0},{16,24},{24,16},{1,9},{9,1},{17,25},{25,17},{2,10},{10... | collective-permute-start | bytes 159752 | tf_op jit(solution)/shard_map/ppermute | solution.py:523
  4.6 6.1 %collective-permute-start.1 = (f32[104,128]{1,0:T(8,128)S(1)}, f32[104,128]{1,0:T(8,128)S(1)}, u32[]{:S(2)}, u32[]{:S(2)}) collective-permute-start(f32[104,128]{1,0:T(8,128)S(1)} %reshape.158), channel_id=1, source_target_pairs={{0,16},{8,24},{16,0},{24,8},{1,17},{9,25},{17,1},{25,9},{2,18},{10... | collective-permute-start | bytes 159752 | tf_op jit(solution)/shard_map/ppermute | solution.py:523
  7.2 5.9 %collective-permute-start.2 = (f32[104,128]{1,0:T(8,128)S(1)}, f32[104,128]{1,0:T(8,128)S(1)}, u32[]{:S(2)}, u32[]{:S(2)}) collective-permute-start(f32[104,128]{1,0:T(8,128)S(1)} %reshape.158), channel_id=1, source_target_pairs={{0,24},{8,16},{16,8},{24,0},{1,25},{9,17},{17,9},{25,1},{2,26},{10... | collective-permute-start | bytes 159752 | tf_op jit(solution)/shard_map/ppermute | solution.py:523
  7.2 0.7 copy-start.1
  7.2 0.8 copy-start.3
  7.2 0.8 copy-start.4
  8.0 11.2 %collective-permute-start.6 = (f32[88,256]{1,0:T(8,128)S(1)}, f32[88,256]{1,0:T(8,128)S(1)}, u32[]{:S(2)}, u32[]{:S(2)}) collective-permute-start(f32[88,256]{1,0:T(8,128)S(1)} %select_maximum_fusion), channel_id=1, source_target_pairs={{0,7},{1,6},{2,5},{3,4},{4,3},{5,2},{6,1},{7,0},{8,15},{9,14},{10,... | collective-permute-start | bytes 270344 | tf_op jit(solution)/shard_map/ppermute | solution.py:523
  9.6 0.7 copy-start.5
  13.2 8.6 %collective-permute-start.3 = (f32[424,128]{1,0:T(8,128)S(1)}, f32[424,128]{1,0:T(8,128)S(1)}, u32[]{:S(2)}, u32[]{:S(2)}) collective-permute-start(f32[424,128]{1,0:T(8,128)S(1)} %constant_dynamic-update-slice_fusion), channel_id=1, source_target_pairs={{0,2},{1,3},{2,0},{3,1},{4,6},{5,7},{6,4},{7,5},{8,10},{9,11},{10,... | collective-permute-start | bytes 651272 | tf_op jit(solution)/shard_map/ppermute | solution.py:523
  14.7 9.9 %collective-permute-start.4 = (f32[424,128]{1,0:T(8,128)S(1)}, f32[424,128]{1,0:T(8,128)S(1)}, u32[]{:S(2)}, u32[]{:S(2)}) collective-permute-start(f32[424,128]{1,0:T(8,128)S(1)} %constant_dynamic-update-slice_fusion), channel_id=1, source_target_pairs={{0,4},{1,5},{2,6},{3,7},{4,0},{5,1},{6,2},{7,3},{8,12},{9,13},{10,... | collective-permute-start | bytes 651272 | tf_op jit(solution)/shard_map/ppermute | solution.py:523
  16.2 8.4 %collective-permute-start.5 = (f32[424,128]{1,0:T(8,128)S(1)}, f32[424,128]{1,0:T(8,128)S(1)}, u32[]{:S(2)}, u32[]{:S(2)}) collective-permute-start(f32[424,128]{1,0:T(8,128)S(1)} %constant_dynamic-update-slice_fusion), channel_id=1, source_target_pairs={{0,6},{1,7},{2,4},{3,5},{4,2},{5,3},{6,0},{7,1},{8,14},{9,15},{10,... | collective-permute-start | bytes 651272 | tf_op jit(solution)/shard_map/ppermute | solution.py:523
  24.7 2.6 %copy-start.2 = (bf16[32,256]{1,0:T(8,128)(2,1)S(1)}, bf16[32,256]{1,0:T(8,128)(2,1)}, u32[]{:S(2)}) copy-start(bf16[32,256]{1,0:T(8,128)(2,1)} %constant.40.clone.mono_ref) | copy-start | bytes 49156
  24.8 2.5 %collective-permute-start.7 = (f32[4,424,128]{2,1,0:T(8,128)S(1)}, f32[4,424,128]{2,1,0:T(8,128)S(1)}, u32[]{:S(2)}, u32[]{:S(2)}) collective-permute-start(f32[4,424,128]{2,1,0:T(8,128)S(1)} %pad_maximum_fusion.mine_ref), channel_id=1, source_target_pairs={{0,1},{1,0},{2,3},{3,2},{4,5},{5,4},{6,7},{7,6},{8,9},{9,8},{10,11... | collective-permute-start | bytes 2605064 | tf_op jit(solution)/shard_map/ppermute | solution.py:523
  55.0 2.7 %collective-permute-start.8 = (f32[16,104,128]{2,1,0:T(8,128)}, f32[16,104,128]{2,1,0:T(8,128)}, u32[]{:S(2)}, u32[]{:S(2)}) collective-permute-start(f32[16,104,128]{2,1,0:T(8,128)} %get-tuple-element.42), channel_id=1, source_target_pairs={{0,1},{1,0},{2,3},{3,2},{4,5},{5,4},{6,7},{7,6},{8,9},{9,8},{10,11... | collective-permute-start | bytes 2555912 | tf_op jit(solution)/shard_map/ppermute | solution.py:523
  59.0 9.1 %collective-permute-start.10 = (f32[4,104,128]{2,1,0:T(8,128)S(1)}, f32[4,104,128]{2,1,0:T(8,128)S(1)}, u32[]{:S(2)}, u32[]{:S(2)}) collective-permute-start(f32[4,104,128]{2,1,0:T(8,128)S(1)} %get-tuple-element.52), channel_id=1, source_target_pairs={{0,6},{1,7},{2,4},{3,5},{4,2},{5,3},{6,0},{7,1},{8,14},{9,15},{10,... | collective-permute-start | bytes 638984 | tf_op jit(solution)/shard_map/ppermute | solution.py:523
  59.8 12.5 %collective-permute-start.11 = (f32[4,104,128]{2,1,0:T(8,128)S(1)}, f32[4,104,128]{2,1,0:T(8,128)S(1)}, u32[]{:S(2)}, u32[]{:S(2)}) collective-permute-start(f32[4,104,128]{2,1,0:T(8,128)S(1)} %get-tuple-element.54), channel_id=1, source_target_pairs={{0,4},{1,5},{2,6},{3,7},{4,0},{5,1},{6,2},{7,3},{8,12},{9,13},{10,... | collective-permute-start | bytes 638984 | tf_op jit(solution)/shard_map/ppermute | solution.py:523
  62.4 11.5 %collective-permute-start.12 = (f32[4,104,128]{2,1,0:T(8,128)S(1)}, f32[4,104,128]{2,1,0:T(8,128)S(1)}, u32[]{:S(2)}, u32[]{:S(2)}) collective-permute-start(f32[4,104,128]{2,1,0:T(8,128)S(1)} %get-tuple-element.53), channel_id=1, source_target_pairs={{0,2},{1,3},{2,0},{3,1},{4,6},{5,7},{6,4},{7,5},{8,10},{9,11},{10,... | collective-permute-start | bytes 638984 | tf_op jit(solution)/shard_map/ppermute | solution.py:523
  64.1 14.4 %collective-permute-start.9 = (f32[2,3,8,256]{3,2,1,0:T(8,128)S(1)}, f32[2,3,8,256]{3,2,1,0:T(8,128)S(1)}, u32[]{:S(2)}, u32[]{:S(2)}) collective-permute-start(f32[2,3,8,256]{3,2,1,0:T(8,128)S(1)} %get-tuple-element.44), channel_id=1, source_target_pairs={{0,7},{1,6},{2,5},{3,4},{4,3},{5,2},{6,1},{7,0},{8,15},{9,14},{10,... | collective-permute-start | bytes 147464 | tf_op jit(solution)/shard_map/ppermute | solution.py:523
  74.0 6.1 %collective-permute-start.13 = (f32[104,128]{1,0:T(8,128)S(1)}, f32[104,128]{1,0:T(8,128)S(1)}, u32[]{:S(2)}, u32[]{:S(2)}) collective-permute-start(f32[104,128]{1,0:T(8,128)S(1)} %get-tuple-element.57), channel_id=1, source_target_pairs={{0,24},{8,16},{16,8},{24,0},{1,25},{9,17},{17,9},{25,1},{2,26},{10... | collective-permute-start | bytes 159752 | tf_op jit(solution)/shard_map/ppermute | solution.py:523
  76.9 5.0 %collective-permute-start.14 = (f32[104,128]{1,0:T(8,128)S(1)}, f32[104,128]{1,0:T(8,128)S(1)}, u32[]{:S(2)}, u32[]{:S(2)}) collective-permute-start(f32[104,128]{1,0:T(8,128)S(1)} %get-tuple-element.56), channel_id=1, source_target_pairs={{0,16},{8,24},{16,0},{24,8},{1,17},{9,25},{17,1},{25,9},{2,18},{10... | collective-permute-start | bytes 159752 | tf_op jit(solution)/shard_map/ppermute | solution.py:523
  76.9 5.2 %collective-permute-start.15 = (f32[104,128]{1,0:T(8,128)S(1)}, f32[104,128]{1,0:T(8,128)S(1)}, u32[]{:S(2)}, u32[]{:S(2)}) collective-permute-start(f32[104,128]{1,0:T(8,128)S(1)} %get-tuple-element.55), channel_id=1, source_target_pairs={{0,8},{8,0},{16,24},{24,16},{1,9},{9,1},{17,25},{25,17},{2,10},{10... | collective-permute-start | bytes 159752 | tf_op jit(solution)/shard_map/ppermute | solution.py:523

commit v6 on v5

--- a/solution.py
+++ b/solution.py
@@ -538,7 +538,9 @@
     me = (view_index * tile_group + tile_index).astype(jnp.int32)
 
     totals = jnp.sum(live_count, axis=1)
-    within = jnp.cumsum(live_count, axis=1) - live_count
+    place = lax.broadcasted_iota(jnp.int32, (1, tiles_view, tiles_view), 2)
+    earlier = place < lax.broadcasted_iota(jnp.int32, (1, tiles_view, tiles_view), 1)
+    within = jnp.sum(jnp.where(earlier, live_count[:, None, :], 0), axis=2)
 
     smem = pl.BlockSpec(memory_space=pltpu.SMEM)
     vmem = pl.BlockSpec(memory_space=pltpu.VMEM)
@@ -652,15 +654,12 @@
         monomials(pixels),
     )
 
-    whole = totals
-    before = jnp.zeros_like(totals)
-    for core, held in enumerate((mine, other)):
-        for m in range(chips):
-            mask = 2 * m + core
-            if mask:
-                theirs = held[m, view_group * FIELDS * GROUPS, 0:views].astype(jnp.int32)
-                whole = whole + theirs
-                before = before + jnp.where((tile_index ^ mask) < tile_index, theirs, 0)
+    row = view_group * FIELDS * GROUPS
+    counts = jnp.stack([mine[:, row, 0:views], other[:, row, 0:views]], axis=1)
+    counts = counts.reshape(tile_group, views).astype(jnp.int32)
+    peer = lax.broadcasted_iota(jnp.int32, counts.shape, 0) ^ tile_index
+    whole = jnp.sum(counts, axis=0)
+    before = jnp.sum(jnp.where(peer < tile_index, counts, 0), axis=0)
     next_owner = (before[:, None] + within) * tile_group // whole[:, None]
 
     grad_other = swap(grad_other, "tile", 1)

time: 82.5 us -> 80.7 us (0.978)
  Pallas kernels: 33.2 us -> 31.9 us
  waiting for transfers between devices: 22.6 us -> 21.3 us
  other arithmetic: 4.16 us -> 3.02 us
  starting transfers between devices: 20.4 us -> 21.5 us
    pallas_call x1, Pallas kernels: 27.8 us -> 26.5 us  [shards(): splat(cam, rows, live_now, own_group, their_group, mine, other, target, m...]
    ppermute x16, waiting for transfers between devices: 22.6 us -> 21.3 us  [swap(): return lax.ppermute(array, axis, [(i, i ^ mask) for i in range(size)])]
    ppermute x16, starting transfers between devices: 20.4 us -> 21.5 us  [swap(): return lax.ppermute(array, axis, [(i, i ^ mask) for i in range(size)])]
    add x1, other arithmetic: 1.24 us -> 0.09 us  [shards(): joined = grad_mine + grad_other]
  transfers between devices with their start and end apart: 16 -> 16, of which waited for: 11 -> 10; matrix products, arithmetic and copies ran while one was open for 3% -> 3% of each run, Pallas kernels for 6% -> 6%
where the time goes in v6:
time: 80.7 us; the launch traced here: 80.4 us
  Pallas kernels  31.9 us (40%)
  starting transfers between devices  21.5 us (27%)
  waiting for transfers between devices  21.3 us (26%)
  other arithmetic  3.02 us (4%)
  local copies, waits for them, and re-layouts  1.68 us (2%)
  between operations  0.82 us (1%)
    pallas_call x1, Pallas kernels, shards(): splat(cam, rows, live_now, own_group, their_group, mine, other, target, m...  26.5 us
    ppermute x16, starting transfers between devices, swap(): return lax.ppermute(array, axis, [(i, i ^ mask) for i in range(size)])  21.5 us
    ppermute x16, waiting for transfers between devices, swap(): return lax.ppermute(array, axis, [(i, i ^ mask) for i in range(size)])  21.3 us
    pallas_call x1, Pallas kernels, shards(): prep_own(me[None], live_count, camera, intersection_ids, depth_order)  2.5 us
    pallas_call x1, Pallas kernels, shards(): their_rows, their_group = prep_their(me[None], live_now, message)  2.29 us
  transfers between devices with their start and end apart: 16, of which 10 were waited for; matrix products, arithmetic and copies ran while one was open for 3% of the time, Pallas kernels for 6%

profile of v6, /device:TPU:0, one launch (start us, length us, event | category | flops | bytes accessed | tf_op | source)
XLA Modules:
  0.0 80.4 jit_solution(11983224990167862092)
XLA Ops:
  0.6 0.8 %pad_maximum_fusion.1 = f32[13,1024]{1,0:T(8,128)S(1)} fusion(f32[3,1024]{1,0:T(4,128)} %param.13, f32[1,1024]{1,0:T(1,128)} %bitcast.36, f32[6,1024]{1,0:T(8,128)} %param.11, f32[3,1024]{1,0:T(4,128)} %param.10), kind=kLoop, calls=%fused_computation.5 | loop fusion | flops 39936 | bytes 106496 | tf_op jit(solution)/shard_map/concatenate | solution.py:596
  1.5 3.1 %collective-permute-start = (f32[104,128]{1,0:T(8,128)S(1)}, f32[104,128]{1,0:T(8,128)S(1)}, u32[]{:S(2)}, u32[]{:S(2)}) collective-permute-start(f32[104,128]{1,0:T(8,128)S(1)} %reshape.69), channel_id=1, source_target_pairs={{0,8},{8,0},{16,24},{24,16},{1,9},{9,1},{17,25},{25,17},{2,10},{10... | collective-permute-start | bytes 159752 | tf_op jit(solution)/shard_map/ppermute | solution.py:523
  4.6 2.6 %collective-permute-start.1 = (f32[104,128]{1,0:T(8,128)S(1)}, f32[104,128]{1,0:T(8,128)S(1)}, u32[]{:S(2)}, u32[]{:S(2)}) collective-permute-start(f32[104,128]{1,0:T(8,128)S(1)} %reshape.69), channel_id=1, source_target_pairs={{0,16},{8,24},{16,0},{24,8},{1,17},{9,25},{17,1},{25,9},{2,18},{10... | collective-permute-start | bytes 159752 | tf_op jit(solution)/shard_map/ppermute | solution.py:523
  7.2 0.0 copy-start.4
  7.3 0.6 copy-done.2
  7.9 0.1 fusion.2
  8.0 0.0 copy-done.3
  8.0 0.0 copy-done.4
  8.0 1.4 %collective-permute-start.6 = (f32[88,256]{1,0:T(8,128)S(1)}, f32[88,256]{1,0:T(8,128)S(1)}, u32[]{:S(2)}, u32[]{:S(2)}) collective-permute-start(f32[88,256]{1,0:T(8,128)S(1)} %select_maximum_fusion), channel_id=1, source_target_pairs={{0,7},{1,6},{2,5},{3,4},{4,3},{5,2},{6,1},{7,0},{8,15},{9,14},{10,... | collective-permute-start | bytes 270344 | tf_op jit(solution)/shard_map/ppermute | solution.py:523
  9.4 0.1 reduce_sum.36
  9.6 0.0 copy-start.5
  9.6 0.1 reshape.70
  9.7 0.6 copy-done.5
  10.3 0.1 copy.17.camera_ref
  10.4 0.3 collective-permute-done.1
  10.7 2.5 %collective-permute-done.2 = f32[104,128]{1,0:T(8,128)S(1)} collective-permute-done((f32[104,128]{1,0:T(8,128)S(1)}, f32[104,128]{1,0:T(8,128)S(1)}, u32[]{:S(2)}, u32[]{:S(2)}) %collective-permute-start.2) | collective-permute-done | bytes 53280 | tf_op jit(solution)/shard_map/ppermute | solution.py:523
  13.2 1.6 %collective-permute-start.3 = (f32[424,128]{1,0:T(8,128)S(1)}, f32[424,128]{1,0:T(8,128)S(1)}, u32[]{:S(2)}, u32[]{:S(2)}) collective-permute-start(f32[424,128]{1,0:T(8,128)S(1)} %constant_dynamic-update-slice_fusion), channel_id=1, source_target_pairs={{0,2},{1,3},{2,0},{3,1},{4,6},{5,7},{6,4},{7,5},{8,10},{9,11},{10,... | collective-permute-start | bytes 651272 | tf_op jit(solution)/shard_map/ppermute | solution.py:523
  14.7 1.5 %collective-permute-start.4 = (f32[424,128]{1,0:T(8,128)S(1)}, f32[424,128]{1,0:T(8,128)S(1)}, u32[]{:S(2)}, u32[]{:S(2)}) collective-permute-start(f32[424,128]{1,0:T(8,128)S(1)} %constant_dynamic-update-slice_fusion), channel_id=1, source_target_pairs={{0,4},{1,5},{2,6},{3,7},{4,0},{5,1},{6,2},{7,3},{8,12},{9,13},{10,... | collective-permute-start | bytes 651272 | tf_op jit(solution)/shard_map/ppermute | solution.py:523
  16.2 0.5 collective-permute-start.5
  16.7 2.5 %prep_own.1 = (s32[16,256]{1,0:T(8,128)S(1)}, s32[16,256]{1,0:T(8,128)S(1)}, f32[16]{0:T(128)S(1)}) custom-call(s32[1]{0:T(128)} %bitcast.6.me_ref, s32[2,16]{1,0:T(2,128)S(1)} %copy-done.2, f32[8,2,4]{2,1,0:T(2,128)S(1)} %copy.17.camera_ref, s32[2,16,256]{2,1,0:T(8,128)S(1)} %copy-done.3, s32[2,16,256]{2,1,0:T(8,128)S(1)} %copy-done.4), custom_call_target="tpu_custom_call" | custom-call | flops 4000000000 | bytes 65536 | tf_op jit(solution)/shard_map/prep_own/pallas_call | solution.py:603
  19.3 0.1 reshape.72
  19.3 0.1 pad_add_fusion.live_ref
  19.4 2.3 %prep_their.1 = (s32[24,256]{1,0:T(8,128)S(1)}, s32[16,256]{1,0:T(8,128)S(1)}) custom-call(s32[1]{0:T(128)} %bitcast.6.me_ref, s32[32]{0:T(128)S(1)} %pad_add_fusion.live_ref, f32[88,256]{1,0:T(8,128)S(1)} %collective-permute-done.6.message_ref), custom_call_target="tpu_custom_call" | custom-call | flops 4000000000 | bytes 65536 | tf_op jit(solution)/shard_map/prep_their/pallas_call | solution.py:606
  21.8 2.9 %collective-permute-done.4 = f32[424,128]{1,0:T(8,128)S(1)} collective-permute-done((f32[424,128]{1,0:T(8,128)S(1)}, f32[424,128]{1,0:T(8,128)S(1)}, u32[]{:S(2)}, u32[]{:S(2)}) %collective-permute-start.4) | collective-permute-done | bytes 217120 | tf_op jit(solution)/shard_map/ppermute | solution.py:523
  24.7 0.1 pad_maximum_fusion.mine_ref
  24.8 0.1 collective-permute-start.7
  24.8 2.4 %collective-permute-done.7.other_ref = f32[4,424,128]{2,1,0:T(8,128)S(1)} collective-permute-done((f32[4,424,128]{2,1,0:T(8,128)S(1)}, f32[4,424,128]{2,1,0:T(8,128)S(1)}, u32[]{:S(2)}, u32[]{:S(2)}) %collective-permute-start.7) | collective-permute-done | bytes 868384 | tf_op jit(solution)/shard_map/ppermute | solution.py:523
  27.2 26.5 %splat.1 = (f32[2,3,8,256]{3,2,1,0:T(8,128)S(1)}, f32[2,3,8,256]{3,2,1,0:T(8,128)S(1)}, f32[16,104,128]{2,1,0:T(8,128)S(1)}, f32[16,104,128]{2,1,0:T(8,128)S(1)}) custom-call(f32[16]{0:T(128)S(1)} %get-tuple-element.35.cam_ref, s32[10240]{0:T(1024)S(1)} %bitcast.30, s32[32]{0:T(128)S(1)} %pad_add_fusion.live_ref, ...), custom_call_target="tpu_custom_call" | custom-call | tf_op jit(solution)/shard_map/splat/pallas_call | solution.py:644
  53.7 1.7 %collective-permute-start.8 = (f32[16,104,128]{2,1,0:T(8,128)S(1)}, f32[16,104,128]{2,1,0:T(8,128)S(1)}, u32[]{:S(2)}, u32[]{:S(2)}) collective-permute-start(f32[16,104,128]{2,1,0:T(8,128)S(1)} %get-tuple-element.42), channel_id=1, source_target_pairs={{0,1},{1,0},{2,3},{3,2},{4,5},{5,4},{6,7},{7,6},{8,9},{9,8},{10,11... | collective-permute-start | bytes 2555912 | tf_op jit(solution)/shard_map/ppermute | solution.py:523
  55.4 0.1 select_reduce_fusion
  55.6 0.1 select_reduce_fusion.1
  55.7 1.8 %collective-permute-done.8 = f32[16,104,128]{2,1,0:T(8,128)S(1)} collective-permute-done((f32[16,104,128]{2,1,0:T(8,128)S(1)}, f32[16,104,128]{2,1,0:T(8,128)S(1)}, u32[]{:S(2)}, u32[]{:S(2)}) %collective-permute-start.8) | collective-permute-done | bytes 852000 | tf_op jit(solution)/shard_map/ppermute | solution.py:523
  57.4 0.1 add.30
  57.6 1.6 %collective-permute-start.10 = (f32[4,104,128]{2,1,0:T(8,128)S(1)}, f32[4,104,128]{2,1,0:T(8,128)S(1)}, u32[]{:S(2)}, u32[]{:S(2)}) collective-permute-start(f32[4,104,128]{2,1,0:T(8,128)S(1)} %get-tuple-element.52), channel_id=1, source_target_pairs={{0,6},{1,7},{2,4},{3,5},{4,2},{5,3},{6,0},{7,1},{8,14},{9,15},{10,... | collective-permute-start | bytes 638984 | tf_op jit(solution)/shard_map/ppermute | solution.py:523
  59.2 1.1 %collective-permute-start.11 = (f32[4,104,128]{2,1,0:T(8,128)S(1)}, f32[4,104,128]{2,1,0:T(8,128)S(1)}, u32[]{:S(2)}, u32[]{:S(2)}) collective-permute-start(f32[4,104,128]{2,1,0:T(8,128)S(1)} %get-tuple-element.54), channel_id=1, source_target_pairs={{0,4},{1,5},{2,6},{3,7},{4,0},{5,1},{6,2},{7,3},{8,12},{9,13},{10,... | collective-permute-start | bytes 638984 | tf_op jit(solution)/shard_map/ppermute | solution.py:523
  60.3 1.3 %collective-permute-start.12 = (f32[4,104,128]{2,1,0:T(8,128)S(1)}, f32[4,104,128]{2,1,0:T(8,128)S(1)}, u32[]{:S(2)}, u32[]{:S(2)}) collective-permute-start(f32[4,104,128]{2,1,0:T(8,128)S(1)} %get-tuple-element.53), channel_id=1, source_target_pairs={{0,2},{1,3},{2,0},{3,1},{4,6},{5,7},{6,4},{7,5},{8,10},{9,11},{10,... | collective-permute-start | bytes 638984 | tf_op jit(solution)/shard_map/ppermute | solution.py:523
  61.6 0.8 and_select_fusion
  62.3 0.6 collective-permute-start.9
  63.0 3.7 %collective-permute-done.10 = f32[4,104,128]{2,1,0:T(8,128)S(1)} collective-permute-done((f32[4,104,128]{2,1,0:T(8,128)S(1)}, f32[4,104,128]{2,1,0:T(8,128)S(1)}, u32[]{:S(2)}, u32[]{:S(2)}) %collective-permute-start.10) | collective-permute-done | bytes 213024 | tf_op jit(solution)/shard_map/ppermute | solution.py:523
  66.7 4.5 %collective-permute-done.11 = f32[4,104,128]{2,1,0:T(8,128)S(1)} collective-permute-done((f32[4,104,128]{2,1,0:T(8,128)S(1)}, f32[4,104,128]{2,1,0:T(8,128)S(1)}, u32[]{:S(2)}, u32[]{:S(2)}) %collective-permute-start.11) | collective-permute-done | bytes 213024 | tf_op jit(solution)/shard_map/ppermute | solution.py:523
  71.2 0.8 %collective-permute-done.12 = f32[4,104,128]{2,1,0:T(8,128)S(1)} collective-permute-done((f32[4,104,128]{2,1,0:T(8,128)S(1)}, f32[4,104,128]{2,1,0:T(8,128)S(1)}, u32[]{:S(2)}, u32[]{:S(2)}) %collective-permute-start.12) | collective-permute-done | bytes 213024 | tf_op jit(solution)/shard_map/ppermute | solution.py:523
  72.0 0.1 add_add_fusion
  72.1 1.9 %collective-permute-start.13 = (f32[104,128]{1,0:T(8,128)S(1)}, f32[104,128]{1,0:T(8,128)S(1)}, u32[]{:S(2)}, u32[]{:S(2)}) collective-permute-start(f32[104,128]{1,0:T(8,128)S(1)} %get-tuple-element.57), channel_id=1, source_target_pairs={{0,24},{8,16},{16,8},{24,0},{1,25},{9,17},{17,9},{25,1},{2,26},{10... | collective-permute-start | bytes 159752 | tf_op jit(solution)/shard_map/ppermute | solution.py:523
  74.0 2.5 %collective-permute-start.15 = (f32[104,128]{1,0:T(8,128)S(1)}, f32[104,128]{1,0:T(8,128)S(1)}, u32[]{:S(2)}, u32[]{:S(2)}) collective-permute-start(f32[104,128]{1,0:T(8,128)S(1)} %get-tuple-element.55), channel_id=1, source_target_pairs={{0,8},{8,0},{16,24},{24,16},{1,9},{9,1},{17,25},{25,17},{2,10},{10... | collective-permute-start | bytes 159752 | tf_op jit(solution)/shard_map/ppermute | solution.py:523
  76.5 0.6 maximum_bitcast_fusion
  77.2 1.4 %collective-permute-done.13.refs_1_ = f32[104,128]{1,0:T(8,128)S(1)} collective-permute-done((f32[104,128]{1,0:T(8,128)S(1)}, f32[104,128]{1,0:T(8,128)S(1)}, u32[]{:S(2)}, u32[]{:S(2)}) %collective-permute-start.13) | collective-permute-done | bytes 53280 | tf_op jit(solution)/shard_map/ppermute | solution.py:523
  78.6 1.1 %collective-permute-done.14.refs_2_ = f32[104,128]{1,0:T(8,128)S(1)} collective-permute-done((f32[104,128]{1,0:T(8,128)S(1)}, f32[104,128]{1,0:T(8,128)S(1)}, u32[]{:S(2)}, u32[]{:S(2)}) %collective-permute-start.14) | collective-permute-done | bytes 53280 | tf_op jit(solution)/shard_map/ppermute | solution.py:523
  79.7 0.7 tail.1
  (34 shorter events, 0.2 us)
Async XLA Ops:
  0.6 6.6 %copy-start = (f32[2,16,3,256]{3,1,2,0:T(8,128)S(1)}, f32[2,16,3,256]{3,1,2,0:T(8,128)}, u32[]{:S(2)}) copy-start(f32[2,16,3,256]{3,1,2,0:T(8,128)} %param.15) | copy-start | bytes 294916
  1.5 8.8 %collective-permute-start = (f32[104,128]{1,0:T(8,128)S(1)}, f32[104,128]{1,0:T(8,128)S(1)}, u32[]{:S(2)}, u32[]{:S(2)}) collective-permute-start(f32[104,128]{1,0:T(8,128)S(1)} %reshape.69), channel_id=1, source_target_pairs={{0,8},{8,0},{16,24},{24,16},{1,9},{9,1},{17,25},{25,17},{2,10},{10... | collective-permute-start | bytes 159752 | tf_op jit(solution)/shard_map/ppermute | solution.py:523
  4.6 6.1 %collective-permute-start.1 = (f32[104,128]{1,0:T(8,128)S(1)}, f32[104,128]{1,0:T(8,128)S(1)}, u32[]{:S(2)}, u32[]{:S(2)}) collective-permute-start(f32[104,128]{1,0:T(8,128)S(1)} %reshape.69), channel_id=1, source_target_pairs={{0,16},{8,24},{16,0},{24,8},{1,17},{9,25},{17,1},{25,9},{2,18},{10... | collective-permute-start | bytes 159752 | tf_op jit(solution)/shard_map/ppermute | solution.py:523
  7.2 5.9 %collective-permute-start.2 = (f32[104,128]{1,0:T(8,128)S(1)}, f32[104,128]{1,0:T(8,128)S(1)}, u32[]{:S(2)}, u32[]{:S(2)}) collective-permute-start(f32[104,128]{1,0:T(8,128)S(1)} %reshape.69), channel_id=1, source_target_pairs={{0,24},{8,16},{16,8},{24,0},{1,25},{9,17},{17,9},{25,1},{2,26},{10... | collective-permute-start | bytes 159752 | tf_op jit(solution)/shard_map/ppermute | solution.py:523
  7.2 0.7 copy-start.2
  7.2 0.8 copy-start.3
  7.2 0.8 copy-start.4
  8.0 11.2 %collective-permute-start.6 = (f32[88,256]{1,0:T(8,128)S(1)}, f32[88,256]{1,0:T(8,128)S(1)}, u32[]{:S(2)}, u32[]{:S(2)}) collective-permute-start(f32[88,256]{1,0:T(8,128)S(1)} %select_maximum_fusion), channel_id=1, source_target_pairs={{0,7},{1,6},{2,5},{3,4},{4,3},{5,2},{6,1},{7,0},{8,15},{9,14},{10,... | collective-permute-start | bytes 270344 | tf_op jit(solution)/shard_map/ppermute | solution.py:523
  9.6 0.7 copy-start.5
  13.2 8.6 %collective-permute-start.3 = (f32[424,128]{1,0:T(8,128)S(1)}, f32[424,128]{1,0:T(8,128)S(1)}, u32[]{:S(2)}, u32[]{:S(2)}) collective-permute-start(f32[424,128]{1,0:T(8,128)S(1)} %constant_dynamic-update-slice_fusion), channel_id=1, source_target_pairs={{0,2},{1,3},{2,0},{3,1},{4,6},{5,7},{6,4},{7,5},{8,10},{9,11},{10,... | collective-permute-start | bytes 651272 | tf_op jit(solution)/shard_map/ppermute | solution.py:523
  14.7 9.9 %collective-permute-start.4 = (f32[424,128]{1,0:T(8,128)S(1)}, f32[424,128]{1,0:T(8,128)S(1)}, u32[]{:S(2)}, u32[]{:S(2)}) collective-permute-start(f32[424,128]{1,0:T(8,128)S(1)} %constant_dynamic-update-slice_fusion), channel_id=1, source_target_pairs={{0,4},{1,5},{2,6},{3,7},{4,0},{5,1},{6,2},{7,3},{8,12},{9,13},{10,... | collective-permute-start | bytes 651272 | tf_op jit(solution)/shard_map/ppermute | solution.py:523
  16.2 8.4 %collective-permute-start.5 = (f32[424,128]{1,0:T(8,128)S(1)}, f32[424,128]{1,0:T(8,128)S(1)}, u32[]{:S(2)}, u32[]{:S(2)}) collective-permute-start(f32[424,128]{1,0:T(8,128)S(1)} %constant_dynamic-update-slice_fusion), channel_id=1, source_target_pairs={{0,6},{1,7},{2,4},{3,5},{4,2},{5,3},{6,0},{7,1},{8,14},{9,15},{10,... | collective-permute-start | bytes 651272 | tf_op jit(solution)/shard_map/ppermute | solution.py:523
  24.7 2.6 %copy-start.1 = (bf16[32,256]{1,0:T(8,128)(2,1)S(1)}, bf16[32,256]{1,0:T(8,128)(2,1)}, u32[]{:S(2)}) copy-start(bf16[32,256]{1,0:T(8,128)(2,1)} %constant.25.clone.mono_ref) | copy-start | bytes 49156
  24.8 2.5 %collective-permute-start.7 = (f32[4,424,128]{2,1,0:T(8,128)S(1)}, f32[4,424,128]{2,1,0:T(8,128)S(1)}, u32[]{:S(2)}, u32[]{:S(2)}) collective-permute-start(f32[4,424,128]{2,1,0:T(8,128)S(1)} %pad_maximum_fusion.mine_ref), channel_id=1, source_target_pairs={{0,1},{1,0},{2,3},{3,2},{4,5},{5,4},{6,7},{7,6},{8,9},{9,8},{10,11... | collective-permute-start | bytes 2605064 | tf_op jit(solution)/shard_map/ppermute | solution.py:523
  53.7 3.7 %collective-permute-start.8 = (f32[16,104,128]{2,1,0:T(8,128)S(1)}, f32[16,104,128]{2,1,0:T(8,128)S(1)}, u32[]{:S(2)}, u32[]{:S(2)}) collective-permute-start(f32[16,104,128]{2,1,0:T(8,128)S(1)} %get-tuple-element.42), channel_id=1, source_target_pairs={{0,1},{1,0},{2,3},{3,2},{4,5},{5,4},{6,7},{7,6},{8,9},{9,8},{10,11... | collective-permute-start | bytes 2555912 | tf_op jit(solution)/shard_map/ppermute | solution.py:523
  57.6 9.1 %collective-permute-start.10 = (f32[4,104,128]{2,1,0:T(8,128)S(1)}, f32[4,104,128]{2,1,0:T(8,128)S(1)}, u32[]{:S(2)}, u32[]{:S(2)}) collective-permute-start(f32[4,104,128]{2,1,0:T(8,128)S(1)} %get-tuple-element.52), channel_id=1, source_target_pairs={{0,6},{1,7},{2,4},{3,5},{4,2},{5,3},{6,0},{7,1},{8,14},{9,15},{10,... | collective-permute-start | bytes 638984 | tf_op jit(solution)/shard_map/ppermute | solution.py:523
  59.2 11.9 %collective-permute-start.11 = (f32[4,104,128]{2,1,0:T(8,128)S(1)}, f32[4,104,128]{2,1,0:T(8,128)S(1)}, u32[]{:S(2)}, u32[]{:S(2)}) collective-permute-start(f32[4,104,128]{2,1,0:T(8,128)S(1)} %get-tuple-element.54), channel_id=1, source_target_pairs={{0,4},{1,5},{2,6},{3,7},{4,0},{5,1},{6,2},{7,3},{8,12},{9,13},{10,... | collective-permute-start | bytes 638984 | tf_op jit(solution)/shard_map/ppermute | solution.py:523
  60.3 11.7 %collective-permute-start.12 = (f32[4,104,128]{2,1,0:T(8,128)S(1)}, f32[4,104,128]{2,1,0:T(8,128)S(1)}, u32[]{:S(2)}, u32[]{:S(2)}) collective-permute-start(f32[4,104,128]{2,1,0:T(8,128)S(1)} %get-tuple-element.53), channel_id=1, source_target_pairs={{0,2},{1,3},{2,0},{3,1},{4,6},{5,7},{6,4},{7,5},{8,10},{9,11},{10,... | collective-permute-start | bytes 638984 | tf_op jit(solution)/shard_map/ppermute | solution.py:523
  62.3 14.2 %collective-permute-start.9 = (f32[2,3,8,256]{3,2,1,0:T(8,128)S(1)}, f32[2,3,8,256]{3,2,1,0:T(8,128)S(1)}, u32[]{:S(2)}, u32[]{:S(2)}) collective-permute-start(f32[2,3,8,256]{3,2,1,0:T(8,128)S(1)} %get-tuple-element.44), channel_id=1, source_target_pairs={{0,7},{1,6},{2,5},{3,4},{4,3},{5,2},{6,1},{7,0},{8,15},{9,14},{10,... | collective-permute-start | bytes 147464 | tf_op jit(solution)/shard_map/ppermute | solution.py:523
  72.1 6.5 %collective-permute-start.13 = (f32[104,128]{1,0:T(8,128)S(1)}, f32[104,128]{1,0:T(8,128)S(1)}, u32[]{:S(2)}, u32[]{:S(2)}) collective-permute-start(f32[104,128]{1,0:T(8,128)S(1)} %get-tuple-element.57), channel_id=1, source_target_pairs={{0,24},{8,16},{16,8},{24,0},{1,25},{9,17},{17,9},{25,1},{2,26},{10... | collective-permute-start | bytes 159752 | tf_op jit(solution)/shard_map/ppermute | solution.py:523
  74.0 5.7 %collective-permute-start.14 = (f32[104,128]{1,0:T(8,128)S(1)}, f32[104,128]{1,0:T(8,128)S(1)}, u32[]{:S(2)}, u32[]{:S(2)}) collective-permute-start(f32[104,128]{1,0:T(8,128)S(1)} %get-tuple-element.56), channel_id=1, source_target_pairs={{0,16},{8,24},{16,0},{24,8},{1,17},{9,25},{17,1},{25,9},{2,18},{10... | collective-permute-start | bytes 159752 | tf_op jit(solution)/shard_map/ppermute | solution.py:523
  74.0 5.7 %collective-permute-start.15 = (f32[104,128]{1,0:T(8,128)S(1)}, f32[104,128]{1,0:T(8,128)S(1)}, u32[]{:S(2)}, u32[]{:S(2)}) collective-permute-start(f32[104,128]{1,0:T(8,128)S(1)} %get-tuple-element.55), channel_id=1, source_target_pairs={{0,8},{8,0},{16,24},{24,16},{1,9},{9,1},{17,25},{25,17},{2,10},{10... | collective-permute-start | bytes 159752 | tf_op jit(solution)/shard_map/ppermute | solution.py:523

commit v7 on v6

--- a/solution.py
+++ b/solution.py
@@ -18,6 +18,7 @@
 UNROLL = 8
 SIZES = 3
 BATCH = 8
+SWEEP = 4
 LOG2E = math.log2(math.e)
 OFF = -1e4
 
@@ -186,7 +187,7 @@
 
     for acc in accs:
         acc[...] = jnp.zeros_like(acc)
-    for ref in (buf, w_hi, w_lo, g_1, g_2, g_3, row_s, row_2):
+    for ref in (w_hi, w_lo, row_s, row_2):
         ref[...] = jnp.zeros_like(ref)
 
     kept = tiles_view // 2
@@ -298,7 +299,15 @@
     def render(tile, positions):
         zero_rows = jnp.zeros((8, positions), F32)
         used = slice(0, positions)
-        blocks = (chunk_rows(functools.reduce(jnp.maximum, [live_of(t) for t in tile])) + 3) >> 2
+        lives = [live_of(t) for t in tile]
+        sweeps = [range(g, g + SWEEP) for g in range(0, BATCH, SWEEP)]
+
+        def sweep(body, carry):
+            out = []
+            for group in sweeps:
+                blocks = (chunk_rows(functools.reduce(jnp.maximum, [lives[g] for g in group])) + 3) >> 2
+                out += lax.fori_loop(0, blocks, partial(body, group), tuple(carry[g] for g in group))
+            return out
         for g, t in enumerate(tile):
             for n in range(6):
                 row_s[g, n : n + 1, :] = rec[n, pl.ds(t, 1), :]
@@ -309,18 +318,18 @@
             c_s[g, used, :] = dot_tn(lhs, mono_ref[...])
         colour = [pieces_of(row_s[g, 8:16, used], 3) for g in range(BATCH)]
 
-        def through(i, prods):
+        def through(group, i, prods):
             rows = pl.ds(pl.multiple_of(i * 32, 32), 32)
             out = []
-            for g in range(BATCH):
+            for g, last in zip(group, prods):
                 cover = jnp.exp2(c_s[g, rows, :])
                 c_s[g, rows, :] = cover
                 keep = 1.0 - cover
-                out.append(prods[g] * ((keep[0:8] * keep[8:16]) * (keep[16:24] * keep[24:32])))
+                out.append(last * ((keep[0:8] * keep[8:16]) * (keep[16:24] * keep[24:32])))
             return tuple(out)
 
         ones = jnp.ones((GROUPS, pixels), F32)
-        lead = list(lax.fori_loop(0, blocks, through, (ones,) * BATCH))
+        lead = sweep(through, [ones] * BATCH)
         for g in range(BATCH):
             scan = lead[g]
             for step in (1, 2, 4):
@@ -335,11 +344,11 @@
                 out.append(weight)
             return out, prod
 
-        def weigh(i, prods):
+        def weigh(group, i, prods):
             rows = pl.ds(pl.multiple_of(i * 32, 32), 32)
             out = []
-            for g in range(BATCH):
-                parts, prod = weights(c_s[g, rows, :], prods[g])
+            for g, last in zip(group, prods):
+                parts, prod = weights(c_s[g, rows, :], last)
                 weight = jnp.concatenate(parts, axis=0)
                 high = weight.astype(BF16)
                 w_hi[g, rows, :] = high
@@ -347,7 +356,7 @@
                 out.append(prod)
             return tuple(out)
 
-        lax.fori_loop(0, blocks, weigh, tuple(lead))
+        sweep(weigh, lead)
 
         after = []
         for g, t in enumerate(tile):
@@ -378,11 +387,10 @@
             rhs = jnp.concatenate([paired(m1, m2), paired(m1, m3), paired(m2, m1), zero_pix], axis=0)
             h_s[g, used, :] = dot_tn(lhs.astype(BF16), rhs.astype(BF16))
 
-        def settle(i, carry):
+        def settle(group, i, carry):
             rows = pl.ds(pl.multiple_of(i * 32, 32), 32)
             out = []
-            for g in range(BATCH):
-                prod, tail = carry[g]
+            for g, (prod, tail) in zip(group, carry):
                 cover = c_s[g, rows, :]
                 pull = h_s[g, rows, :]
                 parts, prod = weights(cover, prod)
@@ -403,14 +411,14 @@
                 out.append((prod, tail))
             return tuple(out)
 
-        lax.fori_loop(0, blocks, settle, tuple(zip(lead, after)))
+        sweep(settle, list(zip(lead, after)))
         mono = mono_ref[0:16, :]
         for g in range(BATCH):
             moments = dot_nt(mono, g_1[g, used, :]) + dot_nt(mono, g_2[g, used, :]) + dot_nt(mono, g_3[g, used, :])
             miss_lhs = jnp.concatenate(missed[g] + [zero_pix], axis=0).astype(BF16)
             tint = dot_nt(miss_lhs, w_hi[g, used, :]) + dot_nt(miss_lhs, w_lo[g, used, :])
-            row_s[g, 0:8, used] = moments[0:8]
-            row_s[g, 8:16, used] = tint[0:8] + tint[8:16] + tint[16:24]
+            row_s[g, 0:6, used] = moments[0:6]
+            row_s[g, 8:11, used] = (tint[0:8] + tint[8:16] + tint[16:24])[0:3]
         for g, t in enumerate(tile):
             for n in range(6):
                 mom[n, pl.ds(t, 1), :] = row_s[g, n : n + 1, :]
@@ -477,9 +485,10 @@
         for base, ref in ((0, grad_mine_ref), (half, grad_other_ref)):
             for d in range(column):
                 start = pl.multiple_of((base + q * column + d) * lanes, lanes)
-                total = accs[0][pl.ds(start, lanes), :]
-                for acc in accs[1:]:
-                    total = total + acc[pl.ds(start, lanes), :]
+                sums = [acc[pl.ds(start, lanes), :] for acc in accs]
+                while len(sums) > 1:
+                    sums = [a + b for a, b in zip(sums[::2], sums[1::2])]
+                total = sums[0]
                 ref[q * column + d] = jnp.transpose(total)[0:used]
         return 0
 

time: 80.7 us -> 79.7 us (0.988)
    ppermute x16, starting transfers between devices: 21.5 us -> 20.7 us  [swap(): return lax.ppermute(array, axis, [(i, i ^ mask) for i in range(size)])]
  transfers between devices with their start and end apart: 16 -> 16, of which waited for: 10 -> 9; matrix products, arithmetic and copies ran while one was open for 3% -> 3% of each run, Pallas kernels for 6% -> 6%
where the time goes in v7:
time: 79.7 us
  Pallas kernels  32.7 us (41%)
  starting transfers between devices  20.7 us (26%)
  waiting for transfers between devices  20.7 us (26%)
  other arithmetic  3.02 us (4%)
  local copies, waits for them, and re-layouts  1.68 us (2%)
  between operations  0.82 us (1%)
    pallas_call x1, Pallas kernels, shards(): splat(cam, rows, live_now, own_group, their_group, mine, other, target, m...  27.3 us
    ppermute x16, waiting for transfers between devices, swap(): return lax.ppermute(array, axis, [(i, i ^ mask) for i in range(size)])  20.7 us
    ppermute x16, starting transfers between devices, swap(): return lax.ppermute(array, axis, [(i, i ^ mask) for i in range(size)])  20.7 us
    pallas_call x1, Pallas kernels, shards(): prep_own(me[None], live_count, camera, intersection_ids, depth_order)  2.5 us
    pallas_call x1, Pallas kernels, shards(): their_rows, their_group = prep_their(me[None], live_now, message)  2.29 us
  transfers between devices with their start and end apart: 16, of which 9 were waited for; matrix products, arithmetic and copies ran while one was open for 3% of the time, Pallas kernels for 6%

profile of v7, /device:TPU:0, one launch (start us, length us, event | category | flops | bytes accessed | tf_op | source)
XLA Modules:
  0.0 79.7 jit_solution(10835779001712857218)
XLA Ops:
  0.6 0.8 %pad_maximum_fusion.1 = f32[13,1024]{1,0:T(8,128)S(1)} fusion(f32[3,1024]{1,0:T(4,128)} %param.13, f32[1,1024]{1,0:T(1,128)} %bitcast.36, f32[6,1024]{1,0:T(8,128)} %param.11, f32[3,1024]{1,0:T(4,128)} %param.10), kind=kLoop, calls=%fused_computation.5 | loop fusion | flops 39936 | bytes 106496 | tf_op jit(solution)/shard_map/concatenate | solution.py:605
  1.5 3.1 %collective-permute-start = (f32[104,128]{1,0:T(8,128)S(1)}, f32[104,128]{1,0:T(8,128)S(1)}, u32[]{:S(2)}, u32[]{:S(2)}) collective-permute-start(f32[104,128]{1,0:T(8,128)S(1)} %reshape.69), channel_id=1, source_target_pairs={{0,8},{8,0},{16,24},{24,16},{1,9},{9,1},{17,25},{25,17},{2,10},{10... | collective-permute-start | bytes 159752 | tf_op jit(solution)/shard_map/ppermute | solution.py:532
  4.6 2.6 %collective-permute-start.1 = (f32[104,128]{1,0:T(8,128)S(1)}, f32[104,128]{1,0:T(8,128)S(1)}, u32[]{:S(2)}, u32[]{:S(2)}) collective-permute-start(f32[104,128]{1,0:T(8,128)S(1)} %reshape.69), channel_id=1, source_target_pairs={{0,16},{8,24},{16,0},{24,8},{1,17},{9,25},{17,1},{25,9},{2,18},{10... | collective-permute-start | bytes 159752 | tf_op jit(solution)/shard_map/ppermute | solution.py:532
  7.2 0.0 copy-start.4
  7.3 0.6 copy-done.2
  7.9 0.1 fusion.2
  8.0 0.0 copy-done.3
  8.0 0.0 copy-done.4
  8.0 1.4 %collective-permute-start.6 = (f32[88,256]{1,0:T(8,128)S(1)}, f32[88,256]{1,0:T(8,128)S(1)}, u32[]{:S(2)}, u32[]{:S(2)}) collective-permute-start(f32[88,256]{1,0:T(8,128)S(1)} %select_maximum_fusion), channel_id=1, source_target_pairs={{0,7},{1,6},{2,5},{3,4},{4,3},{5,2},{6,1},{7,0},{8,15},{9,14},{10,... | collective-permute-start | bytes 270344 | tf_op jit(solution)/shard_map/ppermute | solution.py:532
  9.4 0.1 reduce_sum.36
  9.6 0.0 copy-start.5
  9.6 0.1 reshape.70
  9.7 0.6 copy-done.5
  10.3 0.1 copy.17.camera_ref
  10.3 0.0 collective-permute-done
  10.4 0.3 collective-permute-done.1
  10.7 2.5 %collective-permute-done.2 = f32[104,128]{1,0:T(8,128)S(1)} collective-permute-done((f32[104,128]{1,0:T(8,128)S(1)}, f32[104,128]{1,0:T(8,128)S(1)}, u32[]{:S(2)}, u32[]{:S(2)}) %collective-permute-start.2) | collective-permute-done | bytes 53280 | tf_op jit(solution)/shard_map/ppermute | solution.py:532
  13.2 1.6 %collective-permute-start.3 = (f32[424,128]{1,0:T(8,128)S(1)}, f32[424,128]{1,0:T(8,128)S(1)}, u32[]{:S(2)}, u32[]{:S(2)}) collective-permute-start(f32[424,128]{1,0:T(8,128)S(1)} %constant_dynamic-update-slice_fusion), channel_id=1, source_target_pairs={{0,2},{1,3},{2,0},{3,1},{4,6},{5,7},{6,4},{7,5},{8,10},{9,11},{10,... | collective-permute-start | bytes 651272 | tf_op jit(solution)/shard_map/ppermute | solution.py:532
  14.7 1.5 %collective-permute-start.4 = (f32[424,128]{1,0:T(8,128)S(1)}, f32[424,128]{1,0:T(8,128)S(1)}, u32[]{:S(2)}, u32[]{:S(2)}) collective-permute-start(f32[424,128]{1,0:T(8,128)S(1)} %constant_dynamic-update-slice_fusion), channel_id=1, source_target_pairs={{0,4},{1,5},{2,6},{3,7},{4,0},{5,1},{6,2},{7,3},{8,12},{9,13},{10,... | collective-permute-start | bytes 651272 | tf_op jit(solution)/shard_map/ppermute | solution.py:532
  16.2 0.5 collective-permute-start.5
  16.7 2.5 %prep_own.1 = (s32[16,256]{1,0:T(8,128)S(1)}, s32[16,256]{1,0:T(8,128)S(1)}, f32[16]{0:T(128)S(1)}) custom-call(s32[1]{0:T(128)} %bitcast.6.me_ref, s32[2,16]{1,0:T(2,128)S(1)} %copy-done.2, f32[8,2,4]{2,1,0:T(2,128)S(1)} %copy.17.camera_ref, s32[2,16,256]{2,1,0:T(8,128)S(1)} %copy-done.3, s32[2,16,256]{2,1,0:T(8,128)S(1)} %copy-done.4), custom_call_target="tpu_custom_call" | custom-call | flops 4000000000 | bytes 65536 | tf_op jit(solution)/shard_map/prep_own/pallas_call | solution.py:612
  19.3 0.1 reshape.72
  19.3 0.1 pad_add_fusion.live_ref
  19.4 2.3 %prep_their.1 = (s32[24,256]{1,0:T(8,128)S(1)}, s32[16,256]{1,0:T(8,128)S(1)}) custom-call(s32[1]{0:T(128)} %bitcast.6.me_ref, s32[32]{0:T(128)S(1)} %pad_add_fusion.live_ref, f32[88,256]{1,0:T(8,128)S(1)} %collective-permute-done.6.message_ref), custom_call_target="tpu_custom_call" | custom-call | flops 4000000000 | bytes 65536 | tf_op jit(solution)/shard_map/prep_their/pallas_call | solution.py:615
  21.8 2.9 %collective-permute-done.4 = f32[424,128]{1,0:T(8,128)S(1)} collective-permute-done((f32[424,128]{1,0:T(8,128)S(1)}, f32[424,128]{1,0:T(8,128)S(1)}, u32[]{:S(2)}, u32[]{:S(2)}) %collective-permute-start.4) | collective-permute-done | bytes 217120 | tf_op jit(solution)/shard_map/ppermute | solution.py:532
  24.7 0.1 pad_maximum_fusion.mine_ref
  24.8 0.1 collective-permute-start.7
  24.8 2.4 %collective-permute-done.7.other_ref = f32[4,424,128]{2,1,0:T(8,128)S(1)} collective-permute-done((f32[4,424,128]{2,1,0:T(8,128)S(1)}, f32[4,424,128]{2,1,0:T(8,128)S(1)}, u32[]{:S(2)}, u32[]{:S(2)}) %collective-permute-start.7) | collective-permute-done | bytes 868384 | tf_op jit(solution)/shard_map/ppermute | solution.py:532
  27.2 27.3 %splat.1 = (f32[2,3,8,256]{3,2,1,0:T(8,128)S(1)}, f32[2,3,8,256]{3,2,1,0:T(8,128)S(1)}, f32[16,104,128]{2,1,0:T(8,128)S(1)}, f32[16,104,128]{2,1,0:T(8,128)S(1)}) custom-call(f32[16]{0:T(128)S(1)} %get-tuple-element.35.cam_ref, s32[10240]{0:T(1024)S(1)} %bitcast.30, s32[32]{0:T(128)S(1)} %pad_add_fusion.live_ref, ...), custom_call_target="tpu_custom_call" | custom-call | tf_op jit(solution)/shard_map/splat/pallas_call | solution.py:653
  54.5 0.8 %collective-permute-start.8 = (f32[16,104,128]{2,1,0:T(8,128)S(1)}, f32[16,104,128]{2,1,0:T(8,128)S(1)}, u32[]{:S(2)}, u32[]{:S(2)}) collective-permute-start(f32[16,104,128]{2,1,0:T(8,128)S(1)} %get-tuple-element.42), channel_id=1, source_target_pairs={{0,1},{1,0},{2,3},{3,2},{4,5},{5,4},{6,7},{7,6},{8,9},{9,8},{10,11... | collective-permute-start | bytes 2555912 | tf_op jit(solution)/shard_map/ppermute | solution.py:532
  55.4 0.1 select_reduce_fusion
  55.5 0.1 select_reduce_fusion.1
  55.6 1.8 %collective-permute-done.8 = f32[16,104,128]{2,1,0:T(8,128)S(1)} collective-permute-done((f32[16,104,128]{2,1,0:T(8,128)S(1)}, f32[16,104,128]{2,1,0:T(8,128)S(1)}, u32[]{:S(2)}, u32[]{:S(2)}) %collective-permute-start.8) | collective-permute-done | bytes 852000 | tf_op jit(solution)/shard_map/ppermute | solution.py:532
  57.3 0.1 add.30
  57.5 2.1 %collective-permute-start.10 = (f32[4,104,128]{2,1,0:T(8,128)S(1)}, f32[4,104,128]{2,1,0:T(8,128)S(1)}, u32[]{:S(2)}, u32[]{:S(2)}) collective-permute-start(f32[4,104,128]{2,1,0:T(8,128)S(1)} %get-tuple-element.52), channel_id=1, source_target_pairs={{0,6},{1,7},{2,4},{3,5},{4,2},{5,3},{6,0},{7,1},{8,14},{9,15},{10,... | collective-permute-start | bytes 638984 | tf_op jit(solution)/shard_map/ppermute | solution.py:532
  59.5 0.8 collective-permute-start.11
  60.3 0.7 collective-permute-start.12
  61.0 0.8 and_select_fusion
  61.8 1.1 %collective-permute-start.9 = (f32[2,3,8,256]{3,2,1,0:T(8,128)S(1)}, f32[2,3,8,256]{3,2,1,0:T(8,128)S(1)}, u32[]{:S(2)}, u32[]{:S(2)}) collective-permute-start(f32[2,3,8,256]{3,2,1,0:T(8,128)S(1)} %get-tuple-element.44), channel_id=1, source_target_pairs={{0,7},{1,6},{2,5},{3,4},{4,3},{5,2},{6,1},{7,0},{8,15},{9,14},{10,... | collective-permute-start | bytes 147464 | tf_op jit(solution)/shard_map/ppermute | solution.py:532
  62.9 3.7 %collective-permute-done.10 = f32[4,104,128]{2,1,0:T(8,128)S(1)} collective-permute-done((f32[4,104,128]{2,1,0:T(8,128)S(1)}, f32[4,104,128]{2,1,0:T(8,128)S(1)}, u32[]{:S(2)}, u32[]{:S(2)}) %collective-permute-start.10) | collective-permute-done | bytes 213024 | tf_op jit(solution)/shard_map/ppermute | solution.py:532
  66.6 4.5 %collective-permute-done.11 = f32[4,104,128]{2,1,0:T(8,128)S(1)} collective-permute-done((f32[4,104,128]{2,1,0:T(8,128)S(1)}, f32[4,104,128]{2,1,0:T(8,128)S(1)}, u32[]{:S(2)}, u32[]{:S(2)}) %collective-permute-start.11) | collective-permute-done | bytes 213024 | tf_op jit(solution)/shard_map/ppermute | solution.py:532
  71.1 0.1 add_add_fusion
  71.2 2.0 %collective-permute-start.13 = (f32[104,128]{1,0:T(8,128)S(1)}, f32[104,128]{1,0:T(8,128)S(1)}, u32[]{:S(2)}, u32[]{:S(2)}) collective-permute-start(f32[104,128]{1,0:T(8,128)S(1)} %get-tuple-element.57), channel_id=1, source_target_pairs={{0,24},{8,16},{16,8},{24,0},{1,25},{9,17},{17,9},{25,1},{2,26},{10... | collective-permute-start | bytes 159752 | tf_op jit(solution)/shard_map/ppermute | solution.py:532
  73.1 2.5 %collective-permute-start.15 = (f32[104,128]{1,0:T(8,128)S(1)}, f32[104,128]{1,0:T(8,128)S(1)}, u32[]{:S(2)}, u32[]{:S(2)}) collective-permute-start(f32[104,128]{1,0:T(8,128)S(1)} %get-tuple-element.55), channel_id=1, source_target_pairs={{0,8},{8,0},{16,24},{24,16},{1,9},{9,1},{17,25},{25,17},{2,10},{10... | collective-permute-start | bytes 159752 | tf_op jit(solution)/shard_map/ppermute | solution.py:532
  75.6 0.6 maximum_bitcast_fusion
  76.3 1.1 %collective-permute-done.13.refs_1_ = f32[104,128]{1,0:T(8,128)S(1)} collective-permute-done((f32[104,128]{1,0:T(8,128)S(1)}, f32[104,128]{1,0:T(8,128)S(1)}, u32[]{:S(2)}, u32[]{:S(2)}) %collective-permute-start.13) | collective-permute-done | bytes 53280 | tf_op jit(solution)/shard_map/ppermute | solution.py:532
  77.4 1.6 %collective-permute-done.14.refs_2_ = f32[104,128]{1,0:T(8,128)S(1)} collective-permute-done((f32[104,128]{1,0:T(8,128)S(1)}, f32[104,128]{1,0:T(8,128)S(1)}, u32[]{:S(2)}, u32[]{:S(2)}) %collective-permute-start.14) | collective-permute-done | bytes 53280 | tf_op jit(solution)/shard_map/ppermute | solution.py:532
  79.0 0.7 tail.1
  (34 shorter events, 0.2 us)
Async XLA Ops:
  0.6 6.6 %copy-start = (f32[2,16,3,256]{3,1,2,0:T(8,128)S(1)}, f32[2,16,3,256]{3,1,2,0:T(8,128)}, u32[]{:S(2)}) copy-start(f32[2,16,3,256]{3,1,2,0:T(8,128)} %param.15) | copy-start | bytes 294916
  1.5 8.8 %collective-permute-start = (f32[104,128]{1,0:T(8,128)S(1)}, f32[104,128]{1,0:T(8,128)S(1)}, u32[]{:S(2)}, u32[]{:S(2)}) collective-permute-start(f32[104,128]{1,0:T(8,128)S(1)} %reshape.69), channel_id=1, source_target_pairs={{0,8},{8,0},{16,24},{24,16},{1,9},{9,1},{17,25},{25,17},{2,10},{10... | collective-permute-start | bytes 159752 | tf_op jit(solution)/shard_map/ppermute | solution.py:532
  4.6 6.1 %collective-permute-start.1 = (f32[104,128]{1,0:T(8,128)S(1)}, f32[104,128]{1,0:T(8,128)S(1)}, u32[]{:S(2)}, u32[]{:S(2)}) collective-permute-start(f32[104,128]{1,0:T(8,128)S(1)} %reshape.69), channel_id=1, source_target_pairs={{0,16},{8,24},{16,0},{24,8},{1,17},{9,25},{17,1},{25,9},{2,18},{10... | collective-permute-start | bytes 159752 | tf_op jit(solution)/shard_map/ppermute | solution.py:532
  7.2 5.9 %collective-permute-start.2 = (f32[104,128]{1,0:T(8,128)S(1)}, f32[104,128]{1,0:T(8,128)S(1)}, u32[]{:S(2)}, u32[]{:S(2)}) collective-permute-start(f32[104,128]{1,0:T(8,128)S(1)} %reshape.69), channel_id=1, source_target_pairs={{0,24},{8,16},{16,8},{24,0},{1,25},{9,17},{17,9},{25,1},{2,26},{10... | collective-permute-start | bytes 159752 | tf_op jit(solution)/shard_map/ppermute | solution.py:532
  7.2 0.7 copy-start.2
  7.2 0.8 copy-start.3
  7.2 0.8 copy-start.4
  8.0 11.2 %collective-permute-start.6 = (f32[88,256]{1,0:T(8,128)S(1)}, f32[88,256]{1,0:T(8,128)S(1)}, u32[]{:S(2)}, u32[]{:S(2)}) collective-permute-start(f32[88,256]{1,0:T(8,128)S(1)} %select_maximum_fusion), channel_id=1, source_target_pairs={{0,7},{1,6},{2,5},{3,4},{4,3},{5,2},{6,1},{7,0},{8,15},{9,14},{10,... | collective-permute-start | bytes 270344 | tf_op jit(solution)/shard_map/ppermute | solution.py:532
  9.6 0.7 copy-start.5
  13.2 8.6 %collective-permute-start.3 = (f32[424,128]{1,0:T(8,128)S(1)}, f32[424,128]{1,0:T(8,128)S(1)}, u32[]{:S(2)}, u32[]{:S(2)}) collective-permute-start(f32[424,128]{1,0:T(8,128)S(1)} %constant_dynamic-update-slice_fusion), channel_id=1, source_target_pairs={{0,2},{1,3},{2,0},{3,1},{4,6},{5,7},{6,4},{7,5},{8,10},{9,11},{10,... | collective-permute-start | bytes 651272 | tf_op jit(solution)/shard_map/ppermute | solution.py:532
  14.7 9.9 %collective-permute-start.4 = (f32[424,128]{1,0:T(8,128)S(1)}, f32[424,128]{1,0:T(8,128)S(1)}, u32[]{:S(2)}, u32[]{:S(2)}) collective-permute-start(f32[424,128]{1,0:T(8,128)S(1)} %constant_dynamic-update-slice_fusion), channel_id=1, source_target_pairs={{0,4},{1,5},{2,6},{3,7},{4,0},{5,1},{6,2},{7,3},{8,12},{9,13},{10,... | collective-permute-start | bytes 651272 | tf_op jit(solution)/shard_map/ppermute | solution.py:532
  16.2 8.4 %collective-permute-start.5 = (f32[424,128]{1,0:T(8,128)S(1)}, f32[424,128]{1,0:T(8,128)S(1)}, u32[]{:S(2)}, u32[]{:S(2)}) collective-permute-start(f32[424,128]{1,0:T(8,128)S(1)} %constant_dynamic-update-slice_fusion), channel_id=1, source_target_pairs={{0,6},{1,7},{2,4},{3,5},{4,2},{5,3},{6,0},{7,1},{8,14},{9,15},{10,... | collective-permute-start | bytes 651272 | tf_op jit(solution)/shard_map/ppermute | solution.py:532
  24.7 2.6 %copy-start.1 = (bf16[32,256]{1,0:T(8,128)(2,1)S(1)}, bf16[32,256]{1,0:T(8,128)(2,1)}, u32[]{:S(2)}) copy-start(bf16[32,256]{1,0:T(8,128)(2,1)} %constant.25.clone.mono_ref) | copy-start | bytes 49156
  24.8 2.5 %collective-permute-start.7 = (f32[4,424,128]{2,1,0:T(8,128)S(1)}, f32[4,424,128]{2,1,0:T(8,128)S(1)}, u32[]{:S(2)}, u32[]{:S(2)}) collective-permute-start(f32[4,424,128]{2,1,0:T(8,128)S(1)} %pad_maximum_fusion.mine_ref), channel_id=1, source_target_pairs={{0,1},{1,0},{2,3},{3,2},{4,5},{5,4},{6,7},{7,6},{8,9},{9,8},{10,11... | collective-permute-start | bytes 2605064 | tf_op jit(solution)/shard_map/ppermute | solution.py:532
  54.5 2.8 %collective-permute-start.8 = (f32[16,104,128]{2,1,0:T(8,128)S(1)}, f32[16,104,128]{2,1,0:T(8,128)S(1)}, u32[]{:S(2)}, u32[]{:S(2)}) collective-permute-start(f32[16,104,128]{2,1,0:T(8,128)S(1)} %get-tuple-element.42), channel_id=1, source_target_pairs={{0,1},{1,0},{2,3},{3,2},{4,5},{5,4},{6,7},{7,6},{8,9},{9,8},{10,11... | collective-permute-start | bytes 2555912 | tf_op jit(solution)/shard_map/ppermute | solution.py:532
  57.5 9.1 %collective-permute-start.10 = (f32[4,104,128]{2,1,0:T(8,128)S(1)}, f32[4,104,128]{2,1,0:T(8,128)S(1)}, u32[]{:S(2)}, u32[]{:S(2)}) collective-permute-start(f32[4,104,128]{2,1,0:T(8,128)S(1)} %get-tuple-element.52), channel_id=1, source_target_pairs={{0,6},{1,7},{2,4},{3,5},{4,2},{5,3},{6,0},{7,1},{8,14},{9,15},{10,... | collective-permute-start | bytes 638984 | tf_op jit(solution)/shard_map/ppermute | solution.py:532
  59.5 11.5 %collective-permute-start.11 = (f32[4,104,128]{2,1,0:T(8,128)S(1)}, f32[4,104,128]{2,1,0:T(8,128)S(1)}, u32[]{:S(2)}, u32[]{:S(2)}) collective-permute-start(f32[4,104,128]{2,1,0:T(8,128)S(1)} %get-tuple-element.54), channel_id=1, source_target_pairs={{0,4},{1,5},{2,6},{3,7},{4,0},{5,1},{6,2},{7,3},{8,12},{9,13},{10,... | collective-permute-start | bytes 638984 | tf_op jit(solution)/shard_map/ppermute | solution.py:532
  60.3 10.8 %collective-permute-start.12 = (f32[4,104,128]{2,1,0:T(8,128)S(1)}, f32[4,104,128]{2,1,0:T(8,128)S(1)}, u32[]{:S(2)}, u32[]{:S(2)}) collective-permute-start(f32[4,104,128]{2,1,0:T(8,128)S(1)} %get-tuple-element.53), channel_id=1, source_target_pairs={{0,2},{1,3},{2,0},{3,1},{4,6},{5,7},{6,4},{7,5},{8,10},{9,11},{10,... | collective-permute-start | bytes 638984 | tf_op jit(solution)/shard_map/ppermute | solution.py:532
  61.8 13.8 %collective-permute-start.9 = (f32[2,3,8,256]{3,2,1,0:T(8,128)S(1)}, f32[2,3,8,256]{3,2,1,0:T(8,128)S(1)}, u32[]{:S(2)}, u32[]{:S(2)}) collective-permute-start(f32[2,3,8,256]{3,2,1,0:T(8,128)S(1)} %get-tuple-element.44), channel_id=1, source_target_pairs={{0,7},{1,6},{2,5},{3,4},{4,3},{5,2},{6,1},{7,0},{8,15},{9,14},{10,... | collective-permute-start | bytes 147464 | tf_op jit(solution)/shard_map/ppermute | solution.py:532
  71.2 6.2 %collective-permute-start.13 = (f32[104,128]{1,0:T(8,128)S(1)}, f32[104,128]{1,0:T(8,128)S(1)}, u32[]{:S(2)}, u32[]{:S(2)}) collective-permute-start(f32[104,128]{1,0:T(8,128)S(1)} %get-tuple-element.57), channel_id=1, source_target_pairs={{0,24},{8,16},{16,8},{24,0},{1,25},{9,17},{17,9},{25,1},{2,26},{10... | collective-permute-start | bytes 159752 | tf_op jit(solution)/shard_map/ppermute | solution.py:532
  73.1 5.9 %collective-permute-start.14 = (f32[104,128]{1,0:T(8,128)S(1)}, f32[104,128]{1,0:T(8,128)S(1)}, u32[]{:S(2)}, u32[]{:S(2)}) collective-permute-start(f32[104,128]{1,0:T(8,128)S(1)} %get-tuple-element.56), channel_id=1, source_target_pairs={{0,16},{8,24},{16,0},{24,8},{1,17},{9,25},{17,1},{25,9},{2,18},{10... | collective-permute-start | bytes 159752 | tf_op jit(solution)/shard_map/ppermute | solution.py:532
  73.1 5.9 %collective-permute-start.15 = (f32[104,128]{1,0:T(8,128)S(1)}, f32[104,128]{1,0:T(8,128)S(1)}, u32[]{:S(2)}, u32[]{:S(2)}) collective-permute-start(f32[104,128]{1,0:T(8,128)S(1)} %get-tuple-element.55), channel_id=1, source_target_pairs={{0,8},{8,0},{16,24},{24,16},{1,9},{9,1},{17,25},{25,17},{2,10},{10... | collective-permute-start | bytes 159752 | tf_op jit(solution)/shard_map/ppermute | solution.py:532
